TPU v7x, 128 devices: a whole 4x4x4 slice. The times are simulated.
128 devices in a mesh: gx: 8 (over x_lo, y), gy: 16 (over z, x_hi, core).
Axes of the slice: x: 4 (x_hi: 2, x_lo: 2; x = x_hi * 2 + x_lo), y: 4, z: 4, core: 2. Of those that a mesh axis runs over, the one named last changes fastest.
Arguments:
- node_shift: float32 [2, 512, 8192], P(None, 'gx', 'gy'), may hold values from -1.5 to 1.5
- node_speed: float32 [2, 512, 8192], P(None, 'gx', 'gy'), may hold values from -4 to 4
- damage_initial: int32 [2, 512, 8192], P(None, 'gx', 'gy'), may hold values from 0 to 7
- cohesive_markers: int32 [64, 16], P('gx', 'gy'), may hold values from 0 to 1, as said below
- cell_warmth: float32 [256, 4096], P(('gx', 'gy')), may hold values from 0 to 1
- heat_storage: float32 [256, 4096], P(('gx', 'gy')), may hold values from 0.5 to 2
- surface_transfer: float32 [256, 4096], P(('gx', 'gy')), may hold values from 0.1 to 1
- quench_liquid_heat: float32 [256, 4096], P(('gx', 'gy')), may hold values from 0 to 0.3
Outputs:
- displace_new: float32 [2, 512, 8192], P(None, 'gx', 'gy')
- velocity_new: float32 [2, 512, 8192], P(None, 'gx', 'gy')
- damage: bfloat16 [2, 512, 8192], P(None, 'gx', 'gy')
- warmth_after_solve: float32 [256, 4096], P(('gx', 'gy'))
Inputs may be any that keep to these rules, and one draw needn't show every extreme that they name: `cohesive_markers`: within each column, every block of 8 consecutive tile rows starting at a multiple of 8 holds between 1 and 4 ones, and in every draw some block holds exactly 4.
All inputs are finite; a program needn't handle non-finite values.
Results may differ from a plain program's by a relative error of at most 0.001.
Values sent between devices are 32-bit elements; how exact they have to be, the bound alone decides.
No kernel may reach another device: no remote copies, remote signals or barrier semaphores. Data moves between devices by JAX's collectives and lax.ppermute only.
A program may use at most 64 MiB of HBM per device.

v0:
```python
import jax
import jax.numpy as jnp
from jax import lax
from jax.sharding import PartitionSpec as P

SR = 8
SEG = 128
SUBSTEPS = 8
ITERS = 4


STIFFNESS = 1.0
EXPANSION = 0.6
SOFTENING_SCALE = 0.25
TIME_STEP = 0.4
DAMPING = 0.05
HEAT_INCREMENT = 1.0
GAP_GAIN = 0.5


def with_halo(value, sides, width):
    for axis, dim in sides:
        count, length = (lax.axis_size(axis), value.shape[dim])
        up = [(i, (i + 1) % count) for i in range(count - 1)]
        down = [(j, i) for i, j in up]
        last = lax.slice_in_dim(value, length - width, length, axis=dim)
        first = lax.slice_in_dim(value, 0, width, axis=dim)
        before = lax.ppermute(last, axis, up)
        after = lax.ppermute(first, axis, down)
        value = jnp.concatenate([before, value, after], axis=dim)
    return value


def softening(opening):
    stretch = jnp.maximum(opening, 0.0)
    return 1.0 - jnp.exp(-stretch * stretch / SOFTENING_SCALE)


def edge_masks(row_first, col_first, height_number_all, width_number, total_rows, total_cols):
    row_index = row_first + jnp.arange(height_number_all, dtype=jnp.int32)
    col_index = col_first + jnp.arange(width_number, dtype=jnp.int32)
    in_rows = (row_index >= 0) & (row_index < total_rows)
    in_cols = (col_index >= 0) & (col_index < total_cols)
    present_horizontal = ((row_index >= 1) & (row_index < total_rows))[:, None] & in_cols[None, :]
    present_vertical = in_rows[:, None] & ((col_index >= 1) & (col_index < total_cols))[None, :]
    return (present_horizontal.astype(jnp.float32), present_vertical.astype(jnp.float32))


def march_forward(state_tensors, dense_mesh_heat, present_horizontal, present_vertical):
    disp_x, disp_y, vel_x, vel_y, dam_x, dam_y, weight = [
        state_tensors[number] for number in range(7)
    ]
    average_horizontal = 0.5 * (dense_mesh_heat[1:, :] + dense_mesh_heat[:-1, :])
    open_x = disp_x[1:, :] - disp_x[:-1, :] - EXPANSION * average_horizontal
    shear_x = disp_y[1:, :] - disp_y[:-1, :]
    new_dx = jnp.maximum(
        dam_x[1:, :], softening(open_x) * weight[1:, :] * present_horizontal[1:, :]
    )
    spring_x = STIFFNESS * (1.0 - new_dx) * present_horizontal[1:, :]
    normal_x = spring_x * open_x
    along_x = spring_x * shear_x
    average_vertical = 0.5 * (dense_mesh_heat[:, 1:] + dense_mesh_heat[:, :-1])
    open_y = disp_y[:, 1:] - disp_y[:, :-1] - EXPANSION * average_vertical
    shear_y = disp_x[:, 1:] - disp_x[:, :-1]
    new_dy = jnp.maximum(dam_y[:, 1:], softening(open_y) * weight[:, 1:] * present_vertical[:, 1:])
    spring_y = STIFFNESS * (1.0 - new_dy) * present_vertical[:, 1:]
    normal_y = spring_y * open_y
    along_y = spring_y * shear_y
    force_x = normal_x[1:, 1:-1] - normal_x[:-1, 1:-1] + (along_y[1:-1, 1:] - along_y[1:-1, :-1])
    force_y = along_x[1:, 1:-1] - along_x[:-1, 1:-1] + (normal_y[1:-1, 1:] - normal_y[1:-1, :-1])
    inner_vx = vel_x[1:-1, 1:-1]
    inner_vy = vel_y[1:-1, 1:-1]
    next_vx = inner_vx + TIME_STEP * (force_x - DAMPING * inner_vx)
    next_vy = inner_vy + TIME_STEP * (force_y - DAMPING * inner_vy)
    next_ux = disp_x[1:-1, 1:-1] + TIME_STEP * next_vx
    next_uy = disp_y[1:-1, 1:-1] + TIME_STEP * next_vy
    return jnp.stack(
        [
            next_ux,
            next_uy,
            next_vx,
            next_vy,
            new_dx[:-1, 1:-1],
            new_dy[1:-1, :-1],
            weight[1:-1, 1:-1],
        ]
    )


def widen_upward(padded):
    middle = padded[1:-1]
    even_rows = 0.75 * middle + 0.25 * padded[:-2]
    odd_rows = 0.75 * middle + 0.25 * padded[2:]
    return jnp.stack([even_rows, odd_rows], axis=1).reshape(2 * middle.shape[0], padded.shape[1])


def widen_sideways(padded):
    middle = padded[:, 1:-1]
    even_cols = 0.75 * middle + 0.25 * padded[:, :-2]
    odd_cols = 0.75 * middle + 0.25 * padded[:, 2:]
    return jnp.stack([even_cols, odd_cols], axis=2).reshape(padded.shape[0], 2 * middle.shape[1])


def kernel_table():
    position = jnp.arange(SEG, dtype=jnp.float32)
    return jnp.exp(-4.0 * jnp.abs(position[:, None] - position[None, :]) / SEG) * (2.0 / SEG)


def radiate(values):
    flattened = values.reshape(-1, SEG)
    product = jnp.dot(
        flattened,
        kernel_table(),
        precision=lax.Precision.HIGHEST,
        preferred_element_type=jnp.float32,
    )
    return product.reshape(values.shape)


def prolonged_warmth(cell_patch_slicer):
    height_number_all, width_number = cell_patch_slicer.shape
    padded = with_halo(cell_patch_slicer[None], (("gx", 1), ("gy", 2)), 3)[0]
    row_index = (
        lax.axis_index("gx") * height_number_all
        - 3
        + jnp.arange(height_number_all + 6, dtype=jnp.int32)
    )
    col_index = (
        lax.axis_index("gy") * width_number - 3 + jnp.arange(width_number + 6, dtype=jnp.int32)
    )
    total_rows = height_number_all * lax.axis_size("gx")
    total_cols = width_number * lax.axis_size("gy")
    padded = jnp.where((row_index == -1)[:, None], jnp.roll(padded, -1, 0), padded)
    padded = jnp.where((row_index == total_rows)[:, None], jnp.roll(padded, 1, 0), padded)
    padded = jnp.where((col_index == -1)[None, :], jnp.roll(padded, -1, 1), padded)
    padded = jnp.where((col_index == total_cols)[None, :], jnp.roll(padded, 1, 1), padded)
    return widen_sideways(widen_upward(padded))


def tile_rim(layered_tensors):
    return with_halo(layered_tensors, (("gx", 1), ("gy", 2)), 1)


def heat_solve(
    cell_warmth,
    heat_storage,
    surface_transfer,
    quench_liquid_heat,
    thermal_impedance,
    margin_wrapper,
    row_first,
    total_rows,
    col_first,
    total_cols,
):
    height_number_all, width_number = cell_warmth.shape
    heat_conductance = (1.0 + 0.5 * cell_warmth) / (1.0 + thermal_impedance)
    layered_tensors = margin_wrapper(jnp.stack([heat_conductance, cell_warmth]))
    padded_cond = layered_tensors[0]
    haloed_warmth = layered_tensors[1]
    row_index = (row_first + jnp.arange(height_number_all, dtype=jnp.int32))[:, None]
    col_index = (col_first + jnp.arange(width_number, dtype=jnp.int32))[None, :]
    cond_down = (
        0.5 * (heat_conductance + padded_cond[:-2, 1:-1]) * (row_index >= 1).astype(jnp.float32)
    )
    cond_up = (
        0.5
        * (heat_conductance + padded_cond[2:, 1:-1])
        * (row_index <= total_rows - 2).astype(jnp.float32)
    )
    cond_left = (
        0.5 * (heat_conductance + padded_cond[1:-1, :-2]) * (col_index >= 1).astype(jnp.float32)
    )
    cond_right = (
        0.5
        * (heat_conductance + padded_cond[1:-1, 2:])
        * (col_index <= total_cols - 2).astype(jnp.float32)
    )
    offsum = cond_down + cond_up + cond_left + cond_right
    diagonal = heat_storage / HEAT_INCREMENT + surface_transfer + offsum
    off_ratio = offsum / diagonal
    bound_low = lax.pmin(jnp.min(1.0 - off_ratio), ("gx", "gy"))
    bound_high = lax.pmax(jnp.max(1.0 + off_ratio), ("gx", "gy"))

    def laplace_action(field, padded):
        return diagonal * field - (
            cond_down * padded[:-2, 1:-1]
            + cond_up * padded[2:, 1:-1]
            + cond_left * padded[1:-1, :-2]
            + cond_right * padded[1:-1, 2:]
        )

    center = 0.5 * (bound_high + bound_low)
    spread = 0.5 * (bound_high - bound_low)
    sigma_ratio = center / spread
    rho_now = 1.0 / sigma_ratio
    forcing_entries = (
        heat_storage / HEAT_INCREMENT * cell_warmth + surface_transfer * quench_liquid_heat
    )
    misfit_norm = forcing_entries - laplace_action(cell_warmth, haloed_warmth)
    direction = misfit_norm / diagonal / center
    answer_state = cell_warmth
    for iteration in range(ITERS):
        answer_state = answer_state + direction
        if iteration + 1 < ITERS:
            padded_dir = margin_wrapper(direction[None])[0]
            misfit_norm = misfit_norm - laplace_action(direction, padded_dir)
            rho_next = 1.0 / (2.0 * sigma_ratio - rho_now)
            direction = rho_next * rho_now * direction + 2.0 * rho_next / spread * (
                misfit_norm / diagonal
            )
            rho_now = rho_next
    return answer_state


def per_device(
    node_shift,
    node_speed,
    damage_initial,
    cohesive_markers,
    cell_warmth,
    heat_storage,
    surface_transfer,
    quench_liquid_heat,
):
    height_number_all, width_number = (node_shift.shape[1], node_shift.shape[2])
    cell_patch_slicer, cap_tile, film_tile, bath_tile = (
        lax.all_to_all(cell_warmth, "gy", split_axis=1, concat_axis=0, tiled=True),
        lax.all_to_all(heat_storage, "gy", split_axis=1, concat_axis=0, tiled=True),
        lax.all_to_all(surface_transfer, "gy", split_axis=1, concat_axis=0, tiled=True),
        lax.all_to_all(quench_liquid_heat, "gy", split_axis=1, concat_axis=0, tiled=True),
    )
    dense_mesh_heat = prolonged_warmth(cell_patch_slicer)
    row_first = lax.axis_index("gx") * height_number_all
    col_first = lax.axis_index("gy") * width_number
    total_rows = height_number_all * lax.axis_size("gx")
    total_cols = width_number * lax.axis_size("gy")
    marking = cohesive_markers[:, 0]
    weight = jnp.broadcast_to(
        jnp.repeat(marking, SR)[:, None], (height_number_all, width_number)
    ).astype(jnp.float32)
    present_horizontal, present_vertical = edge_masks(
        row_first, col_first, height_number_all, width_number, total_rows, total_cols
    )
    start_damage = damage_initial.astype(jnp.float32) * 0.125 * weight[None]
    state_tensors = jnp.stack(
        [
            node_shift[0],
            node_shift[1],
            node_speed[0],
            node_speed[1],
            start_damage[0] * present_horizontal,
            start_damage[1] * present_vertical,
            weight,
        ]
    )
    mask_x, mask_y = edge_masks(
        row_first - 1,
        col_first - 1,
        height_number_all + 2,
        width_number + 2,
        total_rows,
        total_cols,
    )
    warmth_lines = dense_mesh_heat[3:-3, 3:-3]
    for substep in range(SUBSTEPS):
        moved = with_halo(
            jnp.stack(
                [
                    state_tensors[0],
                    state_tensors[1],
                    state_tensors[4],
                    state_tensors[5],
                    state_tensors[6],
                ]
            ),
            (("gx", 1), ("gy", 2)),
            1,
        )
        resting = jnp.pad(state_tensors[2:4], ((0, 0), (1, 1), (1, 1)))
        padded = jnp.stack(
            [moved[0], moved[1], resting[0], resting[1], moved[2], moved[3], moved[4]]
        )
        state_tensors = march_forward(padded, warmth_lines, mask_x, mask_y)
    gap_sum = state_tensors[4] + state_tensors[5]
    glowing = radiate(gap_sum)
    resist_tile = GAP_GAIN * glowing.reshape(height_number_all // 2, 2, width_number // 2, 2).sum(
        axis=(1, 3)
    )
    tile_rows, tile_cols = cell_patch_slicer.shape
    updated_tile = heat_solve(
        cell_patch_slicer,
        cap_tile,
        film_tile,
        bath_tile,
        resist_tile,
        tile_rim,
        lax.axis_index("gx") * tile_rows,
        tile_rows * lax.axis_size("gx"),
        lax.axis_index("gy") * tile_cols,
        tile_cols * lax.axis_size("gy"),
    )
    warmth_after_solve = lax.all_to_all(updated_tile, "gy", split_axis=0, concat_axis=1, tiled=True)
    return (
        state_tensors[0:2],
        state_tensors[2:4],
        state_tensors[4:6].astype(jnp.bfloat16),
        warmth_after_solve,
    )


def solution(mesh):
    return jax.shard_map(
        per_device,
        mesh=mesh,
        in_specs=(
            P(None, "gx", "gy"),
            P(None, "gx", "gy"),
            P(None, "gx", "gy"),
            P("gx", "gy"),
            P(("gx", "gy"), None),
            P(("gx", "gy"), None),
            P(("gx", "gy"), None),
            P(("gx", "gy"), None),
        ),
        out_specs=(
            P(None, "gx", "gy"),
            P(None, "gx", "gy"),
            P(None, "gx", "gy"),
            P(("gx", "gy"), None),
        ),
        check_vma=False,
    )
```

profile of v0, /device:TPU:3, one launch (start us, length us, event | category | flops | bytes accessed | tf_op | source)
XLA Modules:
  0.0 557.6 jit_solution(16234106904708818938)
XLA Ops:
  5.8 4.7 collective-permute-start.1
  12.9 8.1 %all-to-all-start = ((f32[2,16,256]{2,0,1:T(2,128)}), f32[2,16,256]{2,0,1:T(2,128)S(1)}, u32[]{:S(2)}, u32[]{:S(2)}) async-start(f32[2,16,256]{2,0,1:T(2,128)} %bitcast.5), calls=%async_computation | async-start | bytes 65536 | tf_op jit(solution)/shard_map/all_to_all | solution.py:228
  29.1 5.1 collective-permute-start.2
  37.0 9.0 %all-to-all-start.1 = ((f32[2,16,256]{2,0,1:T(2,128)}), f32[2,16,256]{2,0,1:T(2,128)S(1)}, u32[]{:S(2)}, u32[]{:S(2)}) async-start(f32[2,16,256]{2,0,1:T(2,128)} %bitcast.146), calls=%async_computation.1 | async-start | bytes 65536 | tf_op jit(solution)/shard_map/all_to_all | solution.py:229
  46.0 6.4 %collective-permute-start.5 = (f32[1,3,256]{2,1,0:T(4,128)S(1)}, f32[1,3,256]{2,1,0:T(4,128)S(1)}, u32[]{:S(2)}, u32[]{:S(2)}) collective-permute-start(f32[1,3,256]{2,1,0:T(4,128)S(1)} %get-tuple-element.198), channel_id=1, source_target_pairs={{16,0},{32,16},{48,32},{64,48},{80,64},{96,80},{112,96},{17,1},{33... | collective-permute-start | bytes 9224 | tf_op jit(solution)/shard_map/ppermute | solution.py:29
  54.5 6.9 %all-to-all-start.2 = ((f32[2,16,256]{2,0,1:T(2,128)}), f32[2,16,256]{2,0,1:T(2,128)S(1)}, u32[]{:S(2)}, u32[]{:S(2)}) async-start(f32[2,16,256]{2,0,1:T(2,128)} %bitcast.148), calls=%async_computation.2 | async-start | bytes 65536 | tf_op jit(solution)/shard_map/all_to_all | solution.py:230
  61.4 7.3 %all-to-all-done.2 = f32[2,16,256]{2,0,1:T(2,128)S(1)} async-done(((f32[2,16,256]{2,0,1:T(2,128)}), f32[2,16,256]{2,0,1:T(2,128)S(1)}, u32[]{:S(2)}, u32[]{:S(2)}) %all-to-all-start.2) | async-done | bytes 32800 | tf_op jit(solution)/shard_map/all_to_all | solution.py:230
  68.7 3.7 all-to-all-start.3
  74.6 4.9 collective-permute-start.6
  89.3 6.3 %collective-permute-start.9 = (f32[5,1,512]{2,1,0:T(1,128)}, f32[5,1,512]{2,1,0:T(1,128)}, u32[]{:S(2)}, u32[]{:S(2)}) collective-permute-start(f32[5,1,512]{2,1,0:T(1,128)} %copy.49), channel_id=1, source_target_pairs={{16,0},{32,16},{48,32},{64,48},{80,64},{96,80},{112,96},{17,1},{33... | collective-permute-start | bytes 30728 | tf_op jit(solution)/shard_map/ppermute | solution.py:29
  106.7 3.7 collective-permute-start.11
  110.4 4.9 collective-permute-start.10
  140.4 6.6 %collective-permute-start.14 = (f32[5,66,1]{1,2,0:T(1,128)S(1)}, f32[5,66,1]{1,2,0:T(1,128)S(1)}, u32[]{:S(2)}, u32[]{:S(2)}) collective-permute-start(f32[5,66,1]{1,2,0:T(1,128)S(1)} %get-tuple-element.101), channel_id=1, source_target_pairs={{0,1},{1,2},{2,3},{3,4},{4,5},{5,6},{6,7},{7,8},{8,9},{9,10},{10,1... | collective-permute-start | bytes 3968 | tf_op jit(solution)/shard_map/ppermute | solution.py:28
  172.2 6.7 %collective-permute-start.18 = (f32[5,66,1]{1,2,0:T(1,128)S(1)}, f32[5,66,1]{1,2,0:T(1,128)S(1)}, u32[]{:S(2)}, u32[]{:S(2)}) collective-permute-start(f32[5,66,1]{1,2,0:T(1,128)S(1)} %get-tuple-element.99), channel_id=1, source_target_pairs={{0,1},{1,2},{2,3},{3,4},{4,5},{5,6},{6,7},{7,8},{8,9},{9,10},{10,1... | collective-permute-start | bytes 3968 | tf_op jit(solution)/shard_map/ppermute | solution.py:28
  204.1 6.5 %collective-permute-start.22 = (f32[5,66,1]{1,2,0:T(1,128)S(1)}, f32[5,66,1]{1,2,0:T(1,128)S(1)}, u32[]{:S(2)}, u32[]{:S(2)}) collective-permute-start(f32[5,66,1]{1,2,0:T(1,128)S(1)} %get-tuple-element.97), channel_id=1, source_target_pairs={{0,1},{1,2},{2,3},{3,4},{4,5},{5,6},{6,7},{7,8},{8,9},{9,10},{10,1... | collective-permute-start | bytes 3968 | tf_op jit(solution)/shard_map/ppermute | solution.py:28
  235.9 6.9 %collective-permute-start.26 = (f32[5,66,1]{1,2,0:T(1,128)S(1)}, f32[5,66,1]{1,2,0:T(1,128)S(1)}, u32[]{:S(2)}, u32[]{:S(2)}) collective-permute-start(f32[5,66,1]{1,2,0:T(1,128)S(1)} %get-tuple-element.95), channel_id=1, source_target_pairs={{0,1},{1,2},{2,3},{3,4},{4,5},{5,6},{6,7},{7,8},{8,9},{9,10},{10,1... | collective-permute-start | bytes 3968 | tf_op jit(solution)/shard_map/ppermute | solution.py:28
  267.7 6.5 %collective-permute-start.30 = (f32[5,66,1]{1,2,0:T(1,128)S(1)}, f32[5,66,1]{1,2,0:T(1,128)S(1)}, u32[]{:S(2)}, u32[]{:S(2)}) collective-permute-start(f32[5,66,1]{1,2,0:T(1,128)S(1)} %get-tuple-element.93), channel_id=1, source_target_pairs={{0,1},{1,2},{2,3},{3,4},{4,5},{5,6},{6,7},{7,8},{8,9},{9,10},{10,1... | collective-permute-start | bytes 3968 | tf_op jit(solution)/shard_map/ppermute | solution.py:28
  299.6 7.3 %collective-permute-start.34 = (f32[5,66,1]{1,2,0:T(1,128)S(1)}, f32[5,66,1]{1,2,0:T(1,128)S(1)}, u32[]{:S(2)}, u32[]{:S(2)}) collective-permute-start(f32[5,66,1]{1,2,0:T(1,128)S(1)} %get-tuple-element.91), channel_id=1, source_target_pairs={{0,1},{1,2},{2,3},{3,4},{4,5},{5,6},{6,7},{7,8},{8,9},{9,10},{10,1... | collective-permute-start | bytes 3968 | tf_op jit(solution)/shard_map/ppermute | solution.py:28
  311.1 9.7 %reshape_reshape.3 = f32[32,2,256,2]{3,2,1,0:T(8,128)} reshape(f32[256,128]{1,0:T(8,128)S(1)} %fusion.272) | data formatting | bytes 262144 | tf_op jit(solution)/shard_map/reshape;reshape | solution.py:287
  320.8 4.6 reduce_sum.9
  325.5 3.4 collective-permute-start.37
  331.7 3.6 collective-permute-done.36
  337.3 7.3 %collective-permute-start.38 = (f32[2,34,1]{2,1,0:T(8,128)S(1)}, f32[2,34,1]{2,1,0:T(8,128)S(1)}, u32[]{:S(2)}, u32[]{:S(2)}) collective-permute-start(f32[2,34,1]{2,1,0:T(8,128)S(1)} %get-tuple-element.177), channel_id=1, source_target_pairs={{0,1},{1,2},{2,3},{3,4},{4,5},{5,6},{6,7},{7,8},{8,9},{9,10},{10,1... | collective-permute-start | bytes 824 | tf_op jit(solution)/shard_map/ppermute | solution.py:28
  347.4 72.4 %pmax.7 = f32[]{:T(128)} all-reduce(f32[]{:T(128)} %get-tuple-element.17), channel_id=1, replica_groups=mesh['gx'=8,'gy'=16] {'gx','gy'}, use_global_device_ids=true, to_apply=%region_2.3 | all-reduce | flops 1 | bytes 8 | tf_op jit(solution)/shard_map/pmax | solution.py:183
  419.8 64.1 %pmin.7 = f32[]{:T(128)} all-reduce(f32[]{:T(128)} %get-tuple-element.16), channel_id=1, replica_groups=mesh['gx'=8,'gy'=16] {'gx','gy'}, use_global_device_ids=true, to_apply=%region_4.5 | all-reduce | flops 1 | bytes 8 | tf_op jit(solution)/shard_map/pmin | solution.py:182
  485.3 3.7 collective-permute-start.41
  495.5 4.2 collective-permute-start.43
  509.1 3.5 collective-permute-done.44
  514.7 6.4 %collective-permute-start.46 = (f32[1,34,1]{2,1,0:T(8,128)S(1)}, f32[1,34,1]{2,1,0:T(8,128)S(1)}, u32[]{:S(2)}, u32[]{:S(2)}) collective-permute-start(f32[1,34,1]{2,1,0:T(8,128)S(1)} %get-tuple-element.185), channel_id=1, source_target_pairs={{0,1},{1,2},{2,3},{3,4},{4,5},{5,6},{6,7},{7,8},{8,9},{9,10},{10,1... | collective-permute-start | bytes 416 | tf_op jit(solution)/shard_map/ppermute | solution.py:28
  532.7 6.8 %collective-permute-start.50 = (f32[1,34,1]{2,1,0:T(8,128)S(1)}, f32[1,34,1]{2,1,0:T(8,128)S(1)}, u32[]{:S(2)}, u32[]{:S(2)}) collective-permute-start(f32[1,34,1]{2,1,0:T(8,128)S(1)} %get-tuple-element.183), channel_id=1, source_target_pairs={{0,1},{1,2},{2,3},{3,4},{4,5},{5,6},{6,7},{7,8},{8,9},{9,10},{10,1... | collective-permute-start | bytes 416 | tf_op jit(solution)/shard_map/ppermute | solution.py:28
  541.3 8.2 %all-to-all-start.4 = ((f32[16,2,256]{2,1,0:T(2,128)}), f32[16,2,256]{2,1,0:T(2,128)S(1)}, u32[]{:S(2)}, u32[]{:S(2)}) async-start(f32[16,2,256]{2,1,0:T(2,128)} %all_to_all.86), calls=%async_computation.4 | async-start | bytes 65536 | tf_op jit(solution)/shard_map/all_to_all | solution.py:303
  552.1 4.7 all-to-all-done.4
  (422 shorter events, 237.4 us)
Async XLA Ops:
  5.8 19.3 %collective-permute-start.1 = (f32[5,1,512]{2,1,0:T(1,128)S(1)}, f32[5,1,512]{2,1,0:T(1,128)S(1)}, u32[]{:S(2)}, u32[]{:S(2)}) collective-permute-start(f32[5,1,512]{2,1,0:T(1,128)S(1)} %copy.41), channel_id=1, source_target_pairs={{16,0},{32,16},{48,32},{64,48},{80,64},{96,80},{112,96},{17,1},{33... | collective-permute-start | bytes 30728 | tf_op jit(solution)/shard_map/ppermute | solution.py:29
  10.9 14.6 %collective-permute-start = (f32[5,1,512]{2,1,0:T(1,128)S(1)}, f32[5,1,512]{2,1,0:T(1,128)S(1)}, u32[]{:S(2)}, u32[]{:S(2)}) collective-permute-start(f32[5,1,512]{2,1,0:T(1,128)S(1)} %copy.40), channel_id=1, source_target_pairs={{0,16},{16,32},{32,48},{48,64},{64,80},{80,96},{96,112},{1,17},{17... | collective-permute-start | bytes 30728 | tf_op jit(solution)/shard_map/ppermute | solution.py:28
  12.9 24.1 %all-to-all-start = ((f32[2,16,256]{2,0,1:T(2,128)}), f32[2,16,256]{2,0,1:T(2,128)S(1)}, u32[]{:S(2)}, u32[]{:S(2)}) async-start(f32[2,16,256]{2,0,1:T(2,128)} %bitcast.5), calls=%async_computation | async-start | bytes 65536 | tf_op jit(solution)/shard_map/all_to_all | solution.py:228
  37.0 17.5 %all-to-all-start.1 = ((f32[2,16,256]{2,0,1:T(2,128)}), f32[2,16,256]{2,0,1:T(2,128)S(1)}, u32[]{:S(2)}, u32[]{:S(2)}) async-start(f32[2,16,256]{2,0,1:T(2,128)} %bitcast.146), calls=%async_computation.1 | async-start | bytes 65536 | tf_op jit(solution)/shard_map/all_to_all | solution.py:229
  46.0 15.3 %collective-permute-start.5 = (f32[1,3,256]{2,1,0:T(4,128)S(1)}, f32[1,3,256]{2,1,0:T(4,128)S(1)}, u32[]{:S(2)}, u32[]{:S(2)}) collective-permute-start(f32[1,3,256]{2,1,0:T(4,128)S(1)} %get-tuple-element.198), channel_id=1, source_target_pairs={{16,0},{32,16},{48,32},{64,48},{80,64},{96,80},{112,96},{17,1},{33... | collective-permute-start | bytes 9224 | tf_op jit(solution)/shard_map/ppermute | solution.py:29
  52.5 8.9 %collective-permute-start.4 = (f32[1,3,256]{2,1,0:T(4,128)S(1)}, f32[1,3,256]{2,1,0:T(4,128)S(1)}, u32[]{:S(2)}, u32[]{:S(2)}) collective-permute-start(f32[1,3,256]{2,1,0:T(4,128)S(1)} %get-tuple-element.197), channel_id=1, source_target_pairs={{0,16},{16,32},{32,48},{48,64},{64,80},{80,96},{96,112},{1,17},{17... | collective-permute-start | bytes 9224 | tf_op jit(solution)/shard_map/ppermute | solution.py:28
  54.5 14.2 %all-to-all-start.2 = ((f32[2,16,256]{2,0,1:T(2,128)}), f32[2,16,256]{2,0,1:T(2,128)S(1)}, u32[]{:S(2)}, u32[]{:S(2)}) async-start(f32[2,16,256]{2,0,1:T(2,128)} %bitcast.148), calls=%async_computation.2 | async-start | bytes 65536 | tf_op jit(solution)/shard_map/all_to_all | solution.py:230
  68.7 11.0 %all-to-all-start.3 = ((f32[2,16,256]{2,0,1:T(2,128)}), f32[2,16,256]{2,0,1:T(2,128)S(1)}, u32[]{:S(2)}, u32[]{:S(2)}) async-start(f32[2,16,256]{2,0,1:T(2,128)} %bitcast.150), calls=%async_computation.3 | async-start | bytes 65536 | tf_op jit(solution)/shard_map/all_to_all | solution.py:231
  72.4 7.9 %collective-permute-start.7 = (f32[1,38,3]{2,1,0:T(8,128)S(1)}, f32[1,38,3]{2,1,0:T(8,128)S(1)}, u32[]{:S(2)}, u32[]{:S(2)}) collective-permute-start(f32[1,38,3]{2,1,0:T(8,128)S(1)} %get-tuple-element.190), channel_id=1, source_target_pairs={{1,0},{2,1},{3,2},{4,3},{5,4},{6,5},{7,6},{8,7},{9,8},{10,9},{11,1... | collective-permute-start | bytes 1376 | tf_op jit(solution)/shard_map/ppermute | solution.py:29
  89.3 11.2 %collective-permute-start.9 = (f32[5,1,512]{2,1,0:T(1,128)}, f32[5,1,512]{2,1,0:T(1,128)}, u32[]{:S(2)}, u32[]{:S(2)}) collective-permute-start(f32[5,1,512]{2,1,0:T(1,128)} %copy.49), channel_id=1, source_target_pairs={{16,0},{32,16},{48,32},{64,48},{80,64},{96,80},{112,96},{17,1},{33... | collective-permute-start | bytes 30728 | tf_op jit(solution)/shard_map/ppermute | solution.py:29
  106.7 8.7 %collective-permute-start.11 = (f32[5,66,1]{1,2,0:T(1,128)S(1)}, f32[5,66,1]{1,2,0:T(1,128)S(1)}, u32[]{:S(2)}, u32[]{:S(2)}) collective-permute-start(f32[5,66,1]{1,2,0:T(1,128)S(1)} %get-tuple-element.104), channel_id=1, source_target_pairs={{1,0},{2,1},{3,2},{4,3},{5,4},{6,5},{7,6},{8,7},{9,8},{10,9},{11,1... | collective-permute-start | bytes 3968 | tf_op jit(solution)/shard_map/ppermute | solution.py:29
  124.0 8.3 %collective-permute-start.13 = (f32[5,1,512]{2,1,0:T(1,128)}, f32[5,1,512]{2,1,0:T(1,128)}, u32[]{:S(2)}, u32[]{:S(2)}) collective-permute-start(f32[5,1,512]{2,1,0:T(1,128)} %copy.53), channel_id=1, source_target_pairs={{16,0},{32,16},{48,32},{64,48},{80,64},{96,80},{112,96},{17,1},{33... | collective-permute-start | bytes 30728 | tf_op jit(solution)/shard_map/ppermute | solution.py:29
  138.5 8.6 %collective-permute-start.15 = (f32[5,66,1]{1,2,0:T(1,128)S(1)}, f32[5,66,1]{1,2,0:T(1,128)S(1)}, u32[]{:S(2)}, u32[]{:S(2)}) collective-permute-start(f32[5,66,1]{1,2,0:T(1,128)S(1)} %get-tuple-element.102), channel_id=1, source_target_pairs={{1,0},{2,1},{3,2},{4,3},{5,4},{6,5},{7,6},{8,7},{9,8},{10,9},{11,1... | collective-permute-start | bytes 3968 | tf_op jit(solution)/shard_map/ppermute | solution.py:29
  140.4 7.3 %collective-permute-start.14 = (f32[5,66,1]{1,2,0:T(1,128)S(1)}, f32[5,66,1]{1,2,0:T(1,128)S(1)}, u32[]{:S(2)}, u32[]{:S(2)}) collective-permute-start(f32[5,66,1]{1,2,0:T(1,128)S(1)} %get-tuple-element.101), channel_id=1, source_target_pairs={{0,1},{1,2},{2,3},{3,4},{4,5},{5,6},{6,7},{7,8},{8,9},{9,10},{10,1... | collective-permute-start | bytes 3968 | tf_op jit(solution)/shard_map/ppermute | solution.py:28
  155.9 8.2 %collective-permute-start.17 = (f32[5,1,512]{2,1,0:T(1,128)}, f32[5,1,512]{2,1,0:T(1,128)}, u32[]{:S(2)}, u32[]{:S(2)}) collective-permute-start(f32[5,1,512]{2,1,0:T(1,128)} %copy.57), channel_id=1, source_target_pairs={{16,0},{32,16},{48,32},{64,48},{80,64},{96,80},{112,96},{17,1},{33... | collective-permute-start | bytes 30728 | tf_op jit(solution)/shard_map/ppermute | solution.py:29
  170.3 8.7 %collective-permute-start.19 = (f32[5,66,1]{1,2,0:T(1,128)S(1)}, f32[5,66,1]{1,2,0:T(1,128)S(1)}, u32[]{:S(2)}, u32[]{:S(2)}) collective-permute-start(f32[5,66,1]{1,2,0:T(1,128)S(1)} %get-tuple-element.100), channel_id=1, source_target_pairs={{1,0},{2,1},{3,2},{4,3},{5,4},{6,5},{7,6},{8,7},{9,8},{10,9},{11,1... | collective-permute-start | bytes 3968 | tf_op jit(solution)/shard_map/ppermute | solution.py:29
  187.7 8.3 %collective-permute-start.21 = (f32[5,1,512]{2,1,0:T(1,128)}, f32[5,1,512]{2,1,0:T(1,128)}, u32[]{:S(2)}, u32[]{:S(2)}) collective-permute-start(f32[5,1,512]{2,1,0:T(1,128)} %copy.61), channel_id=1, source_target_pairs={{16,0},{32,16},{48,32},{64,48},{80,64},{96,80},{112,96},{17,1},{33... | collective-permute-start | bytes 30728 | tf_op jit(solution)/shard_map/ppermute | solution.py:29
  202.1 8.5 %collective-permute-start.23 = (f32[5,66,1]{1,2,0:T(1,128)S(1)}, f32[5,66,1]{1,2,0:T(1,128)S(1)}, u32[]{:S(2)}, u32[]{:S(2)}) collective-permute-start(f32[5,66,1]{1,2,0:T(1,128)S(1)} %get-tuple-element.98), channel_id=1, source_target_pairs={{1,0},{2,1},{3,2},{4,3},{5,4},{6,5},{7,6},{8,7},{9,8},{10,9},{11,1... | collective-permute-start | bytes 3968 | tf_op jit(solution)/shard_map/ppermute | solution.py:29
  219.5 8.3 %collective-permute-start.25 = (f32[5,1,512]{2,1,0:T(1,128)}, f32[5,1,512]{2,1,0:T(1,128)}, u32[]{:S(2)}, u32[]{:S(2)}) collective-permute-start(f32[5,1,512]{2,1,0:T(1,128)} %copy.65), channel_id=1, source_target_pairs={{16,0},{32,16},{48,32},{64,48},{80,64},{96,80},{112,96},{17,1},{33... | collective-permute-start | bytes 30728 | tf_op jit(solution)/shard_map/ppermute | solution.py:29
  234.0 8.9 %collective-permute-start.27 = (f32[5,66,1]{1,2,0:T(1,128)S(1)}, f32[5,66,1]{1,2,0:T(1,128)S(1)}, u32[]{:S(2)}, u32[]{:S(2)}) collective-permute-start(f32[5,66,1]{1,2,0:T(1,128)S(1)} %get-tuple-element.96), channel_id=1, source_target_pairs={{1,0},{2,1},{3,2},{4,3},{5,4},{6,5},{7,6},{8,7},{9,8},{10,9},{11,1... | collective-permute-start | bytes 3968 | tf_op jit(solution)/shard_map/ppermute | solution.py:29
  251.4 8.3 %collective-permute-start.29 = (f32[5,1,512]{2,1,0:T(1,128)}, f32[5,1,512]{2,1,0:T(1,128)}, u32[]{:S(2)}, u32[]{:S(2)}) collective-permute-start(f32[5,1,512]{2,1,0:T(1,128)} %copy.69), channel_id=1, source_target_pairs={{16,0},{32,16},{48,32},{64,48},{80,64},{96,80},{112,96},{17,1},{33... | collective-permute-start | bytes 30728 | tf_op jit(solution)/shard_map/ppermute | solution.py:29
  265.8 8.5 %collective-permute-start.31 = (f32[5,66,1]{1,2,0:T(1,128)S(1)}, f32[5,66,1]{1,2,0:T(1,128)S(1)}, u32[]{:S(2)}, u32[]{:S(2)}) collective-permute-start(f32[5,66,1]{1,2,0:T(1,128)S(1)} %get-tuple-element.94), channel_id=1, source_target_pairs={{1,0},{2,1},{3,2},{4,3},{5,4},{6,5},{7,6},{8,7},{9,8},{10,9},{11,1... | collective-permute-start | bytes 3968 | tf_op jit(solution)/shard_map/ppermute | solution.py:29
  283.2 8.3 %collective-permute-start.33 = (f32[5,1,512]{2,1,0:T(1,128)}, f32[5,1,512]{2,1,0:T(1,128)}, u32[]{:S(2)}, u32[]{:S(2)}) collective-permute-start(f32[5,1,512]{2,1,0:T(1,128)} %copy.73), channel_id=1, source_target_pairs={{16,0},{32,16},{48,32},{64,48},{80,64},{96,80},{112,96},{17,1},{33... | collective-permute-start | bytes 30728 | tf_op jit(solution)/shard_map/ppermute | solution.py:29
  297.7 10.0 %collective-permute-start.35 = (f32[5,66,1]{1,2,0:T(1,128)S(1)}, f32[5,66,1]{1,2,0:T(1,128)S(1)}, u32[]{:S(2)}, u32[]{:S(2)}) collective-permute-start(f32[5,66,1]{1,2,0:T(1,128)S(1)} %get-tuple-element.92), channel_id=1, source_target_pairs={{1,0},{2,1},{3,2},{4,3},{5,4},{6,5},{7,6},{8,7},{9,8},{10,9},{11,1... | collective-permute-start | bytes 3968 | tf_op jit(solution)/shard_map/ppermute | solution.py:29
  299.6 8.1 %collective-permute-start.34 = (f32[5,66,1]{1,2,0:T(1,128)S(1)}, f32[5,66,1]{1,2,0:T(1,128)S(1)}, u32[]{:S(2)}, u32[]{:S(2)}) collective-permute-start(f32[5,66,1]{1,2,0:T(1,128)S(1)} %get-tuple-element.91), channel_id=1, source_target_pairs={{0,1},{1,2},{2,3},{3,4},{4,5},{5,6},{6,7},{7,8},{8,9},{9,10},{10,1... | collective-permute-start | bytes 3968 | tf_op jit(solution)/shard_map/ppermute | solution.py:28
  335.4 9.4 %collective-permute-start.39 = (f32[2,34,1]{2,1,0:T(8,128)S(1)}, f32[2,34,1]{2,1,0:T(8,128)S(1)}, u32[]{:S(2)}, u32[]{:S(2)}) collective-permute-start(f32[2,34,1]{2,1,0:T(8,128)S(1)} %get-tuple-element.178), channel_id=1, source_target_pairs={{1,0},{2,1},{3,2},{4,3},{5,4},{6,5},{7,6},{8,7},{9,8},{10,9},{11,1... | collective-permute-start | bytes 824 | tf_op jit(solution)/shard_map/ppermute | solution.py:29
  337.3 8.4 %collective-permute-start.38 = (f32[2,34,1]{2,1,0:T(8,128)S(1)}, f32[2,34,1]{2,1,0:T(8,128)S(1)}, u32[]{:S(2)}, u32[]{:S(2)}) collective-permute-start(f32[2,34,1]{2,1,0:T(8,128)S(1)} %get-tuple-element.177), channel_id=1, source_target_pairs={{0,1},{1,2},{2,3},{3,4},{4,5},{5,6},{6,7},{7,8},{8,9},{9,10},{10,1... | collective-permute-start | bytes 824 | tf_op jit(solution)/shard_map/ppermute | solution.py:28
  512.7 8.5 %collective-permute-start.47 = (f32[1,34,1]{2,1,0:T(8,128)S(1)}, f32[1,34,1]{2,1,0:T(8,128)S(1)}, u32[]{:S(2)}, u32[]{:S(2)}) collective-permute-start(f32[1,34,1]{2,1,0:T(8,128)S(1)} %get-tuple-element.186), channel_id=1, source_target_pairs={{1,0},{2,1},{3,2},{4,3},{5,4},{6,5},{7,6},{8,7},{9,8},{10,9},{11,1... | collective-permute-start | bytes 416 | tf_op jit(solution)/shard_map/ppermute | solution.py:29
  514.7 7.3 %collective-permute-start.46 = (f32[1,34,1]{2,1,0:T(8,128)S(1)}, f32[1,34,1]{2,1,0:T(8,128)S(1)}, u32[]{:S(2)}, u32[]{:S(2)}) collective-permute-start(f32[1,34,1]{2,1,0:T(8,128)S(1)} %get-tuple-element.185), channel_id=1, source_target_pairs={{0,1},{1,2},{2,3},{3,4},{4,5},{5,6},{6,7},{7,8},{8,9},{9,10},{10,1... | collective-permute-start | bytes 416 | tf_op jit(solution)/shard_map/ppermute | solution.py:28
  530.8 8.8 %collective-permute-start.51 = (f32[1,34,1]{2,1,0:T(8,128)S(1)}, f32[1,34,1]{2,1,0:T(8,128)S(1)}, u32[]{:S(2)}, u32[]{:S(2)}) collective-permute-start(f32[1,34,1]{2,1,0:T(8,128)S(1)} %get-tuple-element.184), channel_id=1, source_target_pairs={{1,0},{2,1},{3,2},{4,3},{5,4},{6,5},{7,6},{8,7},{9,8},{10,9},{11,1... | collective-permute-start | bytes 416 | tf_op jit(solution)/shard_map/ppermute | solution.py:29
  532.7 7.7 %collective-permute-start.50 = (f32[1,34,1]{2,1,0:T(8,128)S(1)}, f32[1,34,1]{2,1,0:T(8,128)S(1)}, u32[]{:S(2)}, u32[]{:S(2)}) collective-permute-start(f32[1,34,1]{2,1,0:T(8,128)S(1)} %get-tuple-element.183), channel_id=1, source_target_pairs={{0,1},{1,2},{2,3},{3,4},{4,5},{5,6},{6,7},{7,8},{8,9},{9,10},{10,1... | collective-permute-start | bytes 416 | tf_op jit(solution)/shard_map/ppermute | solution.py:28
  541.3 15.5 %all-to-all-start.4 = ((f32[16,2,256]{2,1,0:T(2,128)}), f32[16,2,256]{2,1,0:T(2,128)S(1)}, u32[]{:S(2)}, u32[]{:S(2)}) async-start(f32[16,2,256]{2,1,0:T(2,128)} %all_to_all.86), calls=%async_computation.4 | async-start | bytes 65536 | tf_op jit(solution)/shard_map/all_to_all | solution.py:303
  (76 other events, 983.3 us)
where the time goes:
time: 568 us; the launch traced here: 558 us
  starting transfers between devices  221 us (39%)
  blocking collectives  136 us (24%)
  local copies, waits for them, and re-layouts  88.1 us (16%)
  other arithmetic  61.1 us (11%)
  waiting for transfers between devices  45 us (8%)
  between operations  5.88 us (1%)
    ppermute x26, starting transfers between devices, with_halo(): before = lax.ppermute(last, axis, up)  106 us
    ppermute x26, starting transfers between devices, with_halo(): after = lax.ppermute(first, axis, down)  78.8 us
    pmax x1, blocking collectives, heat_solve(): bound_high = lax.pmax(jnp.max(1.0 + off_ratio), ('gx', 'gy'))  72.4 us
    pmin x1, blocking collectives, heat_solve(): bound_low = lax.pmin(jnp.min(1.0 - off_ratio), ('gx', 'gy'))  64.1 us
    ppermute x26, waiting for transfers between devices, with_halo(): before = lax.ppermute(last, axis, up)  32.9 us
    slice x25, local copies, waits for them, and re-layouts, with_halo(): last = lax.slice_in_dim(value, length - width, length, axis=dim)  18.8 us
    slice x8, local copies, waits for them, and re-layouts, with_halo(): first = lax.slice_in_dim(value, 0, width, axis=dim)  16.6 us
    ppermute x8, local copies, waits for them, and re-layouts, with_halo(): before = lax.ppermute(last, axis, up)  16 us
  transfers between devices with their start and end apart: 57, of which 25 were waited for; matrix products, arithmetic and copies ran while one was open for 8% of the time, Pallas kernels for 0%

commit v1 on v0

v1 whole, which is shorter than its diff:
```python
import jax
import jax.numpy as jnp
from jax import lax
from jax.experimental import pallas as pl
from jax.experimental.pallas import tpu as pltpu
from jax.sharding import PartitionSpec as P

F32 = jnp.float32
ROWS, COLS = 64, 512
CROWS, CCOLS = 32, 256
GX, GY = 8, 16
HALO = 8
HROW = 16
EROWS = ROWS + 2 * HROW
ECOLS = COLS + 128
WCOLS = CCOLS + 128
HEAT_ROWS = CROWS + 8
SUBSTEPS = 8
SEG = 128
TIME_STEP = 0.4
DAMPING = 0.05
EXPANSION = 0.6
LOG2E = 1.4426950408889634
HI = lax.Precision.HIGHEST
CHUNK = 56
PAYLOAD = 480 + 48 + 24 + 24 + 16


def lanes(shape):
    return lax.broadcasted_iota(jnp.int32, shape, len(shape) - 1)


def sublanes(shape):
    return lax.broadcasted_iota(jnp.int32, shape, len(shape) - 2)


def turn(value, shift, axis):
    size = value.shape[axis]
    shift %= size
    return value if shift == 0 else pltpu.roll(value, shift, axis)


def mark_rows(marks, first, count, width):
    parts = [
        jnp.full((8, width), marks[first // 8 + k, 0].astype(F32), F32) for k in range(count // 8)
    ]
    return jnp.concatenate(parts, axis=0)


def own_tile(f, u, v, d, marks, rows, first_lane):
    row0, count = rows
    window = (pl.ds(row0, count), pl.ds(first_lane, 128))
    if f < 2:
        return u[(f, *window)]
    if f < 4:
        return TIME_STEP * v[(f - 2, *window)]
    weight = mark_rows(marks, row0, count, 128)
    if f < 6:
        return 1.0 - d[(f - 4, *window)].astype(F32) * (0.125 * weight)
    return weight


def pack_kernel(marks, u, v, d, warm, cap, film, bath, out, lines):
    gy = lax.axis_index("gy")
    lines[0:2, :] = warm[...]
    lines[2:4, :] = cap[...] + film[...]
    lines[4:6, :] = film[...] * (bath[...] - warm[...])
    lines[6:8, :] = jnp.zeros((2, GY * CCOLS), F32)
    lane = lanes((8, 128))
    zero = jnp.zeros((32, 128), F32)
    for g in range(GY):
        at = g * CCOLS
        out[g, 0:8, :] = lines[:, at : at + 128]
        out[g, 8:16, :] = lines[:, at + 128 : at + 256]
        if g > 0:
            left = lines[:, at - 128 : at]
        else:
            left = jnp.broadcast_to(lines[:, 0:1], (8, 128))
        if g < GY - 1:
            right = lines[:, at + 256 : at + 384]
        else:
            right = jnp.broadcast_to(lines[:, GY * CCOLS - 1 : GY * CCOLS], (8, 128))
        out[g, 16:24, :] = jnp.where(lane < 64, right, left)
        out[g, 24:CHUNK, :] = zero

    def edge(first_lane, inner):
        wide = lanes((ROWS, 128))
        packed = jnp.zeros((ROWS, 128), F32)
        for f in range(7):
            tile = own_tile(f, u, v, d, marks, (0, ROWS), first_lane)
            moved = turn(tile, 8 * f - inner, 1)
            packed = jnp.where((wide >= 8 * f) & (wide < 8 * f + 8), moved, packed)
        return packed[:32] + turn(packed[32:], 64, 1)

    @pl.when(gy < GY - 1)
    def _():
        out[gy + 1, 24:CHUNK, :] = edge(COLS - 128, 120)

    @pl.when(gy > 0)
    def _():
        out[gy - 1, 24:CHUNK, :] = edge(0, 0)


def side_tile(f, left, right, row0, count):
    if row0 + count <= 32:
        at, inner = row0, 0
    else:
        at, inner = row0 - 32, 64
    lane = lanes((count, 128))
    from_right = turn(right[at : at + count], -(inner + 8 * f), 1)
    from_left = turn(left[at : at + count], 120 - inner - 8 * f, 1)
    return jnp.where(lane < 8, from_right, jnp.where(lane >= 120, from_left, 0.0))


def sides(recv):
    gy = lax.axis_index("gy")
    left = recv[jnp.maximum(gy - 1, 0), 24:CHUNK, :]
    right = recv[jnp.minimum(gy + 1, GY - 1), 24:CHUNK, :]
    return left, right


def weight_tile(marks, left, right, row0, count):
    lane = lanes((count, 128))
    side = side_tile(6, left, right, row0, count)
    own = mark_rows(marks, row0, count, 128)
    return jnp.where((lane < 8) | (lane >= 120), side, own)


def rim_kernel(marks, u, v, d, recv, up, down):
    left, right = sides(recv)
    for out, row0, coarse0, thin0 in ((up, ROWS - HROW, 16, 24), (down, 0, 0, 0)):
        for f in range(6):
            for k in range(5):
                at = (f * 5 + k) * 16
                if k < 4:
                    tile = own_tile(f, u, v, d, marks, (row0, HROW), 128 * k)
                else:
                    tile = side_tile(f, left, right, row0, HROW)
                out[at : at + 16, :] = tile
        for k in range(3):
            for r in range(0, 16, 2):
                g = (coarse0 + r) // 2
                out[480 + 16 * k + r : 482 + 16 * k + r, :] = recv[g, 8 * k : 8 * k + 2, :]
            for r in range(0, 8, 2):
                g = (thin0 + r) // 2
                for a, base in ((1, 528), (2, 552)):
                    out[base + 8 * k + r : base + 8 * k + r + 2, :] = recv[
                        g, 8 * k + 2 * a : 8 * k + 2 * a + 2, :
                    ]
        out[576:592, :] = weight_tile(marks, left, right, row0, HROW)


def plate_kernel(
    marks, u, v, d, recv, above, below,
    shift_out, speed_out, damage_out, resist_out, coarse_out,
    u0, u1, v0, v1, sx, sy, cw, tx, ty, temp, coarse, gap,
):
    gx = lax.axis_index("gx")
    gy = lax.axis_index("gy")
    left, right = sides(recv)
    fields = (u0, u1, v0, v1, sx, sy)
    pad = 8
    for f, ref in enumerate(fields):
        ref[0:pad, :] = jnp.zeros((pad, ECOLS), F32)
        for k in range(5):
            at = (f * 5 + k) * 16
            cols = pl.ds(128 * k, 128)
            ref[pl.ds(pad, HROW), cols] = above[at : at + 16, :]
            ref[pl.ds(pad + HROW + ROWS, HROW), cols] = below[at : at + 16, :]
            if k < 4:
                ref[pl.ds(pad + HROW, ROWS), cols] = own_tile(f, u, v, d, marks, (0, ROWS), 128 * k)
            else:
                for half in (0, 32):
                    ref[pl.ds(pad + HROW + half, 32), cols] = side_tile(f, left, right, half, 32)
    rate = -4.0 * LOG2E
    for base, source in ((0, above), (HROW + ROWS, below)):
        tile = rate * source[576:592, :]
        cw[pl.ds(base, HROW), pl.ds(COLS, 128)] = tile
        cw[pl.ds(base, HROW), pl.ds(0, COLS)] = jnp.broadcast_to(tile[:, 64:65], (HROW, COLS))
    cw[pl.ds(HROW, ROWS), pl.ds(0, COLS)] = rate * mark_rows(marks, 0, ROWS, COLS)
    for half in (0, 32):
        cw[pl.ds(HROW + half, 32), pl.ds(COLS, 128)] = rate * weight_tile(marks, left, right, half, 32)

    for k in range(3):
        cols = pl.ds(128 * k, 128)
        coarse[0, 0:16, cols] = above[480 + 16 * k : 496 + 16 * k, :]
        coarse[0, 48:64, cols] = below[480 + 16 * k : 496 + 16 * k, :]
        for a, base in ((1, 528), (2, 552)):
            coarse[a, 8:16, cols] = above[base + 8 * k : base + 8 * k + 8, :]
            coarse[a, 48:56, cols] = below[base + 8 * k : base + 8 * k + 8, :]
        for g in range(GY):
            for a in range(3):
                coarse[a, 16 + 2 * g : 18 + 2 * g, cols] = recv[g, 8 * k + 2 * a : 8 * k + 2 * a + 2, :]

    @pl.when(gx == 0)
    def _():
        coarse[0, 0:16, :] = jnp.broadcast_to(coarse[0, 16:17, :], (16, WCOLS))
        coarse[1, 8:16, :] = jnp.ones((8, WCOLS), F32)

    @pl.when(gx == GX - 1)
    def _():
        coarse[0, 48:64, :] = jnp.broadcast_to(coarse[0, 47:48, :], (16, WCOLS))
        coarse[1, 48:56, :] = jnp.ones((8, WCOLS), F32)

    coarse_out[...] = coarse[:, 12 : 12 + HEAT_ROWS, :]

    p = sublanes((128, 128))
    q = lanes((128, 128))
    middle = 32 + q // 2
    beside = middle + 2 * (q % 2) - 1
    widen = jnp.where(p == middle, 0.75, 0.0) + jnp.where(p == beside, 0.25, 0.0)
    i = sublanes((EROWS, 64))
    c = lanes((EROWS, 64))
    middle = 8 + i // 2
    beside = middle + 2 * (i % 2) - 1
    raise_ = jnp.where(c == middle, 0.75, 0.0) + jnp.where(c == beside, 0.25, 0.0)
    warm = coarse[0]

    def columns(k):
        window = turn(warm, 32 - 64 * k, 1)[:, 0:128]
        return jnp.dot(window, widen, precision=HI, preferred_element_type=F32)

    lane64 = lanes((64, 128))
    tiles = [columns(k) for k in range(4)]
    tiles.append(jnp.where(lane64 < 64, columns(4), columns(-1)))
    temp[0:pad, :] = jnp.zeros((pad, ECOLS), F32)
    for k in range(5):
        temp[pl.ds(pad, EROWS), pl.ds(128 * k, 128)] = jnp.dot(
            raise_, tiles[k], precision=HI, preferred_element_type=F32
        )
    lane = lanes((8, ECOLS))
    col = gy * COLS + jnp.where(lane < COLS + 64, lane, lane - ECOLS)
    inner_col = (col >= 1) & (col < GY * COLS)
    for b in range(EROWS // 8):
        own = temp[pl.ds(pad + 8 * b, 8), :]
        tx[pl.ds(8 * b, 8), :] = (0.5 * EXPANSION) * (own + temp[pl.ds(pad + 8 * b - 1, 8), :])
        ty[pl.ds(8 * b, 8), :] = (0.5 * EXPANSION) * (own + turn(own, 1, 1))
        row = gx * ROWS - HROW + 8 * b + sublanes((8, ECOLS))
        here = pl.ds(pad + 8 * b, 8)
        sx[here, :] = jnp.where((row >= 1) & (row < GX * ROWS), sx[here, :], 0.0)
        sy[here, :] = jnp.where(inner_col, sy[here, :], 0.0)

    last_row = sublanes((8, ECOLS)) == 7
    keep = 1.0 - TIME_STEP * DAMPING
    push = TIME_STEP * TIME_STEP

    def substep(_, carry):
        next_nx = jnp.zeros((8, ECOLS), F32)
        next_ax = jnp.zeros((8, ECOLS), F32)
        for b in reversed(range(EROWS // 8)):
            here = pl.ds(pad + 8 * b, 8)
            over = pl.ds(pad + 8 * b - 1, 8)
            flat = pl.ds(8 * b, 8)
            a0, a1 = u0[here, :], u1[here, :]
            rate_here = cw[flat, :]
            open_x = a0 - u0[over, :] - tx[flat, :]
            shear_x = a1 - u1[over, :]
            stretch = jnp.maximum(open_x, 0.0)
            spring_x = jnp.minimum(sx[here, :], jnp.exp2(rate_here * (stretch * stretch)))
            sx[here, :] = spring_x
            nx = spring_x * open_x
            ax = spring_x * shear_x
            open_y = a1 - turn(a1, 1, 1) - ty[flat, :]
            shear_y = a0 - turn(a0, 1, 1)
            stretch = jnp.maximum(open_y, 0.0)
            spring_y = jnp.minimum(sy[here, :], jnp.exp2(rate_here * (stretch * stretch)))
            sy[here, :] = spring_y
            ny = spring_y * open_y
            ay = spring_y * shear_y
            roll_nx = turn(nx, -1, 0)
            roll_ax = turn(ax, -1, 0)
            force0 = jnp.where(last_row, next_nx, roll_nx) - nx + (turn(ay, -1, 1) - ay)
            force1 = jnp.where(last_row, next_ax, roll_ax) - ax + (turn(ny, -1, 1) - ny)
            next_nx, next_ax = roll_nx, roll_ax
            b0 = keep * v0[here, :] + push * force0
            b1 = keep * v1[here, :] + push * force1
            v0[here, :] = b0
            v1[here, :] = b1
            u0[here, :] = a0 + b0
            u1[here, :] = a1 + b1
        return carry

    lax.fori_loop(0, SUBSTEPS, substep, 0)

    own = (pl.ds(pad + HROW, ROWS), pl.ds(0, COLS))
    shift_out[0] = u0[own]
    shift_out[1] = u1[own]
    speed_out[0] = v0[own] * (1.0 / TIME_STEP)
    speed_out[1] = v1[own] * (1.0 / TIME_STEP)
    for b in range(10):
        rows = pl.ds(pad + 8 + 8 * b, 8)
        row = gx * ROWS - 8 + 8 * b + sublanes((8, COLS))
        col = gy * COLS + lanes((8, COLS))
        dx = jnp.where(row >= 1, 1.0 - sx[rows, pl.ds(0, COLS)], 0.0)
        dy = jnp.where(col >= 1, 1.0 - sy[rows, pl.ds(0, COLS)], 0.0)
        gap[pl.ds(8 * b, 8), :] = dx + dy
        if 1 <= b < 9:
            damage_out[0, pl.ds(8 * b - 8, 8), :] = dx.astype(jnp.bfloat16)
            damage_out[1, pl.ds(8 * b - 8, 8), :] = dy.astype(jnp.bfloat16)
    p = sublanes((256, 128))
    q = lanes((256, 128))
    place = (p % SEG).astype(F32)
    even = (2 * (q % 64)).astype(F32)
    table = jnp.exp(jnp.abs(place - even) * (-4.0 / SEG)) + jnp.exp(
        jnp.abs(place - even - 1.0) * (-4.0 / SEG)
    )
    table = jnp.where(p // SEG == q // 64, table * (0.5 * 2.0 / SEG), 0.0)
    for k in range(2):
        wide = pl.ds(256 * k, 256)
        a = sublanes((HEAT_ROWS, 2 * HEAT_ROWS))
        c = lanes((HEAT_ROWS, 2 * HEAT_ROWS))
        pool = jnp.where(c // 2 == a, 1.0, 0.0)
        pair = jnp.dot(pool, gap[:, wide], precision=HI, preferred_element_type=F32)
        resist_out[:, pl.ds(128 * k, 128)] = jnp.dot(
            pair, table, precision=HI, preferred_element_type=F32
        )


def conductances(resist, from_left, from_right, coarse):
    gx = lax.axis_index("gx")
    gy = lax.axis_index("gy")
    shape = (HEAT_ROWS, WCOLS)
    lane = lanes((HEAT_ROWS, 128))
    rim = jnp.where(lane < 64, from_right[...], from_left[...])
    wide = jnp.concatenate([resist[...], rim], axis=1)
    warm = coarse[0]
    conduct = (1.0 + 0.5 * warm) / (1.0 + wide)
    row = gx * CROWS - 4 + sublanes(shape)
    lane = lanes(shape)
    col = gy * CCOLS + jnp.where(lane < CCOLS + 64, lane, lane - WCOLS)
    down = jnp.where(
        (row >= 1) & (row < GX * CROWS), 0.5 * (conduct + turn(conduct, 1, 0)), 0.0
    )
    side = jnp.where(
        (col >= 1) & (col < GY * CCOLS), 0.5 * (conduct + turn(conduct, 1, 1)), 0.0
    )
    up = turn(down, -1, 0)
    far = turn(side, -1, 1)
    offsum = down + up + side + far
    return warm, down, up, side, far, offsum, coarse[1] + offsum


def bound_kernel(resist, from_left, from_right, coarse, out):
    parts = conductances(resist, from_left, from_right, coarse)
    ratio = (parts[5] / parts[6])[4 : 4 + CROWS, 0:CCOLS]
    top = jnp.max(ratio, axis=(0, 1), keepdims=True)
    out[...] = jnp.broadcast_to(top[None], (GX, 8, 128))


def solve_kernel(resist, from_left, from_right, coarse, tops, out):
    warm, down, up, side, far, _, diagonal = conductances(resist, from_left, from_right, coarse)
    inverse = 1.0 / diagonal

    def spread(x):
        return (
            down * turn(x, 1, 0) + up * turn(x, -1, 0) + side * turn(x, 1, 1) + far * turn(x, -1, 1)
        ) * inverse

    start = coarse[2] + (
        down * (turn(warm, 1, 0) - warm)
        + up * (turn(warm, -1, 0) - warm)
        + side * (turn(warm, 1, 1) - warm)
        + far * (turn(warm, -1, 1) - warm)
    )
    z = start * inverse
    y = z + spread(z)
    y2 = spread(spread(y))
    top = jnp.max(jnp.max(tops[...], axis=0), axis=(0, 1), keepdims=True)
    line = jnp.broadcast_to(top, (4, CCOLS))
    for g in range(GY):
        out[g, 0:2, :] = y[4 + 2 * g : 6 + 2 * g, 0:CCOLS]
        out[g, 2:4, :] = y2[4 + 2 * g : 6 + 2 * g, 0:CCOLS]
        out[g, 4:8, :] = line


def finish_kernel(recv, warm, out):
    top = jnp.max(recv[0, 4:8, :], axis=(0, 1), keepdims=True)
    for g in range(1, GY):
        top = jnp.maximum(top, jnp.max(recv[g, 4:8, :], axis=(0, 1), keepdims=True))
    square = top * top
    gain = 8.0 / (8.0 - 8.0 * square + square * square)
    near = gain * (1.0 - square)
    for g in range(GY):
        at = pl.ds(CCOLS * g, CCOLS)
        out[:, at] = warm[:, at] + near * recv[g, 0:2, :] + gain * recv[g, 2:4, :]


def vmem(count):
    return [pl.BlockSpec(memory_space=pltpu.VMEM)] * count


MARKS = pl.BlockSpec(memory_space=pltpu.SMEM)
PARAMS = pltpu.CompilerParams(vmem_limit_bytes=32 * 1024 * 1024)


def shaped(*shape, dtype=F32):
    return jax.ShapeDtypeStruct(shape, dtype)


def neighbours(value_up, value_down, axis):
    count = lax.axis_size(axis)
    ahead = [(i, i + 1) for i in range(count - 1)]
    back = [(j, i) for i, j in ahead]
    return lax.ppermute(value_up, axis, ahead), lax.ppermute(value_down, axis, back)


def exchange(value, axis):
    return lax.all_to_all(value, axis, split_axis=0, concat_axis=0, tiled=True)


def per_device(u, v, d, marks, warm, cap, film, bath):
    packed = pl.pallas_call(
        pack_kernel,
        out_shape=shaped(GY, CHUNK, 128),
        in_specs=[MARKS] + vmem(7),
        out_specs=vmem(1)[0],
        scratch_shapes=[pltpu.VMEM((8, GY * CCOLS), F32)],
        compiler_params=PARAMS,
        name="pack",
    )(marks, u, v, d, warm, cap, film, bath)
    recv = exchange(packed, "gy")
    up, down = pl.pallas_call(
        rim_kernel,
        out_shape=(shaped(PAYLOAD, 128), shaped(PAYLOAD, 128)),
        in_specs=[MARKS] + vmem(4),
        out_specs=tuple(vmem(2)),
        compiler_params=PARAMS,
        name="rim",
    )(marks, u, v, d, recv)
    above, below = neighbours(up, down, "gx")
    fine = pltpu.VMEM((EROWS + 8, ECOLS), F32)
    flat = pltpu.VMEM((EROWS, ECOLS), F32)
    shift, speed, damage, resist, coarse = pl.pallas_call(
        plate_kernel,
        out_shape=(
            shaped(2, ROWS, COLS),
            shaped(2, ROWS, COLS),
            shaped(2, ROWS, COLS, dtype=jnp.bfloat16),
            shaped(HEAT_ROWS, CCOLS),
            shaped(3, HEAT_ROWS, WCOLS),
        ),
        in_specs=[MARKS] + vmem(6),
        out_specs=tuple(vmem(5)),
        scratch_shapes=[fine] * 6
        + [flat] * 3
        + [fine, pltpu.VMEM((3, 64, WCOLS), F32), pltpu.VMEM((80, COLS), F32)],
        compiler_params=PARAMS,
        name="plate",
    )(marks, u, v, d, recv, above, below)
    from_left, from_right = neighbours(resist[:, 128:256], resist[:, 0:128], "gy")
    tops = pl.pallas_call(
        bound_kernel,
        out_shape=shaped(GX, 8, 128),
        in_specs=vmem(4),
        out_specs=vmem(1)[0],
        compiler_params=PARAMS,
        name="bound",
    )(resist, from_left, from_right, coarse)
    tops = exchange(tops, "gx")
    answer = pl.pallas_call(
        solve_kernel,
        out_shape=shaped(GY, 8, CCOLS),
        in_specs=vmem(5),
        out_specs=vmem(1)[0],
        compiler_params=PARAMS,
        name="solve",
    )(resist, from_left, from_right, coarse, tops)
    answer = exchange(answer, "gy")
    warmth = pl.pallas_call(
        finish_kernel,
        out_shape=shaped(2, GY * CCOLS),
        in_specs=vmem(2),
        out_specs=vmem(1)[0],
        compiler_params=PARAMS,
        name="finish",
    )(answer, warm)
    return shift, speed, damage, warmth


def solution(mesh):
    tile = P(None, "gx", "gy")
    line = P(("gx", "gy"), None)
    return jax.shard_map(
        per_device,
        mesh=mesh,
        in_specs=(tile, tile, tile, P("gx", "gy"), line, line, line, line),
        out_specs=(tile, tile, tile, line),
        check_vma=False,
    )
```

time: 568 us -> 86.8 us (0.15)
  the two profiles are of different devices: /device:TPU:3 before, /device:TPU:1 now
where the time goes in v1:
time: 86.8 us; the launch traced here: 86.1 us
  blocking collectives  46 us (53%)
  Pallas kernels  12.2 us (14%)
  starting transfers between devices  11.9 us (14%)
  waiting for transfers between devices  8.7 us (10%)
  local copies, waits for them, and re-layouts  6.62 us (8%)
    all_to_all x3, blocking collectives, exchange(): return lax.all_to_all(value, axis, split_axis=0, concat_axis=0, tiled=True)  46 us
    pallas_call x1, Pallas kernels, per_device(): pl.pallas_call(plate_kernel, out_shape=(shaped(2, ROWS, COLS), shaped(2,...  8.9 us
    unnamed x17, local copies, waits for them, and re-layouts  6.61 us
    ppermute x2, starting transfers between devices, neighbours(): lax.ppermute(value_up, axis, ahead)  6.32 us
    ppermute x2, starting transfers between devices, neighbours(): lax.ppermute(value_down, axis, back)  5.56 us
    ppermute x2, waiting for transfers between devices, neighbours(): lax.ppermute(value_up, axis, ahead)  4.85 us
    ppermute x2, waiting for transfers between devices, neighbours(): lax.ppermute(value_down, axis, back)  3.85 us
  transfers between devices with their start and end apart: 4, of which 3 were waited for; matrix products, arithmetic and copies ran while one was open for 0% of the time, Pallas kernels for 0%

profile of v1, /device:TPU:1, one launch (start us, length us, event | category | flops | bytes accessed | tf_op | source)
XLA Modules:
  0.0 86.1 jit_solution(12235855948816148370)
XLA Ops:
  0.6 0.7 copy.14.marks
  1.4 0.0 copy-start
  1.4 0.9 %copy-done = f32[2,64,512]{2,1,0:T(8,128)S(1)} copy-done((f32[2,64,512]{2,1,0:T(8,128)S(1)}, f32[2,64,512]{2,1,0:T(8,128)}, u32[]{:S(2)}) %copy-start) | copy-done | bytes 262168
  2.3 0.0 copy-start.1
  2.3 0.9 %copy-done.1 = f32[2,64,512]{2,1,0:T(8,128)S(1)} copy-done((f32[2,64,512]{2,1,0:T(8,128)S(1)}, f32[2,64,512]{2,1,0:T(8,128)}, u32[]{:S(2)}) %copy-start.1) | copy-done | bytes 262168
  3.3 0.0 copy-start.2
  3.3 0.9 %copy-done.2 = s32[2,64,512]{2,1,0:T(8,128)S(1)} copy-done((s32[2,64,512]{2,1,0:T(8,128)S(1)}, s32[2,64,512]{2,1,0:T(8,128)}, u32[]{:S(2)}) %copy-start.2) | copy-done | bytes 262168
  4.2 0.0 copy-start.3
  4.2 0.8 copy-done.3
  5.0 0.0 copy-start.5
  5.0 0.8 copy-done.5
  5.7 0.8 copy-done.6
  6.5 0.8 copy-done.7
  7.2 1.0 %pack.1 = f32[16,56,128]{2,1,0:T(8,128)S(1)} custom-call(s32[8,1]{1,0:T(8,128)S(1)} %copy.14.marks, f32[2,64,512]{2,1,0:T(8,128)S(1)} %copy-done, f32[2,64,512]{2,1,0:T(8,128)S(1)} %copy-done.1, s32[2,64,512]{2,1,0:T(8,128)S(1)} %copy-done.2, f32[2,4096]{1,0:T(2,128)S(1)} %copy-done.3, f32[2,4096]{1,0:T(2,128)S(1)} %copy-done.5, f32[2,4096]{1,0:T(2,128)S(1)} %copy-done.6, ...), custom_call_target="tpu_custom_call" | custom-call | tf_op jit(solution)/shard_map/pack/pallas_call | solution.py:412
  8.3 19.7 %all_to_all.15.recv = f32[16,56,128]{2,1,0:T(8,128)S(1)} all-to-all(f32[16,56,128]{2,1,0:T(8,128)S(1)} %pack.1), channel_id=1, replica_groups=mesh['gx'=8,'gy'=16] {'gy'}, dimensions={0} | all-to-all | bytes 917504 | tf_op jit(solution)/shard_map/all_to_all | solution.py:408
  27.9 0.7 rim.1
  28.7 3.2 %collective-permute-start = (f32[592,128]{1,0:T(8,128)S(1)}, f32[592,128]{1,0:T(8,128)S(1)}, u32[]{:S(2)}, u32[]{:S(2)}) collective-permute-start(f32[592,128]{1,0:T(8,128)S(1)} %get-tuple-element.11), channel_id=1, source_target_pairs={{0,16},{16,32},{32,48},{48,64},{64,80},{80,96},{96,112},{1,17},{17... | collective-permute-start | bytes 909320 | tf_op jit(solution)/shard_map/ppermute | solution.py:404
  31.9 1.3 %collective-permute-start.1 = (f32[592,128]{1,0:T(8,128)S(1)}, f32[592,128]{1,0:T(8,128)S(1)}, u32[]{:S(2)}, u32[]{:S(2)}) collective-permute-start(f32[592,128]{1,0:T(8,128)S(1)} %get-tuple-element.12), channel_id=1, source_target_pairs={{16,0},{32,16},{48,32},{64,48},{80,64},{96,80},{112,96},{17,1},{33... | collective-permute-start | bytes 909320 | tf_op jit(solution)/shard_map/ppermute | solution.py:404
  33.2 4.0 %collective-permute-done.above = f32[592,128]{1,0:T(8,128)S(1)} collective-permute-done((f32[592,128]{1,0:T(8,128)S(1)}, f32[592,128]{1,0:T(8,128)S(1)}, u32[]{:S(2)}, u32[]{:S(2)}) %collective-permute-start) | collective-permute-done | bytes 303136 | tf_op jit(solution)/shard_map/ppermute | solution.py:404
  37.2 3.9 %collective-permute-done.1.below = f32[592,128]{1,0:T(8,128)S(1)} collective-permute-done((f32[592,128]{1,0:T(8,128)S(1)}, f32[592,128]{1,0:T(8,128)S(1)}, u32[]{:S(2)}, u32[]{:S(2)}) %collective-permute-start.1) | collective-permute-done | bytes 303136 | tf_op jit(solution)/shard_map/ppermute | solution.py:404
  41.0 8.9 %plate.1 = (f32[2,64,512]{2,1,0:T(8,128)}, f32[2,64,512]{2,1,0:T(8,128)}, bf16[2,64,512]{2,1,0:T(8,128)(2,1)}, f32[40,256]{1,0:T(8,128)S(1)}, f32[3,40,384]{2,1,0:T(8,128)S(1)}) custom-call(s32[8,1]{1,0:T(8,128)S(1)} %copy.14.marks, f32[2,64,512]{2,1,0:T(8,128)S(1)} %copy-done, f32[2,64,512]{2,1,0:T(8,128)S(1)} %copy-done.1, s32[2,64,512]{2,1,0:T(8,128)S(1)} %copy-done.2, ...), custom_call_target="tpu_custom_call" | custom-call | tf_op jit(solution)/shard_map/plate/pallas_call | solution.py:433
  49.9 4.3 %collective-permute-start.3 = (f32[40,128]{1,0:T(8,128)S(1)}, f32[40,128]{1,0:T(8,128)S(1)}, u32[]{:S(2)}, u32[]{:S(2)}) collective-permute-start(f32[40,128]{1,0:T(8,128)S(1)} %get-tuple-element.18), channel_id=1, source_target_pairs={{1,0},{2,1},{3,2},{4,3},{5,4},{6,5},{7,6},{8,7},{9,8},{10,9},{11,1... | collective-permute-start | bytes 61448 | tf_op jit(solution)/shard_map/ppermute | solution.py:404
  54.2 3.1 %collective-permute-start.2 = (f32[40,128]{1,0:T(8,128)S(1)}, f32[40,128]{1,0:T(8,128)S(1)}, u32[]{:S(2)}, u32[]{:S(2)}) collective-permute-start(f32[40,128]{1,0:T(8,128)S(1)} %get-tuple-element.19), channel_id=1, source_target_pairs={{0,1},{1,2},{2,3},{3,4},{4,5},{5,6},{6,7},{7,8},{8,9},{9,10},{10,1... | collective-permute-start | bytes 61448 | tf_op jit(solution)/shard_map/ppermute | solution.py:404
  57.3 0.0 collective-permute-done.3.from_right
  57.3 0.9 %collective-permute-done.2.from_left = f32[40,128]{1,0:T(8,128)S(1)} collective-permute-done((f32[40,128]{1,0:T(8,128)S(1)}, f32[40,128]{1,0:T(8,128)S(1)}, u32[]{:S(2)}, u32[]{:S(2)}) %collective-permute-start.2) | collective-permute-done | bytes 20512 | tf_op jit(solution)/shard_map/ppermute | solution.py:404
  58.2 0.3 bound.1
  58.5 10.3 %all_to_all.16.tops = f32[8,8,128]{2,1,0:T(8,128)S(1)} all-to-all(f32[8,8,128]{2,1,0:T(8,128)S(1)} %bound.1), channel_id=1, replica_groups=mesh['gx'=8,'gy'=16] {'gx'}, dimensions={0} | all-to-all | bytes 65536 | tf_op jit(solution)/shard_map/all_to_all | solution.py:408
  68.8 0.5 solve.1
  69.3 0.0 copy-start.4
  69.3 16.0 %all_to_all.17.recv = f32[16,8,256]{2,1,0:T(8,128)S(1)} all-to-all(f32[16,8,256]{2,1,0:T(8,128)S(1)} %solve.1), channel_id=1, replica_groups=mesh['gx'=8,'gy'=16] {'gy'}, dimensions={0} | all-to-all | bytes 262144 | tf_op jit(solution)/shard_map/all_to_all | solution.py:408
  85.3 0.0 copy-done.4
  85.3 0.8 finish.1
  (3 shorter events, 0.0 us)
Async XLA Ops:
  1.4 0.9 %copy-start = (f32[2,64,512]{2,1,0:T(8,128)S(1)}, f32[2,64,512]{2,1,0:T(8,128)}, u32[]{:S(2)}) copy-start(f32[2,64,512]{2,1,0:T(8,128)} %u.5) | copy-start | bytes 786436
  2.3 0.9 %copy-start.1 = (f32[2,64,512]{2,1,0:T(8,128)S(1)}, f32[2,64,512]{2,1,0:T(8,128)}, u32[]{:S(2)}) copy-start(f32[2,64,512]{2,1,0:T(8,128)} %v.5) | copy-start | bytes 786436
  3.3 0.9 %copy-start.2 = (s32[2,64,512]{2,1,0:T(8,128)S(1)}, s32[2,64,512]{2,1,0:T(8,128)}, u32[]{:S(2)}) copy-start(s32[2,64,512]{2,1,0:T(8,128)} %d.5) | copy-start | bytes 786436
  4.2 0.8 copy-start.3
  5.0 0.8 copy-start.5
  5.7 0.8 copy-start.6
  6.5 0.8 copy-start.7
  28.7 8.5 %collective-permute-start = (f32[592,128]{1,0:T(8,128)S(1)}, f32[592,128]{1,0:T(8,128)S(1)}, u32[]{:S(2)}, u32[]{:S(2)}) collective-permute-start(f32[592,128]{1,0:T(8,128)S(1)} %get-tuple-element.11), channel_id=1, source_target_pairs={{0,16},{16,32},{32,48},{48,64},{64,80},{80,96},{96,112},{1,17},{17... | collective-permute-start | bytes 909320 | tf_op jit(solution)/shard_map/ppermute | solution.py:404
  31.9 9.1 %collective-permute-start.1 = (f32[592,128]{1,0:T(8,128)S(1)}, f32[592,128]{1,0:T(8,128)S(1)}, u32[]{:S(2)}, u32[]{:S(2)}) collective-permute-start(f32[592,128]{1,0:T(8,128)S(1)} %get-tuple-element.12), channel_id=1, source_target_pairs={{16,0},{32,16},{48,32},{64,48},{80,64},{96,80},{112,96},{17,1},{33... | collective-permute-start | bytes 909320 | tf_op jit(solution)/shard_map/ppermute | solution.py:404
  49.9 7.4 %collective-permute-start.3 = (f32[40,128]{1,0:T(8,128)S(1)}, f32[40,128]{1,0:T(8,128)S(1)}, u32[]{:S(2)}, u32[]{:S(2)}) collective-permute-start(f32[40,128]{1,0:T(8,128)S(1)} %get-tuple-element.18), channel_id=1, source_target_pairs={{1,0},{2,1},{3,2},{4,3},{5,4},{6,5},{7,6},{8,7},{9,8},{10,9},{11,1... | collective-permute-start | bytes 61448 | tf_op jit(solution)/shard_map/ppermute | solution.py:404
  54.2 4.0 %collective-permute-start.2 = (f32[40,128]{1,0:T(8,128)S(1)}, f32[40,128]{1,0:T(8,128)S(1)}, u32[]{:S(2)}, u32[]{:S(2)}) collective-permute-start(f32[40,128]{1,0:T(8,128)S(1)} %get-tuple-element.19), channel_id=1, source_target_pairs={{0,1},{1,2},{2,3},{3,4},{4,5},{5,6},{6,7},{7,8},{8,9},{9,10},{10,1... | collective-permute-start | bytes 61448 | tf_op jit(solution)/shard_map/ppermute | solution.py:404
  69.3 16.0 %copy-start.4 = (f32[2,4096]{1,0:T(2,128)S(1)}, f32[2,4096]{1,0:T(2,128)}, u32[]{:S(2)}) copy-start(f32[2,4096]{1,0:T(2,128)} %warm.3) | copy-start | bytes 98308

commit v2 on v1

v2 whole, which is shorter than its diff:
```python
import jax
import jax.numpy as jnp
from jax import lax
from jax.experimental import pallas as pl
from jax.experimental.pallas import tpu as pltpu
from jax.sharding import PartitionSpec as P

F32 = jnp.float32
ROWS, COLS = 64, 512
CROWS, CCOLS = 32, 256
GX, GY = 8, 16
HALO = 8
HROW = 16
EROWS = ROWS + 2 * HROW
ECOLS = COLS + 128
WCOLS = CCOLS + 128
HEAT_ROWS = CROWS + 8
BAND = EROWS // 8
SUBSTEPS = 8
SEG = 128
TIME_STEP = 0.4
DAMPING = 0.05
EXPANSION = 0.6
LOG2E = 1.4426950408889634
HI = lax.Precision.HIGHEST
CHUNK = 56
CORNER = 16 + 48 + 24 + 24


def lanes(shape):
    return lax.broadcasted_iota(jnp.int32, shape, len(shape) - 1)


def sublanes(shape):
    return lax.broadcasted_iota(jnp.int32, shape, len(shape) - 2)


def turn(value, shift, axis):
    size = value.shape[axis]
    shift %= size
    return value if shift == 0 else pltpu.roll(value, shift, axis)


def mark_rows(marks, first, count, width):
    parts = [
        jnp.full((8, width), marks[first // 8 + k].astype(F32), F32) for k in range(count // 8)
    ]
    return jnp.concatenate(parts, axis=0)


def own_spring(d, marks, f, row0, count, first_lane, width):
    weight = mark_rows(marks, row0, count, width)
    level = d[f, pl.ds(row0, count), pl.ds(first_lane, width)].astype(F32)
    return 1.0 - level * (0.125 * weight)


def start_all(copies):
    for copy in copies:
        copy.start()


def wait_all(copies):
    for copy in copies:
        copy.wait()


def pack_kernel(
    marks, u_hbm, v_hbm, d_hbm, warm_hbm, cap_hbm, film_hbm, bath_hbm,
    out, up, down,
    u, v, d, warm, cap, film, bath, lines, sem,
):
    pairs = (
        (warm_hbm, warm), (cap_hbm, cap), (film_hbm, film), (bath_hbm, bath),
        (u_hbm, u), (v_hbm, v), (d_hbm, d),
    )
    copies = [pltpu.make_async_copy(a, b, sem.at[k]) for k, (a, b) in enumerate(pairs)]
    start_all(copies)
    gy = lax.axis_index("gy")
    zero = jnp.zeros((32, 128), F32)
    for g in range(GY):
        out[g, 24:CHUNK, :] = zero
    wait_all(copies)
    for message, row0 in ((up, ROWS - HROW), (down, 0)):
        rows = pl.ds(row0, HROW)
        for f in range(2):
            for k in range(4):
                cols = pl.ds(128 * k, 128)
                message[f, k] = u[f, rows, cols]
                message[2 + f, k] = v[f, rows, cols]
                message[4 + f, k] = own_spring(d, marks, f, row0, HROW, 128 * k, 128)

    lines[0:2, :] = warm[...]
    lines[2:4, :] = cap[...] + film[...]
    lines[4:6, :] = film[...] * (bath[...] - warm[...])
    lines[6:8, :] = jnp.zeros((2, GY * CCOLS), F32)
    lane = lanes((8, 128))
    for g in range(GY):
        at = g * CCOLS
        out[g, 0:8, :] = lines[:, at : at + 128]
        out[g, 8:16, :] = lines[:, at + 128 : at + 256]
        if g > 0:
            left = lines[:, at - 128 : at]
        else:
            left = jnp.broadcast_to(lines[:, 0:1], (8, 128))
        if g < GY - 1:
            right = lines[:, at + 256 : at + 384]
        else:
            right = jnp.broadcast_to(lines[:, GY * CCOLS - 1 : GY * CCOLS], (8, 128))
        out[g, 16:24, :] = jnp.where(lane < 64, right, left)

    def edge(first_lane, inner):
        wide = lanes((ROWS, 128))
        window = (slice(None), pl.ds(first_lane, 128))
        packed = jnp.zeros((ROWS, 128), F32)
        for f in range(7):
            if f < 2:
                tile = u[(f, *window)]
            elif f < 4:
                tile = v[(f - 2, *window)]
            elif f < 6:
                tile = own_spring(d, marks, f - 4, 0, ROWS, first_lane, 128)
            else:
                tile = mark_rows(marks, 0, ROWS, 128)
            moved = turn(tile, 8 * f - inner, 1)
            packed = jnp.where((wide >= 8 * f) & (wide < 8 * f + 8), moved, packed)
        return packed[:32] + turn(packed[32:], 64, 1)

    @pl.when(gy < GY - 1)
    def _():
        out[gy + 1, 24:CHUNK, :] = edge(COLS - 128, 120)

    @pl.when(gy > 0)
    def _():
        out[gy - 1, 24:CHUNK, :] = edge(0, 0)


def join_sides(f, left, left_at, right, right_at):
    lane = lanes(left.shape)
    from_right = turn(right, -(right_at + 8 * f), 1)
    from_left = turn(left, 120 - left_at - 8 * f, 1)
    return jnp.where(lane < 8, from_right, jnp.where(lane >= 120, from_left, 0.0))


def sides(recv):
    gy = lax.axis_index("gy")
    left = recv[jnp.maximum(gy - 1, 0), 24:CHUNK, :]
    right = recv[jnp.minimum(gy + 1, GY - 1), 24:CHUNK, :]
    return left, right


def rim_kernel(marks, recv, up, down):
    left, right = sides(recv)
    lane = lanes((HROW, 128))
    for out, row0, coarse0, thin0 in ((up, ROWS - HROW, 16, 24), (down, 0, 0, 0)):
        if row0 == 0:
            near, off = left[0:16], turn(right[0:16], 64, 1)
        else:
            near, off = turn(left[16:32], 64, 1), right[16:32]
        corner = jnp.where(lane < 56, near, off)
        out[0:16, :] = jnp.where(
            (lane >= 56) & (lane < 64), mark_rows(marks, row0, HROW, 128), corner
        )
        for k in range(3):
            for r in range(0, 16, 2):
                g = (coarse0 + r) // 2
                out[16 + 16 * k + r : 18 + 16 * k + r, :] = recv[g, 8 * k : 8 * k + 2, :]
            for r in range(0, 8, 2):
                g = (thin0 + r) // 2
                for a, base in ((1, 64), (2, 88)):
                    out[base + 8 * k + r : base + 8 * k + r + 2, :] = recv[
                        g, 8 * k + 2 * a : 8 * k + 2 * a + 2, :
                    ]


def plate_kernel(
    marks, u, v, d, recv, above_rows, below_rows, above, below,
    shift_out, speed_out, damage_out, resist_out, coarse_out, tops_out,
    field, cw, temp, state, rate, warmth, tx, ty, coarse, gap, worn, sem,
):
    gx = lax.axis_index("gx")
    gy = lax.axis_index("gy")
    top = pl.ds(0, HROW)
    mid = pl.ds(HROW, ROWS)
    low = pl.ds(HROW + ROWS, HROW)
    copies = [
        pltpu.make_async_copy(above_rows, field.at[:, 0:4, top], sem.at[0]),
        pltpu.make_async_copy(below_rows, field.at[:, 0:4, low], sem.at[1]),
    ]
    results = []
    for k in range(4):
        cols = pl.ds(128 * k, 128)
        for f, (source, target) in enumerate(((u, shift_out), (v, speed_out))):
            here = field.at[2 * f : 2 * f + 2, k, mid]
            at = 2 + 2 * k + f
            copies.append(pltpu.make_async_copy(source.at[:, :, cols], here, sem.at[at]))
            results.append(pltpu.make_async_copy(here, target.at[:, :, cols], sem.at[8 + at]))
    results.append(pltpu.make_async_copy(worn, damage_out, sem.at[18]))
    start_all(copies)

    for k in range(3):
        cols = pl.ds(128 * k, 128)
        coarse[0, 0:16, cols] = above[16 + 16 * k : 32 + 16 * k, :]
        coarse[0, 48:64, cols] = below[16 + 16 * k : 32 + 16 * k, :]
        for a, base in ((1, 64), (2, 88)):
            coarse[a, 8:16, cols] = above[base + 8 * k : base + 8 * k + 8, :]
            coarse[a, 48:56, cols] = below[base + 8 * k : base + 8 * k + 8, :]
        for g in range(GY):
            for a in range(3):
                coarse[a, 16 + 2 * g : 18 + 2 * g, cols] = recv[g, 8 * k + 2 * a : 8 * k + 2 * a + 2, :]

    @pl.when(gx == 0)
    def _():
        coarse[0, 0:16, :] = jnp.broadcast_to(coarse[0, 16:17, :], (16, WCOLS))
        coarse[1, 8:16, :] = jnp.ones((8, WCOLS), F32)

    @pl.when(gx == GX - 1)
    def _():
        coarse[0, 48:64, :] = jnp.broadcast_to(coarse[0, 47:48, :], (16, WCOLS))
        coarse[1, 48:56, :] = jnp.ones((8, WCOLS), F32)

    coarse_out[...] = coarse[:, 12 : 12 + HEAT_ROWS, :]

    p = sublanes((128, 128))
    q = lanes((128, 128))
    middle = 32 + q // 2
    beside = middle + 2 * (q % 2) - 1
    widen = jnp.where(p == middle, 0.75, 0.0) + jnp.where(p == beside, 0.25, 0.0)
    i = sublanes((EROWS, 64))
    c = lanes((EROWS, 64))
    middle = 8 + i // 2
    beside = middle + 2 * (i % 2) - 1
    raise_ = jnp.where(c == middle, 0.75, 0.0) + jnp.where(c == beside, 0.25, 0.0)
    warm = coarse[0]

    def columns(k):
        window = turn(warm, 32 - 64 * k, 1)[:, 0:128]
        return jnp.dot(window, widen, precision=HI, preferred_element_type=F32)

    lane64 = lanes((64, 128))
    tiles = [columns(k) for k in range(4)]
    tiles.append(jnp.where(lane64 < 64, columns(4), columns(-1)))
    for k in range(5):
        temp[k] = jnp.dot(
            raise_, tiles[k], precision=HI, preferred_element_type=F32
        )

    left, right = sides(recv)
    for f in range(6):
        for rows, source in ((top, above), (low, below)):
            tile = source[0:16, :]
            field[f, 4, rows, :] = join_sides(f, tile, 0, tile, 64)
        for half in (0, 32):
            field[f, 4, pl.ds(HROW + half, 32), :] = join_sides(f, left, half * 2, right, half * 2)
    factor = -4.0 * LOG2E
    for base, source in ((0, above), (HROW + ROWS, below)):
        tile = factor * source[0:16, :]
        cw[1, pl.ds(base, HROW), :] = join_sides(6, tile, 0, tile, 64)
        cw[0, pl.ds(base, HROW), :] = jnp.broadcast_to(tile[:, 60:61], (HROW, 128))
    cw[0, mid, :] = factor * mark_rows(marks, 0, ROWS, 128)
    for half in (0, 32):
        cw[1, pl.ds(HROW + half, 32), :] = factor * join_sides(6, left, half * 2, right, half * 2)
    for f in range(2):
        for k in range(4):
            field[4 + f, k, mid, :] = own_spring(d, marks, f, 0, ROWS, 128 * k, 128)
    wait_all(copies)

    lane = lanes((8, 128))
    first = gx * ROWS - HROW + BAND * sublanes((8, 128))
    for t in range(BAND):
        strip = pl.ds(t, 8, stride=BAND)
        row = first + t
        inner_row = (row >= 1) & (row < GX * ROWS)
        own_rate = cw[0, strip, :]
        side_rate = cw[1, strip, :]
        for k in range(5):
            cols = pl.ds(128 * k, 128)
            rate[t, :, cols] = own_rate if k < 4 else side_rate
            warmth[t, :, cols] = (0.5 * EXPANSION) * temp[k, strip, :]
            for f in range(4):
                state[f, t, :, cols] = field[f, k, strip, :]
            state[4, t, :, cols] = jnp.where(inner_row, field[4, k, strip, :], 0.0)
            spring = field[5, k, strip, :]
            if k in (0, 4):
                col = gy * COLS + (lane if k == 0 else jnp.where(lane < 64, lane + COLS, lane - 128))
                spring = jnp.where((col >= 1) & (col < GY * COLS), spring, 0.0)
            state[5, t, :, cols] = spring
    before = turn(warmth[BAND - 1], 1, 0)
    for t in range(BAND):
        own = warmth[t]
        tx[t] = own + before
        ty[t] = own + turn(own, 1, 1)
        before = own

    keep = 1.0 - TIME_STEP * DAMPING

    def edge_x(t, a0, a1, o0, o1):
        open_x = a0 - o0 - tx[t]
        stretch = jnp.maximum(open_x, 0.0)
        spring = jnp.minimum(state[4, t], jnp.exp2(rate[t] * (stretch * stretch)))
        state[4, t] = spring
        return spring * open_x, spring * (a1 - o1)

    def substep(_, carry):
        a0, a1 = state[0, BAND - 1], state[1, BAND - 1]
        first_nx, first_ax = edge_x(0, state[0, 0], state[1, 0], turn(a0, 1, 0), turn(a1, 1, 0))
        next_nx, next_ax = turn(first_nx, -1, 0), turn(first_ax, -1, 0)
        for t in reversed(range(BAND)):
            open_y = a1 - turn(a1, 1, 1) - ty[t]
            stretch = jnp.maximum(open_y, 0.0)
            spring = jnp.minimum(state[5, t], jnp.exp2(rate[t] * (stretch * stretch)))
            state[5, t] = spring
            ny = spring * open_y
            ay = spring * (a0 - turn(a0, 1, 1))
            if t > 0:
                o0, o1 = state[0, t - 1], state[1, t - 1]
                nx, ax = edge_x(t, a0, a1, o0, o1)
            else:
                o0, o1 = a0, a1
                nx, ax = first_nx, first_ax
            force0 = (next_nx - nx) + (turn(ay, -1, 1) - ay)
            force1 = (next_ax - ax) + (turn(ny, -1, 1) - ny)
            next_nx, next_ax = nx, ax
            b0 = keep * state[2, t] + TIME_STEP * force0
            b1 = keep * state[3, t] + TIME_STEP * force1
            state[2, t] = b0
            state[3, t] = b1
            state[0, t] = a0 + TIME_STEP * b0
            state[1, t] = a1 + TIME_STEP * b1
            a0, a1 = o0, o1
        return carry

    lax.fori_loop(0, SUBSTEPS, substep, 0)
    for f in range(6):
        for t in range(BAND):
            for k in range(4):
                field[f, k, pl.ds(t, 8, stride=BAND), :] = state[f, t, :, pl.ds(128 * k, 128)]
        if f == 3:
            start_all(results[:-1])
    for b in range(10):
        rows = pl.ds(8 + 8 * b, 8)
        row = gx * ROWS - 8 + 8 * b + sublanes((8, 128))
        for k in range(4):
            cols = pl.ds(128 * k, 128)
            dx = jnp.where(row >= 1, 1.0 - field[4, k, rows, :], 0.0)
            dy = 1.0 - field[5, k, rows, :]
            if k == 0:
                dy = jnp.where(gy * COLS + lane >= 1, dy, 0.0)
            gap[pl.ds(8 * b, 8), cols] = dx + dy
            if 1 <= b < 9:
                worn[0, pl.ds(8 * b - 8, 8), cols] = dx.astype(jnp.bfloat16)
                worn[1, pl.ds(8 * b - 8, 8), cols] = dy.astype(jnp.bfloat16)
    start_all(results[-1:])
    p = sublanes((256, 128))
    q = lanes((256, 128))
    place = (p % SEG).astype(F32)
    even = (2 * (q % 64)).astype(F32)
    table = jnp.exp(jnp.abs(place - even) * (-4.0 / SEG)) + jnp.exp(
        jnp.abs(place - even - 1.0) * (-4.0 / SEG)
    )
    table = jnp.where(p // SEG == q // 64, table * (0.5 * 2.0 / SEG), 0.0)
    a = sublanes((HEAT_ROWS, 2 * HEAT_ROWS))
    c = lanes((HEAT_ROWS, 2 * HEAT_ROWS))
    pool = jnp.where(c // 2 == a, 1.0, 0.0)
    for k in range(2):
        pair = jnp.dot(pool, gap[:, pl.ds(256 * k, 256)], precision=HI, preferred_element_type=F32)
        resist_out[:, pl.ds(128 * k, 128)] = jnp.dot(
            pair, table, precision=HI, preferred_element_type=F32
        )
    conduct = (1.0 + 0.5 * coarse[0, 12 : 12 + HEAT_ROWS, 0:CCOLS]) / (1.0 + resist_out[...])
    shape = (HEAT_ROWS, CCOLS)
    row = gx * CROWS - 4 + sublanes(shape)
    down = jnp.where((row >= 1) & (row < GX * CROWS), 0.5 * (conduct + turn(conduct, 1, 0)), 0.0)
    side = jnp.where(lanes(shape) >= 1, 0.5 * (conduct + turn(conduct, 1, 1)), 0.0)
    offsum = (down + turn(down, -1, 0) + side + turn(side, -1, 1))[4 : 4 + CROWS]
    capacity = coarse[1, 16:48, 0:CCOLS]
    top = jnp.max(offsum / (capacity + offsum), axis=(0, 1), keepdims=True)
    a = sublanes((8, CCOLS))
    c = lanes((8, CCOLS))
    border = jnp.where(sublanes((8, 128)) >= 6, top, 0.0)
    for k, value in enumerate((offsum, capacity, conduct[4 : 4 + CROWS])):
        pick = jnp.where(
            ((a == 2 * k) & (c == 0)) | ((a == 2 * k + 1) & (c == CCOLS - 1)), 1.0, 0.0
        )
        border += lax.dot_general(
            pick,
            jnp.concatenate([value] * 4, axis=0),
            (((1,), (1,)), ((), ())),
            precision=HI,
            preferred_element_type=F32,
        )
    for g in range(GX):
        tops_out[g] = border
    wait_all(results)


def conductances(resist, from_left, coarse):
    gx = lax.axis_index("gx")
    gy = lax.axis_index("gy")
    shape = (HEAT_ROWS, WCOLS)
    lane = lanes((HEAT_ROWS, 128))
    rim = jnp.where(lane < 64, 0.0, from_left[...])
    wide = jnp.concatenate([resist[...], rim], axis=1)
    warm = coarse[0]
    conduct = (1.0 + 0.5 * warm) / (1.0 + wide)
    row = gx * CROWS - 4 + sublanes(shape)
    lane = lanes(shape)
    col = gy * CCOLS + jnp.where(lane < CCOLS + 64, lane, lane - WCOLS)
    down = jnp.where(
        (row >= 1) & (row < GX * CROWS), 0.5 * (conduct + turn(conduct, 1, 0)), 0.0
    )
    side = jnp.where(
        (col >= 1) & (col < GY * CCOLS), 0.5 * (conduct + turn(conduct, 1, 1)), 0.0
    )
    up = turn(down, -1, 0)
    far = turn(side, -1, 1)
    offsum = down + up + side + far
    return warm, down, up, side, far, offsum, coarse[1] + offsum


def solve_kernel(resist, from_left, coarse, tops, out):
    warm, down, up, side, far, _, diagonal = conductances(resist, from_left, coarse)
    inverse = 1.0 / diagonal

    def spread(x):
        return (
            down * turn(x, 1, 0) + up * turn(x, -1, 0) + side * turn(x, 1, 1) + far * turn(x, -1, 1)
        ) * inverse

    start = coarse[2] + (
        down * (turn(warm, 1, 0) - warm)
        + up * (turn(warm, -1, 0) - warm)
        + side * (turn(warm, 1, 1) - warm)
        + far * (turn(warm, -1, 1) - warm)
    )
    z = start * inverse
    y = z + spread(z)
    y2 = turn(spread(spread(y)), 4, 1)
    y = turn(y, 4, 1)
    group = lanes((8, 128)) // 32
    strip = []
    for h in range(2):
        tile = tops[4 * h]
        for k in range(1, 4):
            tile = jnp.where(group == k, tops[4 * h + k], tile)
        strip.append(tile)
    for g in range(GY):
        rows = slice(4 + 2 * g, 6 + 2 * g)
        out[g, 0:2, :] = y[rows, 0:CCOLS]
        out[g, 2:4, :] = y2[rows, 0:CCOLS]
        out[g, 4:6, 0:128] = y[rows, CCOLS:]
        out[g, 4:6, 128:256] = y2[rows, CCOLS:]
        out[g, 8:16, 0:128] = strip[0]
        out[g, 8:16, 128:256] = strip[1]


def finish_kernel(recv, warm, out, wide, border):
    for g in range(GY):
        for k in range(7):
            border[k, g : g + 1, :] = recv[g, 8 + k : 9 + k, :]
    across = 0.5 * (turn(border[5], 1, 0) + border[4])
    across = jnp.where(sublanes((GY, CCOLS)) >= 1, across, 0.0)
    top = border[6]
    for k, face in ((0, across), (1, turn(across, -1, 0))):
        offsum = border[k] + face
        top = jnp.maximum(top, offsum / (border[2 + k] + offsum))
    top = jnp.max(top, axis=(0, 1), keepdims=True)
    square = top * top
    gain = 8.0 / (8.0 - 8.0 * square + square * square)
    near = gain * (1.0 - square)
    for g in range(GY):
        wide[:, pl.ds(CCOLS * g, CCOLS)] = near * recv[g, 0:2, :] + gain * recv[g, 2:4, :]
    wide[:, pl.ds(CCOLS * GY, 128)] = (
        near * recv[GY - 1, 4:6, 0:128] + gain * recv[GY - 1, 4:6, 128:256]
    )
    out[...] = warm[...] + turn(wide[...], -4, 1)[:, : GY * CCOLS]


def vmem(count):
    return [pl.BlockSpec(memory_space=pltpu.VMEM)] * count


MARKS = pl.BlockSpec(memory_space=pltpu.SMEM)
ANY = pl.BlockSpec(memory_space=pl.ANY)
FAR = pl.BlockSpec(memory_space=pltpu.MemorySpace.HBM)
PARAMS = pltpu.CompilerParams(vmem_limit_bytes=32 * 1024 * 1024)
ALL_ROOM = pltpu.CompilerParams(vmem_limit_bytes=63 * 1024 * 1024)


def shaped(*shape, dtype=F32):
    return jax.ShapeDtypeStruct(shape, dtype)


def ahead(axis):
    return [(i, i + 1) for i in range(lax.axis_size(axis) - 1)]


def neighbours(value_up, value_down, axis):
    back = [(j, i) for i, j in ahead(axis)]
    return lax.ppermute(value_up, axis, ahead(axis)), lax.ppermute(value_down, axis, back)


def exchange(value, axis):
    return lax.all_to_all(value, axis, split_axis=0, concat_axis=0, tiled=True)


def per_device(u, v, d, marks, warm, cap, film, bath):
    marks = marks.reshape(ROWS // 8)
    tile = pltpu.VMEM((2, ROWS, COLS), F32)
    line = pltpu.VMEM((2, GY * CCOLS), F32)
    packed, up_rows, down_rows = pl.pallas_call(
        pack_kernel,
        out_shape=(shaped(GY, CHUNK, 128), shaped(6, 4, HROW, 128), shaped(6, 4, HROW, 128)),
        in_specs=[MARKS] + [FAR] * 7,
        out_specs=tuple(vmem(3)),
        scratch_shapes=[tile, tile, pltpu.VMEM((2, ROWS, COLS), jnp.int32)]
        + [line] * 4
        + [pltpu.VMEM((8, GY * CCOLS), F32), pltpu.SemaphoreType.DMA((7,))],
        compiler_params=ALL_ROOM,
        name="pack",
    )(marks, u, v, d, warm, cap, film, bath)
    above_rows, below_rows = neighbours(up_rows, down_rows, "gx")
    recv = exchange(packed, "gy")
    up, down = pl.pallas_call(
        rim_kernel,
        out_shape=(shaped(CORNER, 128), shaped(CORNER, 128)),
        in_specs=[MARKS] + vmem(1),
        out_specs=tuple(vmem(2)),
        compiler_params=PARAMS,
        name="rim",
    )(marks, recv)
    above, below = neighbours(up, down, "gx")
    band = pltpu.VMEM((BAND, 8, ECOLS), F32)
    shift, speed, damage, resist, coarse, tops = pl.pallas_call(
        plate_kernel,
        out_shape=(
            shaped(2, ROWS, COLS),
            shaped(2, ROWS, COLS),
            shaped(2, ROWS, COLS, dtype=jnp.bfloat16),
            shaped(HEAT_ROWS, CCOLS),
            shaped(3, HEAT_ROWS, WCOLS),
            shaped(GX, 8, 128),
        ),
        in_specs=[MARKS, ANY, ANY] + vmem(2) + [ANY, ANY] + vmem(2),
        out_specs=(ANY, ANY, ANY) + tuple(vmem(3)),
        scratch_shapes=[
            pltpu.VMEM((6, 5, EROWS, 128), F32),
            pltpu.VMEM((2, EROWS, 128), F32),
            pltpu.VMEM((5, EROWS, 128), F32),
            pltpu.VMEM((6, BAND, 8, ECOLS), F32),
            band,
            band,
            band,
            band,
            pltpu.VMEM((3, 64, WCOLS), F32),
            pltpu.VMEM((80, COLS), F32),
            pltpu.VMEM((2, ROWS, COLS), jnp.bfloat16),
            pltpu.SemaphoreType.DMA((19,)),
        ],
        compiler_params=PARAMS,
        name="plate",
    )(marks, u, v, d, recv, above_rows, below_rows, above, below)
    from_left = lax.ppermute(resist[:, 128:256], "gy", ahead("gy"))
    tops = exchange(tops, "gx")
    answer = pl.pallas_call(
        solve_kernel,
        out_shape=shaped(GY, 16, CCOLS),
        in_specs=vmem(4),
        out_specs=vmem(1)[0],
        compiler_params=PARAMS,
        name="solve",
    )(resist, from_left, coarse, tops)
    answer = exchange(answer, "gy")
    warmth = pl.pallas_call(
        finish_kernel,
        out_shape=shaped(2, GY * CCOLS),
        in_specs=vmem(2),
        out_specs=vmem(1)[0],
        scratch_shapes=[pltpu.VMEM((2, GY * CCOLS + 128), F32), pltpu.VMEM((7, GY, CCOLS), F32)],
        compiler_params=PARAMS,
        name="finish",
    )(answer, warm)
    return shift, speed, damage, warmth


def solution(mesh):
    tile = P(None, "gx", "gy")
    line = P(("gx", "gy"), None)
    return jax.shard_map(
        per_device,
        mesh=mesh,
        in_specs=(tile, tile, tile, P("gx", "gy"), line, line, line, line),
        out_specs=(tile, tile, tile, line),
        check_vma=False,
    )
```

time: 86.8 us -> 71.5 us (0.82)
  blocking collectives: 46 us -> 15.5 us
  starting transfers between devices: 11.9 us -> 29.2 us
  local copies, waits for them, and re-layouts: 6.62 us -> 0.04 us
  Pallas kernels: 12.2 us -> 15.1 us
  waiting for transfers between devices: 8.7 us -> 10.4 us
    all_to_all x3 -> x1, blocking collectives: 46 us -> 15.5 us  [exchange(): return lax.all_to_all(value, axis, split_axis=0, concat_axis=0, tiled=True)]
    all_to_all x0 -> x2, starting transfers between devices: none -> 14.3 us  [exchange(): return lax.all_to_all(value, axis, split_axis=0, concat_axis=0, tiled=True)]
    unnamed x17 -> x14, local copies, waits for them, and re-layouts: 6.61 us -> 0.04 us
    ppermute x2 -> x3, starting transfers between devices: 6.32 us -> 12.3 us  [the longest x2 6.56 us: neighbours(): lax.ppermute(value_up, axis, ahead(axis))]
    all_to_all x0 -> x2, waiting for transfers between devices: none -> 5.89 us  [exchange(): return lax.all_to_all(value, axis, split_axis=0, concat_axis=0, tiled=True)]
    ppermute x2 -> x3, waiting for transfers between devices: 4.85 us -> 0.89 us  [the longest x1 0.89 us: per_device(): from_left = lax.ppermute(resist[:, 128:256], 'gy', ahead('gy'))]
    ppermute x2, starting transfers between devices: 5.56 us -> 2.58 us  [neighbours(): lax.ppermute(value_down, axis, back)]
    pallas_call x4 -> x3, Pallas kernels: 2.53 us -> 4.38 us  [the longest x1 3.21 us: per_device(): pl.pallas_call(pack_kernel, out_shape=(shaped(GY, CHUNK, 128), shaped(6,...]
  transfers between devices with their start and end apart: 4 -> 7, of which waited for: 3 -> 3; matrix products, arithmetic and copies ran while one was open for 0% -> 0% of each run, Pallas kernels for 0% -> 1%
where the time goes in v2:
time: 71.5 us; the launch traced here: 71 us
  starting transfers between devices  29.2 us (41%)
  blocking collectives  15.5 us (22%)
  Pallas kernels  15.1 us (21%)
  waiting for transfers between devices  10.4 us (15%)
  between operations  0.8 us (1%)
    all_to_all x1, blocking collectives, exchange(): return lax.all_to_all(value, axis, split_axis=0, concat_axis=0, tiled=True)  15.5 us
    all_to_all x2, starting transfers between devices, exchange(): return lax.all_to_all(value, axis, split_axis=0, concat_axis=0, tiled=True)  14.3 us
    pallas_call x1, Pallas kernels, per_device(): pl.pallas_call(plate_kernel, out_shape=(shaped(2, ROWS, COLS), shaped(2,...  9.76 us
    ppermute x2, starting transfers between devices, neighbours(): lax.ppermute(value_up, axis, ahead(axis))  6.56 us
    all_to_all x2, waiting for transfers between devices, exchange(): return lax.all_to_all(value, axis, split_axis=0, concat_axis=0, tiled=True)  5.89 us
    ppermute x1, starting transfers between devices, per_device(): from_left = lax.ppermute(resist[:, 128:256], 'gy', ahead('gy'))  5.76 us
    ppermute x2, waiting for transfers between devices, neighbours(): lax.ppermute(value_down, axis, back)  3.59 us
    pallas_call x1, Pallas kernels, per_device(): pl.pallas_call(pack_kernel, out_shape=(shaped(GY, CHUNK, 128), shaped(6,...  3.21 us
  transfers between devices with their start and end apart: 7, of which 3 were waited for; matrix products, arithmetic and copies ran while one was open for 0% of the time, Pallas kernels for 1%

profile of v2, /device:TPU:1, one launch (start us, length us, event | category | flops | bytes accessed | tf_op | source)
XLA Modules:
  0.0 71.0 jit_solution(13700808253452344939)
XLA Ops:
  0.6 3.2 %pack.1 = (f32[16,56,128]{2,1,0:T(8,128)}, f32[6,4,16,128]{3,2,1,0:T(8,128)}, f32[6,4,16,128]{3,2,1,0:T(8,128)}) custom-call(s32[8]{0:T(128)} %bitcast.1, f32[2,64,512]{2,1,0:T(8,128)} %u.1, f32[2,64,512]{2,1,0:T(8,128)} %v.1, s32[2,64,512]{2,1,0:T(8,128)} %d.1, f32[2,4096]{1,0:T(2,128)} %warm.1, f32[2,4096]{1,0:T(2,128)} %cap_hbm.1, f32[2,4096]{1,0:T(2,128)} %film_hbm.1, ...), custom_call_target="tpu_custom_call" | custom-call | tf_op jit(solution)/shard_map/pack/pallas_call | solution.py:510
  3.8 0.0 copy-start.6
  3.9 0.0 copy-start.5
  3.9 0.0 copy-start.4
  3.9 0.0 copy-start.1
  3.9 0.0 copy-start.2
  3.9 9.4 %all-to-all-start = ((f32[16,56,128]{2,1,0:T(8,128)}), f32[16,56,128]{2,1,0:T(8,128)S(1)}, u32[]{:S(2)}, u32[]{:S(2)}) async-start(f32[16,56,128]{2,1,0:T(8,128)} %get-tuple-element.15), calls=%async_computation | async-start | bytes 917504 | tf_op jit(solution)/shard_map/all_to_all | solution.py:503
  13.3 0.0 copy-done.6
  13.4 3.4 %collective-permute-start = (f32[6,4,16,128]{3,2,1,0:T(8,128)S(1)}, f32[6,4,16,128]{3,2,1,0:T(8,128)S(1)}, u32[]{:S(2)}, u32[]{:S(2)}) collective-permute-start(f32[6,4,16,128]{3,2,1,0:T(8,128)S(1)} %copy-done.6), channel_id=1, source_target_pairs={{0,16},{16,32},{32,48},{48,64},{64,80},{80,96},{96,112},{1,17},{17... | collective-permute-start | bytes 589832 | tf_op jit(solution)/shard_map/ppermute | solution.py:499
  16.7 0.0 copy-done.5
  16.7 1.3 %collective-permute-start.1 = (f32[6,4,16,128]{3,2,1,0:T(8,128)S(1)}, f32[6,4,16,128]{3,2,1,0:T(8,128)S(1)}, u32[]{:S(2)}, u32[]{:S(2)}) collective-permute-start(f32[6,4,16,128]{3,2,1,0:T(8,128)S(1)} %copy-done.5), channel_id=1, source_target_pairs={{16,0},{32,16},{48,32},{64,48},{80,64},{96,80},{112,96},{17,1},{33... | collective-permute-start | bytes 589832 | tf_op jit(solution)/shard_map/ppermute | solution.py:499
  18.0 5.9 %all-to-all-done.recv = f32[16,56,128]{2,1,0:T(8,128)S(1)} async-done(((f32[16,56,128]{2,1,0:T(8,128)}), f32[16,56,128]{2,1,0:T(8,128)S(1)}, u32[]{:S(2)}, u32[]{:S(2)}) %all-to-all-start) | async-done | bytes 458784 | tf_op jit(solution)/shard_map/all_to_all | solution.py:503
  23.9 0.0 copy-done.4
  23.9 0.6 rim.1
  24.6 3.2 %collective-permute-start.2 = (f32[112,128]{1,0:T(8,128)S(1)}, f32[112,128]{1,0:T(8,128)S(1)}, u32[]{:S(2)}, u32[]{:S(2)}) collective-permute-start(f32[112,128]{1,0:T(8,128)S(1)} %get-tuple-element.18), channel_id=1, source_target_pairs={{0,16},{16,32},{32,48},{48,64},{64,80},{80,96},{96,112},{1,17},{17... | collective-permute-start | bytes 172040 | tf_op jit(solution)/shard_map/ppermute | solution.py:499
  27.8 1.3 %collective-permute-start.3 = (f32[112,128]{1,0:T(8,128)S(1)}, f32[112,128]{1,0:T(8,128)S(1)}, u32[]{:S(2)}, u32[]{:S(2)}) collective-permute-start(f32[112,128]{1,0:T(8,128)S(1)} %get-tuple-element.19), channel_id=1, source_target_pairs={{16,0},{32,16},{48,32},{64,48},{80,64},{96,80},{112,96},{17,1},{33... | collective-permute-start | bytes 172040 | tf_op jit(solution)/shard_map/ppermute | solution.py:499
  29.1 0.0 collective-permute-done.above_rows
  29.1 0.0 collective-permute-done.1.below_rows
  29.1 0.0 collective-permute-done.2.above
  29.1 3.6 %collective-permute-done.3.below = f32[112,128]{1,0:T(8,128)S(1)} collective-permute-done((f32[112,128]{1,0:T(8,128)S(1)}, f32[112,128]{1,0:T(8,128)S(1)}, u32[]{:S(2)}, u32[]{:S(2)}) %collective-permute-start.3) | collective-permute-done | bytes 57376 | tf_op jit(solution)/shard_map/ppermute | solution.py:499
  32.7 0.0 copy-done.1
  32.7 0.0 copy-done.2
  32.7 0.0 copy-done
  32.7 9.8 %plate.1 = (f32[2,64,512]{2,1,0:T(8,128)}, f32[2,64,512]{2,1,0:T(8,128)}, bf16[2,64,512]{2,1,0:T(8,128)(2,1)}, f32[40,256]{1,0:T(8,128)S(1)}, f32[3,40,384]{2,1,0:T(8,128)S(1)}, /*index=5*/f32[8,8,128]{2,1,0:T(8,128)}) custom-call(s32[8]{0:T(128)S(1)} %bitcast.3, f32[2,64,512]{2,1,0:T(8,128)S(1)} %copy-done, f32[2,64,512]{2,1,0:T(8,128)S(1)} %copy-done.1, ...), custom_call_target="tpu_custom_call" | custom-call | tf_op jit(solution)/shard_map/plate/pallas_call | solution.py:533
  42.5 4.8 %all-to-all-start.1 = ((f32[8,8,128]{2,1,0:T(8,128)}), f32[8,8,128]{2,1,0:T(8,128)S(1)}, u32[]{:S(2)}, u32[]{:S(2)}) async-start(f32[8,8,128]{2,1,0:T(8,128)} %get-tuple-element.25), calls=%async_computation.1 | async-start | bytes 65536 | tf_op jit(solution)/shard_map/all_to_all | solution.py:503
  47.3 5.8 %collective-permute-start.4 = (f32[40,128]{1,0:T(8,128)S(1)}, f32[40,128]{1,0:T(8,128)S(1)}, u32[]{:S(2)}, u32[]{:S(2)}) collective-permute-start(f32[40,128]{1,0:T(8,128)S(1)} %slice.3), channel_id=1, source_target_pairs={{0,1},{1,2},{2,3},{3,4},{4,5},{5,6},{6,7},{7,8},{8,9},{9,10},{10,1... | collective-permute-start | bytes 61448 | tf_op jit(solution)/shard_map/ppermute | solution.py:562
  53.1 0.9 %collective-permute-done.4.from_left = f32[40,128]{1,0:T(8,128)S(1)} collective-permute-done((f32[40,128]{1,0:T(8,128)S(1)}, f32[40,128]{1,0:T(8,128)S(1)}, u32[]{:S(2)}, u32[]{:S(2)}) %collective-permute-start.4) | collective-permute-done | bytes 20512 | tf_op jit(solution)/shard_map/ppermute | solution.py:562
  54.0 0.0 all-to-all-done.1.tops
  54.0 0.6 solve.1
  54.5 0.0 copy-start.3
  54.5 15.5 %all_to_all.15.recv = f32[16,16,256]{2,1,0:T(8,128)S(1)} all-to-all(f32[16,16,256]{2,1,0:T(8,128)S(1)} %solve.1), channel_id=1, replica_groups=mesh['gx'=8,'gy'=16] {'gy'}, dimensions={0} | all-to-all | bytes 524288 | tf_op jit(solution)/shard_map/all_to_all | solution.py:503
  70.0 1.0 %finish.1 = f32[2,4096]{1,0:T(2,128)} custom-call(f32[16,16,256]{2,1,0:T(8,128)S(1)} %all_to_all.15.recv, f32[2,4096]{1,0:T(2,128)S(1)} %copy-done.3), custom_call_target="tpu_custom_call" | custom-call | tf_op jit(solution)/shard_map/finish/pallas_call | solution.py:573
  (3 shorter events, 0.0 us)
Async XLA Ops:
  3.8 9.5 %copy-start.6 = (f32[6,4,16,128]{3,2,1,0:T(8,128)S(1)}, f32[6,4,16,128]{3,2,1,0:T(8,128)}, u32[]{:S(2)}) copy-start(f32[6,4,16,128]{3,2,1,0:T(8,128)} %get-tuple-element.16) | copy-start | bytes 589828
  3.9 12.9 %copy-start.5 = (f32[6,4,16,128]{3,2,1,0:T(8,128)S(1)}, f32[6,4,16,128]{3,2,1,0:T(8,128)}, u32[]{:S(2)}) copy-start(f32[6,4,16,128]{3,2,1,0:T(8,128)} %get-tuple-element.17) | copy-start | bytes 589828
  3.9 20.1 %copy-start.4 = (s32[8,1]{0,1:T(1,128)S(1)}, s32[8,1]{0,1:T(1,128)}, u32[]{:S(2)}) copy-start(s32[8,1]{0,1:T(1,128)} %param.11) | copy-start | bytes 100
  3.9 28.8 %copy-start.1 = (f32[2,64,512]{2,1,0:T(8,128)S(1)}, f32[2,64,512]{2,1,0:T(8,128)}, u32[]{:S(2)}) copy-start(f32[2,64,512]{2,1,0:T(8,128)} %v.1) | copy-start | bytes 786436
  3.9 28.8 %copy-start.2 = (s32[2,64,512]{2,1,0:T(8,128)S(1)}, s32[2,64,512]{2,1,0:T(8,128)}, u32[]{:S(2)}) copy-start(s32[2,64,512]{2,1,0:T(8,128)} %d.1) | copy-start | bytes 786436
  3.9 20.0 %all-to-all-start = ((f32[16,56,128]{2,1,0:T(8,128)}), f32[16,56,128]{2,1,0:T(8,128)S(1)}, u32[]{:S(2)}, u32[]{:S(2)}) async-start(f32[16,56,128]{2,1,0:T(8,128)} %get-tuple-element.15), calls=%async_computation | async-start | bytes 917504 | tf_op jit(solution)/shard_map/all_to_all | solution.py:503
  13.3 19.4 %copy-start = (f32[2,64,512]{2,1,0:T(8,128)S(1)}, f32[2,64,512]{2,1,0:T(8,128)}, u32[]{:S(2)}) copy-start(f32[2,64,512]{2,1,0:T(8,128)} %u.1) | copy-start | bytes 786436
  13.4 15.7 %collective-permute-start = (f32[6,4,16,128]{3,2,1,0:T(8,128)S(1)}, f32[6,4,16,128]{3,2,1,0:T(8,128)S(1)}, u32[]{:S(2)}, u32[]{:S(2)}) collective-permute-start(f32[6,4,16,128]{3,2,1,0:T(8,128)S(1)} %copy-done.6), channel_id=1, source_target_pairs={{0,16},{16,32},{32,48},{48,64},{64,80},{80,96},{96,112},{1,17},{17... | collective-permute-start | bytes 589832 | tf_op jit(solution)/shard_map/ppermute | solution.py:499
  16.7 12.3 %collective-permute-start.1 = (f32[6,4,16,128]{3,2,1,0:T(8,128)S(1)}, f32[6,4,16,128]{3,2,1,0:T(8,128)S(1)}, u32[]{:S(2)}, u32[]{:S(2)}) collective-permute-start(f32[6,4,16,128]{3,2,1,0:T(8,128)S(1)} %copy-done.5), channel_id=1, source_target_pairs={{16,0},{32,16},{48,32},{64,48},{80,64},{96,80},{112,96},{17,1},{33... | collective-permute-start | bytes 589832 | tf_op jit(solution)/shard_map/ppermute | solution.py:499
  24.6 4.5 %collective-permute-start.2 = (f32[112,128]{1,0:T(8,128)S(1)}, f32[112,128]{1,0:T(8,128)S(1)}, u32[]{:S(2)}, u32[]{:S(2)}) collective-permute-start(f32[112,128]{1,0:T(8,128)S(1)} %get-tuple-element.18), channel_id=1, source_target_pairs={{0,16},{16,32},{32,48},{48,64},{64,80},{80,96},{96,112},{1,17},{17... | collective-permute-start | bytes 172040 | tf_op jit(solution)/shard_map/ppermute | solution.py:499
  27.8 4.9 %collective-permute-start.3 = (f32[112,128]{1,0:T(8,128)S(1)}, f32[112,128]{1,0:T(8,128)S(1)}, u32[]{:S(2)}, u32[]{:S(2)}) collective-permute-start(f32[112,128]{1,0:T(8,128)S(1)} %get-tuple-element.19), channel_id=1, source_target_pairs={{16,0},{32,16},{48,32},{64,48},{80,64},{96,80},{112,96},{17,1},{33... | collective-permute-start | bytes 172040 | tf_op jit(solution)/shard_map/ppermute | solution.py:499
  42.5 11.5 %all-to-all-start.1 = ((f32[8,8,128]{2,1,0:T(8,128)}), f32[8,8,128]{2,1,0:T(8,128)S(1)}, u32[]{:S(2)}, u32[]{:S(2)}) async-start(f32[8,8,128]{2,1,0:T(8,128)} %get-tuple-element.25), calls=%async_computation.1 | async-start | bytes 65536 | tf_op jit(solution)/shard_map/all_to_all | solution.py:503
  47.3 6.7 %collective-permute-start.4 = (f32[40,128]{1,0:T(8,128)S(1)}, f32[40,128]{1,0:T(8,128)S(1)}, u32[]{:S(2)}, u32[]{:S(2)}) collective-permute-start(f32[40,128]{1,0:T(8,128)S(1)} %slice.3), channel_id=1, source_target_pairs={{0,1},{1,2},{2,3},{3,4},{4,5},{5,6},{6,7},{7,8},{8,9},{9,10},{10,1... | collective-permute-start | bytes 61448 | tf_op jit(solution)/shard_map/ppermute | solution.py:562
  54.5 15.5 %copy-start.3 = (f32[2,4096]{1,0:T(2,128)S(1)}, f32[2,4096]{1,0:T(2,128)}, u32[]{:S(2)}) copy-start(f32[2,4096]{1,0:T(2,128)} %warm.1) | copy-start | bytes 98308

commit v3 on v2

--- a/solution.py
+++ b/solution.py
@@ -41,17 +41,12 @@
     return value if shift == 0 else pltpu.roll(value, shift, axis)
 
 
-def mark_rows(marks, first, count, width):
+def mark_rows(weights, first, count):
     parts = [
-        jnp.full((8, width), marks[first // 8 + k].astype(F32), F32) for k in range(count // 8)
+        jnp.broadcast_to(weights[first // 8 + k : first // 8 + k + 1, :], (8, 128))
+        for k in range(count // 8)
     ]
     return jnp.concatenate(parts, axis=0)
-
-
-def own_spring(d, marks, f, row0, count, first_lane, width):
-    weight = mark_rows(marks, row0, count, width)
-    level = d[f, pl.ds(row0, count), pl.ds(first_lane, width)].astype(F32)
-    return 1.0 - level * (0.125 * weight)
 
 
 def start_all(copies):
@@ -65,30 +60,24 @@
 
 
 def pack_kernel(
-    marks, u_hbm, v_hbm, d_hbm, warm_hbm, cap_hbm, film_hbm, bath_hbm,
-    out, up, down,
-    u, v, d, warm, cap, film, bath, lines, sem,
+    marks_hbm, u_hbm, v_hbm, d_hbm, warm_hbm, cap_hbm, film_hbm, bath_hbm,
+    out, weights,
+    marks, u, v, d, warm, cap, film, bath, lines, sem,
 ):
-    pairs = (
-        (warm_hbm, warm), (cap_hbm, cap), (film_hbm, film), (bath_hbm, bath),
-        (u_hbm, u), (v_hbm, v), (d_hbm, d),
-    )
+    pairs = [(marks_hbm, marks)]
+    pairs += [(warm_hbm, warm), (cap_hbm, cap), (film_hbm, film), (bath_hbm, bath)]
+    for far, near in ((u_hbm, u), (v_hbm, v), (d_hbm, d)):
+        for side, at in ((0, 0), (1, COLS - 128)):
+            pairs.append((far.at[:, :, pl.ds(at, 128)], near.at[side]))
     copies = [pltpu.make_async_copy(a, b, sem.at[k]) for k, (a, b) in enumerate(pairs)]
     start_all(copies)
     gy = lax.axis_index("gy")
     zero = jnp.zeros((32, 128), F32)
     for g in range(GY):
         out[g, 24:CHUNK, :] = zero
-    wait_all(copies)
-    for message, row0 in ((up, ROWS - HROW), (down, 0)):
-        rows = pl.ds(row0, HROW)
-        for f in range(2):
-            for k in range(4):
-                cols = pl.ds(128 * k, 128)
-                message[f, k] = u[f, rows, cols]
-                message[2 + f, k] = v[f, rows, cols]
-                message[4 + f, k] = own_spring(d, marks, f, row0, HROW, 128 * k, 128)
-
+    wait_all(copies[:5])
+    for k in range(ROWS // 8):
+        weights[k : k + 1, :] = jnp.full((1, 128), marks[k].astype(F32), F32)
     lines[0:2, :] = warm[...]
     lines[2:4, :] = cap[...] + film[...]
     lines[4:6, :] = film[...] * (bath[...] - warm[...])
@@ -107,31 +96,52 @@
         else:
             right = jnp.broadcast_to(lines[:, GY * CCOLS - 1 : GY * CCOLS], (8, 128))
         out[g, 16:24, :] = jnp.where(lane < 64, right, left)
-
-    def edge(first_lane, inner):
+    wait_all(copies[5:])
+
+    def edge(side, inner):
         wide = lanes((ROWS, 128))
-        window = (slice(None), pl.ds(first_lane, 128))
+        weight = mark_rows(weights, 0, ROWS)
+        tiles = [u[side, 0], u[side, 1], v[side, 0], v[side, 1]]
+        tiles += [1.0 - d[side, f].astype(F32) * (0.125 * weight) for f in range(2)]
         packed = jnp.zeros((ROWS, 128), F32)
-        for f in range(7):
-            if f < 2:
-                tile = u[(f, *window)]
-            elif f < 4:
-                tile = v[(f - 2, *window)]
-            elif f < 6:
-                tile = own_spring(d, marks, f - 4, 0, ROWS, first_lane, 128)
-            else:
-                tile = mark_rows(marks, 0, ROWS, 128)
+        for f, tile in enumerate(tiles + [weight]):
             moved = turn(tile, 8 * f - inner, 1)
             packed = jnp.where((wide >= 8 * f) & (wide < 8 * f + 8), moved, packed)
         return packed[:32] + turn(packed[32:], 64, 1)
 
     @pl.when(gy < GY - 1)
     def _():
-        out[gy + 1, 24:CHUNK, :] = edge(COLS - 128, 120)
+        out[gy + 1, 24:CHUNK, :] = edge(1, 120)
 
     @pl.when(gy > 0)
     def _():
         out[gy - 1, 24:CHUNK, :] = edge(0, 0)
+
+
+def rows_kernel(weights, u_hbm, v_hbm, d_hbm, up, down, d, sem):
+    copies, levels = [], []
+    for m, (message, row0) in enumerate(((up, ROWS - HROW), (down, 0))):
+        rows = pl.ds(row0, HROW)
+        for k in range(4):
+            cols = pl.ds(128 * k, 128)
+            for f, far in enumerate((u_hbm, v_hbm)):
+                copies.append(
+                    pltpu.make_async_copy(
+                        far.at[:, rows, cols],
+                        message.at[2 * f : 2 * f + 2, k],
+                        sem.at[8 * m + 2 * k + f],
+                    )
+                )
+        levels.append(pltpu.make_async_copy(d_hbm.at[:, rows, :], d.at[m], sem.at[16 + m]))
+    start_all(levels + copies)
+    wait_all(levels)
+    for m, (message, row0) in enumerate(((up, ROWS - HROW), (down, 0))):
+        weight = 0.125 * mark_rows(weights, row0, HROW)
+        for f in range(2):
+            for k in range(4):
+                level = d[m, f, :, pl.ds(128 * k, 128)].astype(F32)
+                message[4 + f, k] = 1.0 - level * weight
+    wait_all(copies)
 
 
 def join_sides(f, left, left_at, right, right_at):
@@ -148,7 +158,7 @@
     return left, right
 
 
-def rim_kernel(marks, recv, up, down):
+def rim_kernel(weights, recv, up, down):
     left, right = sides(recv)
     lane = lanes((HROW, 128))
     for out, row0, coarse0, thin0 in ((up, ROWS - HROW, 16, 24), (down, 0, 0, 0)):
@@ -158,7 +168,7 @@
             near, off = turn(left[16:32], 64, 1), right[16:32]
         corner = jnp.where(lane < 56, near, off)
         out[0:16, :] = jnp.where(
-            (lane >= 56) & (lane < 64), mark_rows(marks, row0, HROW, 128), corner
+            (lane >= 56) & (lane < 64), mark_rows(weights, row0, HROW), corner
         )
         for k in range(3):
             for r in range(0, 16, 2):
@@ -172,9 +182,74 @@
                     ]
 
 
+def strip_of(t):
+    return pl.ds(t, 8, stride=BAND)
+
+
+def prep_kernel(
+    weights, u, v, d, recv, above_rows, below_rows,
+    state, side, coarse, table,
+    field, sem,
+):
+    gx = lax.axis_index("gx")
+    gy = lax.axis_index("gy")
+    top = pl.ds(0, HROW)
+    mid = pl.ds(HROW, ROWS)
+    low = pl.ds(HROW + ROWS, HROW)
+    copies = [
+        pltpu.make_async_copy(above_rows, field.at[:, :, top], sem.at[0]),
+        pltpu.make_async_copy(below_rows, field.at[:, :, low], sem.at[1]),
+    ]
+    for k in range(4):
+        cols = pl.ds(128 * k, 128)
+        for f, source in enumerate((u, v)):
+            here = field.at[2 * f : 2 * f + 2, k, mid]
+            copies.append(pltpu.make_async_copy(source.at[:, :, cols], here, sem.at[2 + 2 * k + f]))
+    start_all(copies)
+    left, right = sides(recv)
+    for k in range(3):
+        cols = pl.ds(128 * k, 128)
+        for g in range(GY):
+            for a in range(3):
+                coarse[a, 2 * g : 2 * g + 2, cols] = recv[g, 8 * k + 2 * a : 8 * k + 2 * a + 2, :]
+    p = sublanes((256, 128))
+    q = lanes((256, 128))
+    place = (p % SEG).astype(F32)
+    even = (2 * (q % 64)).astype(F32)
+    spread = jnp.exp(jnp.abs(place - even) * (-4.0 / SEG)) + jnp.exp(
+        jnp.abs(place - even - 1.0) * (-4.0 / SEG)
+    )
+    table[...] = jnp.where(p // SEG == q // 64, spread * (0.5 * 2.0 / SEG), 0.0)
+    for f in range(7):
+        for half in (0, 32):
+            side[f, pl.ds(half, 32), :] = join_sides(
+                f, left, half * 2, right, half * 2
+            )
+    weight = 0.125 * mark_rows(weights, 0, ROWS)
+    for f in range(2):
+        for k in range(4):
+            level = d[f, :, pl.ds(128 * k, 128)].astype(F32)
+            field[4 + f, k, mid, :] = 1.0 - level * weight
+    wait_all(copies)
+    lane = lanes((8, 128))
+    first = gx * ROWS - HROW + BAND * sublanes((8, 128))
+    for t in range(BAND):
+        row = first + t
+        inner_row = (row >= 1) & (row < GX * ROWS)
+        for k in range(4):
+            cols = pl.ds(128 * k, 128)
+            for f in range(4):
+                state[f, t, :, cols] = field[f, k, strip_of(t), :]
+            state[4, t, :, cols] = jnp.where(inner_row, field[4, k, strip_of(t), :], 0.0)
+            spring = field[5, k, strip_of(t), :]
+            if k == 0:
+                spring = jnp.where(gy * COLS + lane >= 1, spring, 0.0)
+            state[5, t, :, cols] = spring
+
+
 def plate_kernel(
-    marks, u, v, d, recv, above_rows, below_rows, above, below,
-    shift_out, speed_out, damage_out, resist_out, coarse_out, tops_out,
+    weights, state_in, side, coarse_in, table, above, below,
+    shift_out, speed_out, damage_out, resist_out, coarse_out, edge_out,
     field, cw, temp, state, rate, warmth, tx, ty, coarse, gap, worn, sem,
 ):
     gx = lax.axis_index("gx")
@@ -182,21 +257,22 @@
     top = pl.ds(0, HROW)
     mid = pl.ds(HROW, ROWS)
     low = pl.ds(HROW + ROWS, HROW)
-    copies = [
-        pltpu.make_async_copy(above_rows, field.at[:, 0:4, top], sem.at[0]),
-        pltpu.make_async_copy(below_rows, field.at[:, 0:4, low], sem.at[1]),
-    ]
+    main = pl.ds(0, COLS)
+    fetch = pltpu.make_async_copy(
+        state_in.at[:, :, :, main], state.at[:, :, :, main], sem.at[9]
+    )
+    fetch.start()
     results = []
     for k in range(4):
         cols = pl.ds(128 * k, 128)
-        for f, (source, target) in enumerate(((u, shift_out), (v, speed_out))):
+        for f, target in enumerate((shift_out, speed_out)):
             here = field.at[2 * f : 2 * f + 2, k, mid]
-            at = 2 + 2 * k + f
-            copies.append(pltpu.make_async_copy(source.at[:, :, cols], here, sem.at[at]))
-            results.append(pltpu.make_async_copy(here, target.at[:, :, cols], sem.at[8 + at]))
-    results.append(pltpu.make_async_copy(worn, damage_out, sem.at[18]))
-    start_all(copies)
-
+            results.append(
+                pltpu.make_async_copy(here, target.at[:, :, cols], sem.at[2 * k + f])
+            )
+    results.append(pltpu.make_async_copy(worn, damage_out, sem.at[8]))
+
+    coarse[:, 16:48, :] = coarse_in[...]
     for k in range(3):
         cols = pl.ds(128 * k, 128)
         coarse[0, 0:16, cols] = above[16 + 16 * k : 32 + 16 * k, :]
@@ -204,9 +280,6 @@
         for a, base in ((1, 64), (2, 88)):
             coarse[a, 8:16, cols] = above[base + 8 * k : base + 8 * k + 8, :]
             coarse[a, 48:56, cols] = below[base + 8 * k : base + 8 * k + 8, :]
-        for g in range(GY):
-            for a in range(3):
-                coarse[a, 16 + 2 * g : 18 + 2 * g, cols] = recv[g, 8 * k + 2 * a : 8 * k + 2 * a + 2, :]
 
     @pl.when(gx == 0)
     def _():
@@ -240,56 +313,45 @@
     tiles = [columns(k) for k in range(4)]
     tiles.append(jnp.where(lane64 < 64, columns(4), columns(-1)))
     for k in range(5):
-        temp[k] = jnp.dot(
-            raise_, tiles[k], precision=HI, preferred_element_type=F32
-        )
-
-    left, right = sides(recv)
+        temp[k] = jnp.dot(raise_, tiles[k], precision=HI, preferred_element_type=F32)
+
+    factor = -4.0 * LOG2E
+    for rows, source in ((top, above), (low, below)):
+        tile = source[0:16, :]
+        for f in range(6):
+            field[f, 4, rows, :] = join_sides(f, tile, 0, tile, 64)
+        cw[1, rows, :] = factor * join_sides(6, tile, 0, tile, 64)
+        cw[0, rows, :] = jnp.broadcast_to(factor * tile[:, 60:61], (HROW, 128))
     for f in range(6):
-        for rows, source in ((top, above), (low, below)):
-            tile = source[0:16, :]
-            field[f, 4, rows, :] = join_sides(f, tile, 0, tile, 64)
-        for half in (0, 32):
-            field[f, 4, pl.ds(HROW + half, 32), :] = join_sides(f, left, half * 2, right, half * 2)
-    factor = -4.0 * LOG2E
-    for base, source in ((0, above), (HROW + ROWS, below)):
-        tile = factor * source[0:16, :]
-        cw[1, pl.ds(base, HROW), :] = join_sides(6, tile, 0, tile, 64)
-        cw[0, pl.ds(base, HROW), :] = jnp.broadcast_to(tile[:, 60:61], (HROW, 128))
-    cw[0, mid, :] = factor * mark_rows(marks, 0, ROWS, 128)
-    for half in (0, 32):
-        cw[1, pl.ds(HROW + half, 32), :] = factor * join_sides(6, left, half * 2, right, half * 2)
-    for f in range(2):
-        for k in range(4):
-            field[4 + f, k, mid, :] = own_spring(d, marks, f, 0, ROWS, 128 * k, 128)
-    wait_all(copies)
+        field[f, 4, mid, :] = side[f]
+    cw[1, mid, :] = factor * side[6]
+    cw[0, mid, :] = factor * mark_rows(weights, 0, ROWS)
 
     lane = lanes((8, 128))
     first = gx * ROWS - HROW + BAND * sublanes((8, 128))
+    rest = pl.ds(COLS, 128)
+    col = gy * COLS + jnp.where(lane < 64, lane + COLS, lane - 128)
+    inner_col = (col >= 1) & (col < GY * COLS)
     for t in range(BAND):
-        strip = pl.ds(t, 8, stride=BAND)
         row = first + t
         inner_row = (row >= 1) & (row < GX * ROWS)
-        own_rate = cw[0, strip, :]
-        side_rate = cw[1, strip, :]
+        own_rate = cw[0, strip_of(t), :]
+        for k in range(4):
+            rate[t, :, pl.ds(128 * k, 128)] = own_rate
+        rate[t, :, rest] = cw[1, strip_of(t), :]
         for k in range(5):
-            cols = pl.ds(128 * k, 128)
-            rate[t, :, cols] = own_rate if k < 4 else side_rate
-            warmth[t, :, cols] = (0.5 * EXPANSION) * temp[k, strip, :]
-            for f in range(4):
-                state[f, t, :, cols] = field[f, k, strip, :]
-            state[4, t, :, cols] = jnp.where(inner_row, field[4, k, strip, :], 0.0)
-            spring = field[5, k, strip, :]
-            if k in (0, 4):
-                col = gy * COLS + (lane if k == 0 else jnp.where(lane < 64, lane + COLS, lane - 128))
-                spring = jnp.where((col >= 1) & (col < GY * COLS), spring, 0.0)
-            state[5, t, :, cols] = spring
+            warmth[t, :, pl.ds(128 * k, 128)] = (0.5 * EXPANSION) * temp[k, strip_of(t), :]
+        for f in range(4):
+            state[f, t, :, rest] = field[f, 4, strip_of(t), :]
+        state[4, t, :, rest] = jnp.where(inner_row, field[4, 4, strip_of(t), :], 0.0)
+        state[5, t, :, rest] = jnp.where(inner_col, field[5, 4, strip_of(t), :], 0.0)
     before = turn(warmth[BAND - 1], 1, 0)
     for t in range(BAND):
         own = warmth[t]
         tx[t] = own + before
         ty[t] = own + turn(own, 1, 1)
         before = own
+    fetch.wait()
 
     keep = 1.0 - TIME_STEP * DAMPING
 
@@ -350,29 +412,27 @@
                 worn[0, pl.ds(8 * b - 8, 8), cols] = dx.astype(jnp.bfloat16)
                 worn[1, pl.ds(8 * b - 8, 8), cols] = dy.astype(jnp.bfloat16)
     start_all(results[-1:])
-    p = sublanes((256, 128))
-    q = lanes((256, 128))
-    place = (p % SEG).astype(F32)
-    even = (2 * (q % 64)).astype(F32)
-    table = jnp.exp(jnp.abs(place - even) * (-4.0 / SEG)) + jnp.exp(
-        jnp.abs(place - even - 1.0) * (-4.0 / SEG)
-    )
-    table = jnp.where(p // SEG == q // 64, table * (0.5 * 2.0 / SEG), 0.0)
     a = sublanes((HEAT_ROWS, 2 * HEAT_ROWS))
     c = lanes((HEAT_ROWS, 2 * HEAT_ROWS))
     pool = jnp.where(c // 2 == a, 1.0, 0.0)
     for k in range(2):
         pair = jnp.dot(pool, gap[:, pl.ds(256 * k, 256)], precision=HI, preferred_element_type=F32)
         resist_out[:, pl.ds(128 * k, 128)] = jnp.dot(
-            pair, table, precision=HI, preferred_element_type=F32
+            pair, table[...], precision=HI, preferred_element_type=F32
         )
-    conduct = (1.0 + 0.5 * coarse[0, 12 : 12 + HEAT_ROWS, 0:CCOLS]) / (1.0 + resist_out[...])
+    edge_out[...] = resist_out[:, 128:256]
+    wait_all(results)
+
+
+def border_kernel(resist, coarse, out):
+    gx = lax.axis_index("gx")
+    conduct = (1.0 + 0.5 * coarse[0, :, 0:CCOLS]) / (1.0 + resist[...])
     shape = (HEAT_ROWS, CCOLS)
     row = gx * CROWS - 4 + sublanes(shape)
     down = jnp.where((row >= 1) & (row < GX * CROWS), 0.5 * (conduct + turn(conduct, 1, 0)), 0.0)
     side = jnp.where(lanes(shape) >= 1, 0.5 * (conduct + turn(conduct, 1, 1)), 0.0)
     offsum = (down + turn(down, -1, 0) + side + turn(side, -1, 1))[4 : 4 + CROWS]
-    capacity = coarse[1, 16:48, 0:CCOLS]
+    capacity = coarse[1, 4 : 4 + CROWS, 0:CCOLS]
     top = jnp.max(offsum / (capacity + offsum), axis=(0, 1), keepdims=True)
     a = sublanes((8, CCOLS))
     c = lanes((8, CCOLS))
@@ -389,8 +449,7 @@
             preferred_element_type=F32,
         )
     for g in range(GX):
-        tops_out[g] = border
-    wait_all(results)
+        out[g] = border
 
 
 def conductances(resist, from_left, coarse):
@@ -443,20 +502,23 @@
         for k in range(1, 4):
             tile = jnp.where(group == k, tops[4 * h + k], tile)
         strip.append(tile)
+    last_y, last_y2 = y[:, CCOLS:], turn(y2[:, CCOLS:], 64, 1)
+    tail = jnp.where(lanes(last_y.shape) < 64, last_y, last_y2)
     for g in range(GY):
         rows = slice(4 + 2 * g, 6 + 2 * g)
-        out[g, 0:2, :] = y[rows, 0:CCOLS]
-        out[g, 2:4, :] = y2[rows, 0:CCOLS]
-        out[g, 4:6, 0:128] = y[rows, CCOLS:]
-        out[g, 4:6, 128:256] = y2[rows, CCOLS:]
-        out[g, 8:16, 0:128] = strip[0]
-        out[g, 8:16, 128:256] = strip[1]
+        for h in range(2):
+            cols = slice(128 * h, 128 * h + 128)
+            out[g, 2 * h : 2 * h + 2, :] = y[rows, cols]
+            out[g, 4 + 2 * h : 6 + 2 * h, :] = y2[rows, cols]
+            out[g, 8 + 8 * h : 16 + 8 * h, :] = strip[h]
+            out[g, 15 + 8 * h : 16 + 8 * h, :] = tail[4 + 2 * g + h : 5 + 2 * g + h]
 
 
 def finish_kernel(recv, warm, out, wide, border):
     for g in range(GY):
         for k in range(7):
-            border[k, g : g + 1, :] = recv[g, 8 + k : 9 + k, :]
+            for h in range(2):
+                border[k, g : g + 1, pl.ds(128 * h, 128)] = recv[g, 8 + 8 * h + k : 9 + 8 * h + k, :]
     across = 0.5 * (turn(border[5], 1, 0) + border[4])
     across = jnp.where(sublanes((GY, CCOLS)) >= 1, across, 0.0)
     top = border[6]
@@ -468,10 +530,13 @@
     gain = 8.0 / (8.0 - 8.0 * square + square * square)
     near = gain * (1.0 - square)
     for g in range(GY):
-        wide[:, pl.ds(CCOLS * g, CCOLS)] = near * recv[g, 0:2, :] + gain * recv[g, 2:4, :]
-    wide[:, pl.ds(CCOLS * GY, 128)] = (
-        near * recv[GY - 1, 4:6, 0:128] + gain * recv[GY - 1, 4:6, 128:256]
-    )
+        for h in range(2):
+            wide[:, pl.ds(CCOLS * g + 128 * h, 128)] = (
+                near * recv[g, 2 * h : 2 * h + 2, :] + gain * recv[g, 4 + 2 * h : 6 + 2 * h, :]
+            )
+    for h in range(2):
+        tail = recv[GY - 1, 15 + 8 * h : 16 + 8 * h, :]
+        wide[h : h + 1, pl.ds(CCOLS * GY, 128)] = near * tail + gain * turn(tail, 64, 1)
     out[...] = warm[...] + turn(wide[...], -4, 1)[:, : GY * CCOLS]
 
 
@@ -479,11 +544,9 @@
     return [pl.BlockSpec(memory_space=pltpu.VMEM)] * count
 
 
-MARKS = pl.BlockSpec(memory_space=pltpu.SMEM)
 ANY = pl.BlockSpec(memory_space=pl.ANY)
 FAR = pl.BlockSpec(memory_space=pltpu.MemorySpace.HBM)
 PARAMS = pltpu.CompilerParams(vmem_limit_bytes=32 * 1024 * 1024)
-ALL_ROOM = pltpu.CompilerParams(vmem_limit_bytes=63 * 1024 * 1024)
 
 
 def shaped(*shape, dtype=F32):
@@ -491,7 +554,8 @@
 
 
 def ahead(axis):
-    return [(i, i + 1) for i in range(lax.axis_size(axis) - 1)]
+    count = lax.axis_size(axis)
+    return [(i, (i + 1) % count) for i in range(count)]
 
 
 def neighbours(value_up, value_down, axis):
@@ -504,33 +568,66 @@
 
 
 def per_device(u, v, d, marks, warm, cap, film, bath):
-    marks = marks.reshape(ROWS // 8)
-    tile = pltpu.VMEM((2, ROWS, COLS), F32)
+    far = [
+        pltpu.with_memory_space_constraint(x, pltpu.MemorySpace.HBM)
+        for x in (marks.reshape(ROWS // 8), u, v, d, warm, cap, film, bath)
+    ]
+    side = pltpu.VMEM((2, 2, ROWS, 128), F32)
     line = pltpu.VMEM((2, GY * CCOLS), F32)
-    packed, up_rows, down_rows = pl.pallas_call(
+    packed, weights = pl.pallas_call(
         pack_kernel,
-        out_shape=(shaped(GY, CHUNK, 128), shaped(6, 4, HROW, 128), shaped(6, 4, HROW, 128)),
-        in_specs=[MARKS] + [FAR] * 7,
-        out_specs=tuple(vmem(3)),
-        scratch_shapes=[tile, tile, pltpu.VMEM((2, ROWS, COLS), jnp.int32)]
+        out_shape=(shaped(GY, CHUNK, 128), shaped(8, 128)),
+        in_specs=[FAR] * 8,
+        out_specs=tuple(vmem(2)),
+        scratch_shapes=[pltpu.SMEM((ROWS // 8,), jnp.int32)]
+        + [side, side, pltpu.VMEM((2, 2, ROWS, 128), jnp.int32)]
         + [line] * 4
-        + [pltpu.VMEM((8, GY * CCOLS), F32), pltpu.SemaphoreType.DMA((7,))],
-        compiler_params=ALL_ROOM,
+        + [pltpu.VMEM((8, GY * CCOLS), F32), pltpu.SemaphoreType.DMA((11,))],
+        compiler_params=PARAMS,
         name="pack",
-    )(marks, u, v, d, warm, cap, film, bath)
+    )(*far)
+    recv = exchange(packed, "gy")
+    up_rows, down_rows = pl.pallas_call(
+        rows_kernel,
+        out_shape=(shaped(6, 4, HROW, 128), shaped(6, 4, HROW, 128)),
+        in_specs=vmem(1) + [FAR] * 3,
+        out_specs=tuple(vmem(2)),
+        scratch_shapes=[
+            pltpu.VMEM((2, 2, HROW, COLS), jnp.int32),
+            pltpu.SemaphoreType.DMA((18,)),
+        ],
+        compiler_params=PARAMS,
+        name="rows",
+    )(weights, *far[1:4])
     above_rows, below_rows = neighbours(up_rows, down_rows, "gx")
-    recv = exchange(packed, "gy")
     up, down = pl.pallas_call(
         rim_kernel,
         out_shape=(shaped(CORNER, 128), shaped(CORNER, 128)),
-        in_specs=[MARKS] + vmem(1),
+        in_specs=vmem(2),
         out_specs=tuple(vmem(2)),
         compiler_params=PARAMS,
         name="rim",
-    )(marks, recv)
+    )(weights, recv)
     above, below = neighbours(up, down, "gx")
+    state, side, coarse, table = pl.pallas_call(
+        prep_kernel,
+        out_shape=(
+            shaped(6, BAND, 8, ECOLS),
+            shaped(7, ROWS, 128),
+            shaped(3, CROWS, WCOLS),
+            shaped(256, 128),
+        ),
+        in_specs=vmem(1) + [ANY, ANY] + vmem(2) + [ANY, ANY],
+        out_specs=tuple(vmem(4)),
+        scratch_shapes=[
+            pltpu.VMEM((6, 4, EROWS, 128), F32),
+            pltpu.SemaphoreType.DMA((10,)),
+        ],
+        compiler_params=PARAMS,
+        name="prep",
+    )(weights, u, v, d, recv, above_rows, below_rows)
     band = pltpu.VMEM((BAND, 8, ECOLS), F32)
-    shift, speed, damage, resist, coarse, tops = pl.pallas_call(
+    shift, speed, damage, resist, coarse, edge = pl.pallas_call(
         plate_kernel,
         out_shape=(
             shaped(2, ROWS, COLS),
@@ -538,9 +635,9 @@
             shaped(2, ROWS, COLS, dtype=jnp.bfloat16),
             shaped(HEAT_ROWS, CCOLS),
             shaped(3, HEAT_ROWS, WCOLS),
-            shaped(GX, 8, 128),
+            shaped(HEAT_ROWS, 128),
         ),
-        in_specs=[MARKS, ANY, ANY] + vmem(2) + [ANY, ANY] + vmem(2),
+        in_specs=vmem(1) + [ANY] + vmem(5),
         out_specs=(ANY, ANY, ANY) + tuple(vmem(3)),
         scratch_shapes=[
             pltpu.VMEM((6, 5, EROWS, 128), F32),
@@ -554,16 +651,24 @@
             pltpu.VMEM((3, 64, WCOLS), F32),
             pltpu.VMEM((80, COLS), F32),
             pltpu.VMEM((2, ROWS, COLS), jnp.bfloat16),
-            pltpu.SemaphoreType.DMA((19,)),
+            pltpu.SemaphoreType.DMA((10,)),
         ],
         compiler_params=PARAMS,
         name="plate",
-    )(marks, u, v, d, recv, above_rows, below_rows, above, below)
-    from_left = lax.ppermute(resist[:, 128:256], "gy", ahead("gy"))
+    )(weights, state, side, coarse, table, above, below)
+    from_left = lax.ppermute(edge, "gy", ahead("gy"))
+    tops = pl.pallas_call(
+        border_kernel,
+        out_shape=shaped(GX, 8, 128),
+        in_specs=vmem(2),
+        out_specs=vmem(1)[0],
+        compiler_params=PARAMS,
+        name="border",
+    )(resist, coarse)
     tops = exchange(tops, "gx")
     answer = pl.pallas_call(
         solve_kernel,
-        out_shape=shaped(GY, 16, CCOLS),
+        out_shape=shaped(GY, 24, 128),
         in_specs=vmem(4),
         out_specs=vmem(1)[0],
         compiler_params=PARAMS,

time: 71.5 us -> 64.6 us (0.903)
  starting transfers between devices: 29.2 us -> 24.7 us
  waiting for transfers between devices: 10.4 us -> 8.59 us
    ppermute x2, starting transfers between devices: 6.56 us -> 2.69 us  [neighbours(): lax.ppermute(value_up, axis, ahead(axis))]
    ppermute x2, waiting for transfers between devices: 3.59 us -> 0.01 us  [neighbours(): lax.ppermute(value_down, axis, back)]
    ppermute x1, starting transfers between devices: 5.76 us -> 3.29 us  [per_device(): from_left = lax.ppermute(edge, 'gy', ahead('gy'))]
    pallas_call x2 -> x5, Pallas kernels: 3.76 us -> 5.85 us  [the longest x1 2.33 us: per_device(): pl.pallas_call(pack_kernel, out_shape=(shaped(GY, CHUNK, 128), shaped(8,...]
    pallas_call x1, Pallas kernels: 9.76 us -> 7.74 us  [per_device(): pl.pallas_call(plate_kernel, out_shape=(shaped(2, ROWS, COLS), shaped(2,...]
    ppermute x2, starting transfers between devices: 2.58 us -> 4.56 us  [neighbours(): lax.ppermute(value_down, axis, back)]
    ppermute x2, waiting for transfers between devices: 0.01 us -> 0.92 us  [neighbours(): lax.ppermute(value_up, axis, ahead(axis))]
    all_to_all x2, waiting for transfers between devices: 5.89 us -> 6.76 us  [exchange(): return lax.all_to_all(value, axis, split_axis=0, concat_axis=0, tiled=True)]
  transfers between devices with their start and end apart: 7 -> 7, of which waited for: 3 -> 4; matrix products, arithmetic and copies ran while one was open for 0% -> 0% of each run, Pallas kernels for 1% -> 3%
where the time goes in v3:
time: 64.6 us; the launch traced here: 64.2 us
  starting transfers between devices  24.7 us (38%)
  blocking collectives  15.5 us (24%)
  Pallas kernels  14.6 us (23%)
  waiting for transfers between devices  8.59 us (13%)
  between operations  0.72 us (1%)
    all_to_all x1, blocking collectives, exchange(): return lax.all_to_all(value, axis, split_axis=0, concat_axis=0, tiled=True)  15.5 us
    all_to_all x2, starting transfers between devices, exchange(): return lax.all_to_all(value, axis, split_axis=0, concat_axis=0, tiled=True)  14.1 us
    pallas_call x1, Pallas kernels, per_device(): pl.pallas_call(plate_kernel, out_shape=(shaped(2, ROWS, COLS), shaped(2,...  7.74 us
    all_to_all x2, waiting for transfers between devices, exchange(): return lax.all_to_all(value, axis, split_axis=0, concat_axis=0, tiled=True)  6.76 us
    ppermute x2, starting transfers between devices, neighbours(): lax.ppermute(value_down, axis, back)  4.56 us
    ppermute x1, starting transfers between devices, per_device(): from_left = lax.ppermute(edge, 'gy', ahead('gy'))  3.29 us
    ppermute x2, starting transfers between devices, neighbours(): lax.ppermute(value_up, axis, ahead(axis))  2.69 us
    pallas_call x1, Pallas kernels, per_device(): pl.pallas_call(pack_kernel, out_shape=(shaped(GY, CHUNK, 128), shaped(8,...  2.33 us
  transfers between devices with their start and end apart: 7, of which 4 were waited for; matrix products, arithmetic and copies ran while one was open for 0% of the time, Pallas kernels for 3%

profile of v3, /device:TPU:1, one launch (start us, length us, event | category | flops | bytes accessed | tf_op | source)
XLA Modules:
  0.0 64.2 jit_solution(16774056473321252750)
XLA Ops:
  0.6 0.0 copy-start
  0.6 0.0 copy-start.1
  0.7 0.0 copy-start.2
  0.7 2.3 %pack.1 = (f32[16,56,128]{2,1,0:T(8,128)}, f32[8,128]{1,0:T(8,128)S(1)}) custom-call(s32[8]{0:T(128)} %bitcast.1, f32[2,64,512]{2,1,0:T(8,128)} %u.1, f32[2,64,512]{2,1,0:T(8,128)} %v.1, s32[2,64,512]{2,1,0:T(8,128)} %d.1, f32[2,4096]{1,0:T(2,128)} %warm.1, f32[2,4096]{1,0:T(2,128)} %cap_hbm.1, f32[2,4096]{1,0:T(2,128)} %film_hbm.1, f32[2,4096]{1,0:T(2,128)} %bath_hbm.1), custom_call_target="tpu_custom_call" | custom-call | tf_op jit(solution)/shard_map/pack/pallas_call | solution.py:577
  3.0 9.3 %all-to-all-start = ((f32[16,56,128]{2,1,0:T(8,128)}), f32[16,56,128]{2,1,0:T(8,128)S(1)}, u32[]{:S(2)}, u32[]{:S(2)}) async-start(f32[16,56,128]{2,1,0:T(8,128)} %get-tuple-element.21), calls=%async_computation | async-start | bytes 917504 | tf_op jit(solution)/shard_map/all_to_all | solution.py:567
  12.3 1.1 %rows.1 = (f32[6,4,16,128]{3,2,1,0:T(8,128)S(1)}, f32[6,4,16,128]{3,2,1,0:T(8,128)S(1)}) custom-call(f32[8,128]{1,0:T(8,128)S(1)} %get-tuple-element.20.weights, f32[2,64,512]{2,1,0:T(8,128)} %u.1, f32[2,64,512]{2,1,0:T(8,128)} %v.1, s32[2,64,512]{2,1,0:T(8,128)} %d.1), custom_call_target="tpu_custom_call" | custom-call | tf_op jit(solution)/shard_map/rows/pallas_call | solution.py:590
  13.4 1.4 %collective-permute-start = (f32[6,4,16,128]{3,2,1,0:T(8,128)S(1)}, f32[6,4,16,128]{3,2,1,0:T(8,128)S(1)}, u32[]{:S(2)}, u32[]{:S(2)}) collective-permute-start(f32[6,4,16,128]{3,2,1,0:T(8,128)S(1)} %get-tuple-element.22), channel_id=1, source_target_pairs={{0,16},{16,32},{32,48},{48,64},{64,80},{80,96},{96,112},{112,0},{1... | collective-permute-start | bytes 589832 | tf_op jit(solution)/shard_map/ppermute | solution.py:563
  14.8 2.3 %collective-permute-start.1 = (f32[6,4,16,128]{3,2,1,0:T(8,128)S(1)}, f32[6,4,16,128]{3,2,1,0:T(8,128)S(1)}, u32[]{:S(2)}, u32[]{:S(2)}) collective-permute-start(f32[6,4,16,128]{3,2,1,0:T(8,128)S(1)} %get-tuple-element.23), channel_id=1, source_target_pairs={{16,0},{32,16},{48,32},{64,48},{80,64},{96,80},{112,96},{0,112},{1... | collective-permute-start | bytes 589832 | tf_op jit(solution)/shard_map/ppermute | solution.py:563
  17.1 5.8 %all-to-all-done.recv = f32[16,56,128]{2,1,0:T(8,128)S(1)} async-done(((f32[16,56,128]{2,1,0:T(8,128)}), f32[16,56,128]{2,1,0:T(8,128)S(1)}, u32[]{:S(2)}, u32[]{:S(2)}) %all-to-all-start) | async-done | bytes 458784 | tf_op jit(solution)/shard_map/all_to_all | solution.py:567
  22.9 0.1 rim.1
  23.0 1.3 %collective-permute-start.2 = (f32[112,128]{1,0:T(8,128)S(1)}, f32[112,128]{1,0:T(8,128)S(1)}, u32[]{:S(2)}, u32[]{:S(2)}) collective-permute-start(f32[112,128]{1,0:T(8,128)S(1)} %get-tuple-element.28), channel_id=1, source_target_pairs={{0,16},{16,32},{32,48},{48,64},{64,80},{80,96},{96,112},{112,0},{1... | collective-permute-start | bytes 172040 | tf_op jit(solution)/shard_map/ppermute | solution.py:563
  24.3 2.3 %collective-permute-start.3 = (f32[112,128]{1,0:T(8,128)S(1)}, f32[112,128]{1,0:T(8,128)S(1)}, u32[]{:S(2)}, u32[]{:S(2)}) collective-permute-start(f32[112,128]{1,0:T(8,128)S(1)} %get-tuple-element.29), channel_id=1, source_target_pairs={{16,0},{32,16},{48,32},{64,48},{80,64},{96,80},{112,96},{0,112},{1... | collective-permute-start | bytes 172040 | tf_op jit(solution)/shard_map/ppermute | solution.py:563
  26.6 0.0 collective-permute-done.above_rows
  26.6 0.0 collective-permute-done.1.below_rows
  26.6 0.0 copy-done
  26.6 0.0 copy-done.1
  26.6 0.0 copy-done.2
  26.6 0.6 prep.1
  27.2 0.9 %collective-permute-done.2.above = f32[112,128]{1,0:T(8,128)S(1)} collective-permute-done((f32[112,128]{1,0:T(8,128)S(1)}, f32[112,128]{1,0:T(8,128)S(1)}, u32[]{:S(2)}, u32[]{:S(2)}) %collective-permute-start.2) | collective-permute-done | bytes 57376 | tf_op jit(solution)/shard_map/ppermute | solution.py:563
  28.2 0.0 collective-permute-done.3.below
  28.2 0.0 copy-start.3
  28.2 7.7 %plate.1 = (f32[2,64,512]{2,1,0:T(8,128)}, f32[2,64,512]{2,1,0:T(8,128)}, bf16[2,64,512]{2,1,0:T(8,128)(2,1)}, f32[40,256]{1,0:T(8,128)S(1)}, f32[3,40,384]{2,1,0:T(8,128)S(1)}, /*index=5*/f32[40,128]{1,0:T(8,128)S(1)}) custom-call(f32[8,128]{1,0:T(8,128)S(1)} %get-tuple-element.20.weights, f32[6,12,8,640]{3,2,1,0:T(8,128)S(1)} %get-tuple-element.24.state_in, ...), custom_call_target="tpu_custom_call" | custom-call | tf_op jit(solution)/shard_map/plate/pallas_call | solution.py:630
  35.9 1.2 %border.1 = f32[8,8,128]{2,1,0:T(8,128)} custom-call(f32[40,256]{1,0:T(8,128)S(1)} %get-tuple-element.33.resist, f32[3,40,384]{2,1,0:T(8,128)S(1)} %get-tuple-element.35.coarse), custom_call_target="tpu_custom_call" | custom-call | tf_op jit(solution)/shard_map/border/pallas_call | solution.py:660
  37.1 4.8 %all-to-all-start.1 = ((f32[8,8,128]{2,1,0:T(8,128)}), f32[8,8,128]{2,1,0:T(8,128)S(1)}, u32[]{:S(2)}, u32[]{:S(2)}) async-start(f32[8,8,128]{2,1,0:T(8,128)} %border.1), calls=%async_computation.1 | async-start | bytes 65536 | tf_op jit(solution)/shard_map/all_to_all | solution.py:567
  42.0 3.3 %collective-permute-start.4 = (f32[40,128]{1,0:T(8,128)S(1)}, f32[40,128]{1,0:T(8,128)S(1)}, u32[]{:S(2)}, u32[]{:S(2)}) collective-permute-start(f32[40,128]{1,0:T(8,128)S(1)} %get-tuple-element.34), channel_id=1, source_target_pairs={{0,1},{1,2},{2,3},{3,4},{4,5},{5,6},{6,7},{7,8},{8,9},{9,10},{10,1... | collective-permute-start | bytes 61448 | tf_op jit(solution)/shard_map/ppermute | solution.py:659
  45.2 0.9 %collective-permute-done.4.from_left = f32[40,128]{1,0:T(8,128)S(1)} collective-permute-done((f32[40,128]{1,0:T(8,128)S(1)}, f32[40,128]{1,0:T(8,128)S(1)}, u32[]{:S(2)}, u32[]{:S(2)}) %collective-permute-start.4) | collective-permute-done | bytes 20512 | tf_op jit(solution)/shard_map/ppermute | solution.py:659
  46.2 0.9 %all-to-all-done.1.tops = f32[8,8,128]{2,1,0:T(8,128)S(1)} async-done(((f32[8,8,128]{2,1,0:T(8,128)}), f32[8,8,128]{2,1,0:T(8,128)S(1)}, u32[]{:S(2)}, u32[]{:S(2)}) %all-to-all-start.1) | async-done | bytes 32800 | tf_op jit(solution)/shard_map/all_to_all | solution.py:567
  47.1 0.6 solve.1
  47.7 15.5 %all_to_all.15.recv = f32[16,24,128]{2,1,0:T(8,128)S(1)} all-to-all(f32[16,24,128]{2,1,0:T(8,128)S(1)} %solve.1), channel_id=1, replica_groups=mesh['gx'=8,'gy'=16] {'gy'}, dimensions={0} | all-to-all | bytes 393216 | tf_op jit(solution)/shard_map/all_to_all | solution.py:567
  63.2 0.0 copy-done.3
  63.2 1.0 %finish.1 = f32[2,4096]{1,0:T(2,128)} custom-call(f32[16,24,128]{2,1,0:T(8,128)S(1)} %all_to_all.15.recv, f32[2,4096]{1,0:T(2,128)S(1)} %copy-done.3), custom_call_target="tpu_custom_call" | custom-call | tf_op jit(solution)/shard_map/finish/pallas_call | solution.py:678
Async XLA Ops:
  0.6 26.0 %copy-start = (f32[2,64,512]{2,1,0:T(8,128)S(1)}, f32[2,64,512]{2,1,0:T(8,128)}, u32[]{:S(2)}) copy-start(f32[2,64,512]{2,1,0:T(8,128)} %u.1) | copy-start | bytes 786436
  0.6 26.0 %copy-start.1 = (f32[2,64,512]{2,1,0:T(8,128)S(1)}, f32[2,64,512]{2,1,0:T(8,128)}, u32[]{:S(2)}) copy-start(f32[2,64,512]{2,1,0:T(8,128)} %v.1) | copy-start | bytes 786436
  0.7 26.0 %copy-start.2 = (s32[2,64,512]{2,1,0:T(8,128)S(1)}, s32[2,64,512]{2,1,0:T(8,128)}, u32[]{:S(2)}) copy-start(s32[2,64,512]{2,1,0:T(8,128)} %d.1) | copy-start | bytes 786436
  3.0 19.9 %all-to-all-start = ((f32[16,56,128]{2,1,0:T(8,128)}), f32[16,56,128]{2,1,0:T(8,128)S(1)}, u32[]{:S(2)}, u32[]{:S(2)}) async-start(f32[16,56,128]{2,1,0:T(8,128)} %get-tuple-element.21), calls=%async_computation | async-start | bytes 917504 | tf_op jit(solution)/shard_map/all_to_all | solution.py:567
  13.4 13.2 %collective-permute-start = (f32[6,4,16,128]{3,2,1,0:T(8,128)S(1)}, f32[6,4,16,128]{3,2,1,0:T(8,128)S(1)}, u32[]{:S(2)}, u32[]{:S(2)}) collective-permute-start(f32[6,4,16,128]{3,2,1,0:T(8,128)S(1)} %get-tuple-element.22), channel_id=1, source_target_pairs={{0,16},{16,32},{32,48},{48,64},{64,80},{80,96},{96,112},{112,0},{1... | collective-permute-start | bytes 589832 | tf_op jit(solution)/shard_map/ppermute | solution.py:563
  14.8 11.8 %collective-permute-start.1 = (f32[6,4,16,128]{3,2,1,0:T(8,128)S(1)}, f32[6,4,16,128]{3,2,1,0:T(8,128)S(1)}, u32[]{:S(2)}, u32[]{:S(2)}) collective-permute-start(f32[6,4,16,128]{3,2,1,0:T(8,128)S(1)} %get-tuple-element.23), channel_id=1, source_target_pairs={{16,0},{32,16},{48,32},{64,48},{80,64},{96,80},{112,96},{0,112},{1... | collective-permute-start | bytes 589832 | tf_op jit(solution)/shard_map/ppermute | solution.py:563
  23.0 5.2 %collective-permute-start.2 = (f32[112,128]{1,0:T(8,128)S(1)}, f32[112,128]{1,0:T(8,128)S(1)}, u32[]{:S(2)}, u32[]{:S(2)}) collective-permute-start(f32[112,128]{1,0:T(8,128)S(1)} %get-tuple-element.28), channel_id=1, source_target_pairs={{0,16},{16,32},{32,48},{48,64},{64,80},{80,96},{96,112},{112,0},{1... | collective-permute-start | bytes 172040 | tf_op jit(solution)/shard_map/ppermute | solution.py:563
  24.3 3.8 %collective-permute-start.3 = (f32[112,128]{1,0:T(8,128)S(1)}, f32[112,128]{1,0:T(8,128)S(1)}, u32[]{:S(2)}, u32[]{:S(2)}) collective-permute-start(f32[112,128]{1,0:T(8,128)S(1)} %get-tuple-element.29), channel_id=1, source_target_pairs={{16,0},{32,16},{48,32},{64,48},{80,64},{96,80},{112,96},{0,112},{1... | collective-permute-start | bytes 172040 | tf_op jit(solution)/shard_map/ppermute | solution.py:563
  28.2 35.0 %copy-start.3 = (f32[2,4096]{1,0:T(2,128)S(1)}, f32[2,4096]{1,0:T(2,128)}, u32[]{:S(2)}) copy-start(f32[2,4096]{1,0:T(2,128)} %warm.1) | copy-start | bytes 98308
  37.1 10.0 %all-to-all-start.1 = ((f32[8,8,128]{2,1,0:T(8,128)}), f32[8,8,128]{2,1,0:T(8,128)S(1)}, u32[]{:S(2)}, u32[]{:S(2)}) async-start(f32[8,8,128]{2,1,0:T(8,128)} %border.1), calls=%async_computation.1 | async-start | bytes 65536 | tf_op jit(solution)/shard_map/all_to_all | solution.py:567
  42.0 4.2 %collective-permute-start.4 = (f32[40,128]{1,0:T(8,128)S(1)}, f32[40,128]{1,0:T(8,128)S(1)}, u32[]{:S(2)}, u32[]{:S(2)}) collective-permute-start(f32[40,128]{1,0:T(8,128)S(1)} %get-tuple-element.34), channel_id=1, source_target_pairs={{0,1},{1,2},{2,3},{3,4},{4,5},{5,6},{6,7},{7,8},{8,9},{9,10},{10,1... | collective-permute-start | bytes 61448 | tf_op jit(solution)/shard_map/ppermute | solution.py:659

commit v4 on v3

--- a/solution.py
+++ b/solution.py
@@ -249,8 +249,8 @@
 
 def plate_kernel(
     weights, state_in, side, coarse_in, table, above, below,
-    shift_out, speed_out, damage_out, resist_out, coarse_out, edge_out,
-    field, cw, temp, state, rate, warmth, tx, ty, coarse, gap, worn, sem,
+    shift_out, speed_out, damage_out, resist_out, coarse_out, edge_out, tops_out,
+    field, cw, temp, state, rate, warmth, tx, ty, coarse, gap, worn, border_tiles, sem,
 ):
     gx = lax.axis_index("gx")
     gy = lax.axis_index("gy")
@@ -407,49 +407,51 @@
             dy = 1.0 - field[5, k, rows, :]
             if k == 0:
                 dy = jnp.where(gy * COLS + lane >= 1, dy, 0.0)
-            gap[pl.ds(8 * b, 8), cols] = dx + dy
+            gap[k, pl.ds(8 * b, 8), :] = dx + dy
             if 1 <= b < 9:
                 worn[0, pl.ds(8 * b - 8, 8), cols] = dx.astype(jnp.bfloat16)
                 worn[1, pl.ds(8 * b - 8, 8), cols] = dy.astype(jnp.bfloat16)
     start_all(results[-1:])
-    a = sublanes((HEAT_ROWS, 2 * HEAT_ROWS))
-    c = lanes((HEAT_ROWS, 2 * HEAT_ROWS))
-    pool = jnp.where(c // 2 == a, 1.0, 0.0)
+    pairs = [
+        gap[k, pl.ds(0, HEAT_ROWS, stride=2), :] + gap[k, pl.ds(1, HEAT_ROWS, stride=2), :]
+        for k in range(4)
+    ]
     for k in range(2):
-        pair = jnp.dot(pool, gap[:, pl.ds(256 * k, 256)], precision=HI, preferred_element_type=F32)
         resist_out[:, pl.ds(128 * k, 128)] = jnp.dot(
-            pair, table[...], precision=HI, preferred_element_type=F32
+            jnp.concatenate(pairs[2 * k : 2 * k + 2], axis=1),
+            table[...],
+            precision=HI,
+            preferred_element_type=F32,
         )
     edge_out[...] = resist_out[:, 128:256]
-    wait_all(results)
-
-
-def border_kernel(resist, coarse, out):
-    gx = lax.axis_index("gx")
-    conduct = (1.0 + 0.5 * coarse[0, :, 0:CCOLS]) / (1.0 + resist[...])
+    conduct = (1.0 + 0.5 * coarse[0, 12 : 12 + HEAT_ROWS, 0:CCOLS]) / (1.0 + resist_out[...])
     shape = (HEAT_ROWS, CCOLS)
     row = gx * CROWS - 4 + sublanes(shape)
     down = jnp.where((row >= 1) & (row < GX * CROWS), 0.5 * (conduct + turn(conduct, 1, 0)), 0.0)
     side = jnp.where(lanes(shape) >= 1, 0.5 * (conduct + turn(conduct, 1, 1)), 0.0)
     offsum = (down + turn(down, -1, 0) + side + turn(side, -1, 1))[4 : 4 + CROWS]
-    capacity = coarse[1, 4 : 4 + CROWS, 0:CCOLS]
+    capacity = coarse[1, 16:48, 0:CCOLS]
     top = jnp.max(offsum / (capacity + offsum), axis=(0, 1), keepdims=True)
     a = sublanes((8, CCOLS))
     c = lanes((8, CCOLS))
-    border = jnp.where(sublanes((8, 128)) >= 6, top, 0.0)
+    border = jnp.where(sublanes((8, CROWS)) >= 6, top, 0.0)
     for k, value in enumerate((offsum, capacity, conduct[4 : 4 + CROWS])):
         pick = jnp.where(
             ((a == 2 * k) & (c == 0)) | ((a == 2 * k + 1) & (c == CCOLS - 1)), 1.0, 0.0
         )
         border += lax.dot_general(
             pick,
-            jnp.concatenate([value] * 4, axis=0),
+            value,
             (((1,), (1,)), ((), ())),
             precision=HI,
             preferred_element_type=F32,
         )
     for g in range(GX):
-        out[g] = border
+        border_tiles[g] = jnp.zeros((8, 128), F32)
+        border_tiles[g, :, 0:CROWS] = border
+    send = pltpu.make_async_copy(border_tiles, tops_out, sem.at[10])
+    send.start()
+    wait_all(results + [send])
 
 
 def conductances(resist, from_left, coarse):
@@ -500,7 +502,7 @@
     for h in range(2):
         tile = tops[4 * h]
         for k in range(1, 4):
-            tile = jnp.where(group == k, tops[4 * h + k], tile)
+            tile = jnp.where(group == k, turn(tops[4 * h + k], 32 * k, 1), tile)
         strip.append(tile)
     last_y, last_y2 = y[:, CCOLS:], turn(y2[:, CCOLS:], 64, 1)
     tail = jnp.where(lanes(last_y.shape) < 64, last_y, last_y2)
@@ -627,7 +629,7 @@
         name="prep",
     )(weights, u, v, d, recv, above_rows, below_rows)
     band = pltpu.VMEM((BAND, 8, ECOLS), F32)
-    shift, speed, damage, resist, coarse, edge = pl.pallas_call(
+    shift, speed, damage, resist, coarse, edge, tops = pl.pallas_call(
         plate_kernel,
         out_shape=(
             shaped(2, ROWS, COLS),
@@ -636,9 +638,10 @@
             shaped(HEAT_ROWS, CCOLS),
             shaped(3, HEAT_ROWS, WCOLS),
             shaped(HEAT_ROWS, 128),
+            shaped(GX, 8, 128),
         ),
         in_specs=vmem(1) + [ANY] + vmem(5),
-        out_specs=(ANY, ANY, ANY) + tuple(vmem(3)),
+        out_specs=(ANY, ANY, ANY) + tuple(vmem(3)) + (ANY,),
         scratch_shapes=[
             pltpu.VMEM((6, 5, EROWS, 128), F32),
             pltpu.VMEM((2, EROWS, 128), F32),
@@ -649,22 +652,15 @@
             band,
             band,
             pltpu.VMEM((3, 64, WCOLS), F32),
-            pltpu.VMEM((80, COLS), F32),
+            pltpu.VMEM((4, 2 * HEAT_ROWS, 128), F32),
             pltpu.VMEM((2, ROWS, COLS), jnp.bfloat16),
-            pltpu.SemaphoreType.DMA((10,)),
+            pltpu.VMEM((GX, 8, 128), F32),
+            pltpu.SemaphoreType.DMA((11,)),
         ],
         compiler_params=PARAMS,
         name="plate",
     )(weights, state, side, coarse, table, above, below)
     from_left = lax.ppermute(edge, "gy", ahead("gy"))
-    tops = pl.pallas_call(
-        border_kernel,
-        out_shape=shaped(GX, 8, 128),
-        in_specs=vmem(2),
-        out_specs=vmem(1)[0],
-        compiler_params=PARAMS,
-        name="border",
-    )(resist, coarse)
     tops = exchange(tops, "gx")
     answer = pl.pallas_call(
         solve_kernel,

time: 64.6 us -> 64 us (level)
    pallas_call x1 -> x0, Pallas kernels: 1.21 us -> none  [per_device(): pl.pallas_call(border_kernel, out_shape=shaped(GX, 8, 128), in_specs=vmem...]
    pallas_call x1, Pallas kernels: 7.74 us -> 8.42 us  [per_device(): pl.pallas_call(plate_kernel, out_shape=(shaped(2, ROWS, COLS), shaped(2,...]
where the time goes in v4:
time: 64 us; the launch traced here: 63.6 us
  starting transfers between devices  24.7 us (39%)
  blocking collectives  15.5 us (24%)
  Pallas kernels  14.1 us (22%)
  waiting for transfers between devices  8.59 us (13%)
  between operations  0.72 us (1%)
    all_to_all x1, blocking collectives, exchange(): return lax.all_to_all(value, axis, split_axis=0, concat_axis=0, tiled=True)  15.5 us
    all_to_all x2, starting transfers between devices, exchange(): return lax.all_to_all(value, axis, split_axis=0, concat_axis=0, tiled=True)  14.2 us
    pallas_call x1, Pallas kernels, per_device(): pl.pallas_call(plate_kernel, out_shape=(shaped(2, ROWS, COLS), shaped(2,...  8.42 us
    all_to_all x2, waiting for transfers between devices, exchange(): return lax.all_to_all(value, axis, split_axis=0, concat_axis=0, tiled=True)  6.76 us
    ppermute x2, starting transfers between devices, neighbours(): lax.ppermute(value_down, axis, back)  4.56 us
    ppermute x1, starting transfers between devices, per_device(): from_left = lax.ppermute(edge, 'gy', ahead('gy'))  3.29 us
    ppermute x2, starting transfers between devices, neighbours(): lax.ppermute(value_up, axis, ahead(axis))  2.69 us
    pallas_call x1, Pallas kernels, per_device(): pl.pallas_call(pack_kernel, out_shape=(shaped(GY, CHUNK, 128), shaped(8,...  2.33 us
  transfers between devices with their start and end apart: 7, of which 4 were waited for; matrix products, arithmetic and copies ran while one was open for 0% of the time, Pallas kernels for 3%

profile of v4, /device:TPU:1, one launch (start us, length us, event | category | flops | bytes accessed | tf_op | source)
XLA Modules:
  0.0 63.6 jit_solution(14961215964416603024)
XLA Ops:
  0.6 0.0 copy-start
  0.6 0.0 copy-start.1
  0.7 0.0 copy-start.2
  0.7 2.3 %pack.1 = (f32[16,56,128]{2,1,0:T(8,128)}, f32[8,128]{1,0:T(8,128)S(1)}) custom-call(s32[8]{0:T(128)} %bitcast.1, f32[2,64,512]{2,1,0:T(8,128)} %u.1, f32[2,64,512]{2,1,0:T(8,128)} %v.1, s32[2,64,512]{2,1,0:T(8,128)} %d.1, f32[2,4096]{1,0:T(2,128)} %warm.1, f32[2,4096]{1,0:T(2,128)} %cap_hbm.1, f32[2,4096]{1,0:T(2,128)} %film_hbm.1, f32[2,4096]{1,0:T(2,128)} %bath_hbm.1), custom_call_target="tpu_custom_call" | custom-call | tf_op jit(solution)/shard_map/pack/pallas_call | solution.py:579
  3.0 9.3 %all-to-all-start = ((f32[16,56,128]{2,1,0:T(8,128)}), f32[16,56,128]{2,1,0:T(8,128)S(1)}, u32[]{:S(2)}, u32[]{:S(2)}) async-start(f32[16,56,128]{2,1,0:T(8,128)} %get-tuple-element.22), calls=%async_computation | async-start | bytes 917504 | tf_op jit(solution)/shard_map/all_to_all | solution.py:569
  12.3 1.1 %rows.1 = (f32[6,4,16,128]{3,2,1,0:T(8,128)S(1)}, f32[6,4,16,128]{3,2,1,0:T(8,128)S(1)}) custom-call(f32[8,128]{1,0:T(8,128)S(1)} %get-tuple-element.21.weights, f32[2,64,512]{2,1,0:T(8,128)} %u.1, f32[2,64,512]{2,1,0:T(8,128)} %v.1, s32[2,64,512]{2,1,0:T(8,128)} %d.1), custom_call_target="tpu_custom_call" | custom-call | tf_op jit(solution)/shard_map/rows/pallas_call | solution.py:592
  13.4 1.4 %collective-permute-start = (f32[6,4,16,128]{3,2,1,0:T(8,128)S(1)}, f32[6,4,16,128]{3,2,1,0:T(8,128)S(1)}, u32[]{:S(2)}, u32[]{:S(2)}) collective-permute-start(f32[6,4,16,128]{3,2,1,0:T(8,128)S(1)} %get-tuple-element.23), channel_id=1, source_target_pairs={{0,16},{16,32},{32,48},{48,64},{64,80},{80,96},{96,112},{112,0},{1... | collective-permute-start | bytes 589832 | tf_op jit(solution)/shard_map/ppermute | solution.py:565
  14.8 2.3 %collective-permute-start.1 = (f32[6,4,16,128]{3,2,1,0:T(8,128)S(1)}, f32[6,4,16,128]{3,2,1,0:T(8,128)S(1)}, u32[]{:S(2)}, u32[]{:S(2)}) collective-permute-start(f32[6,4,16,128]{3,2,1,0:T(8,128)S(1)} %get-tuple-element.24), channel_id=1, source_target_pairs={{16,0},{32,16},{48,32},{64,48},{80,64},{96,80},{112,96},{0,112},{1... | collective-permute-start | bytes 589832 | tf_op jit(solution)/shard_map/ppermute | solution.py:565
  17.1 5.8 %all-to-all-done.recv = f32[16,56,128]{2,1,0:T(8,128)S(1)} async-done(((f32[16,56,128]{2,1,0:T(8,128)}), f32[16,56,128]{2,1,0:T(8,128)S(1)}, u32[]{:S(2)}, u32[]{:S(2)}) %all-to-all-start) | async-done | bytes 458784 | tf_op jit(solution)/shard_map/all_to_all | solution.py:569
  22.9 0.1 rim.1
  23.0 1.3 %collective-permute-start.2 = (f32[112,128]{1,0:T(8,128)S(1)}, f32[112,128]{1,0:T(8,128)S(1)}, u32[]{:S(2)}, u32[]{:S(2)}) collective-permute-start(f32[112,128]{1,0:T(8,128)S(1)} %get-tuple-element.29), channel_id=1, source_target_pairs={{0,16},{16,32},{32,48},{48,64},{64,80},{80,96},{96,112},{112,0},{1... | collective-permute-start | bytes 172040 | tf_op jit(solution)/shard_map/ppermute | solution.py:565
  24.3 2.3 %collective-permute-start.3 = (f32[112,128]{1,0:T(8,128)S(1)}, f32[112,128]{1,0:T(8,128)S(1)}, u32[]{:S(2)}, u32[]{:S(2)}) collective-permute-start(f32[112,128]{1,0:T(8,128)S(1)} %get-tuple-element.30), channel_id=1, source_target_pairs={{16,0},{32,16},{48,32},{64,48},{80,64},{96,80},{112,96},{0,112},{1... | collective-permute-start | bytes 172040 | tf_op jit(solution)/shard_map/ppermute | solution.py:565
  26.6 0.0 collective-permute-done.above_rows
  26.6 0.0 collective-permute-done.1.below_rows
  26.6 0.0 copy-done
  26.6 0.0 copy-done.1
  26.6 0.0 copy-done.2
  26.6 0.6 prep.1
  27.2 0.9 %collective-permute-done.2.above = f32[112,128]{1,0:T(8,128)S(1)} collective-permute-done((f32[112,128]{1,0:T(8,128)S(1)}, f32[112,128]{1,0:T(8,128)S(1)}, u32[]{:S(2)}, u32[]{:S(2)}) %collective-permute-start.2) | collective-permute-done | bytes 57376 | tf_op jit(solution)/shard_map/ppermute | solution.py:565
  28.2 0.0 collective-permute-done.3.below
  28.2 0.0 copy-start.3
  28.2 8.4 %plate.1 = (f32[2,64,512]{2,1,0:T(8,128)}, f32[2,64,512]{2,1,0:T(8,128)}, bf16[2,64,512]{2,1,0:T(8,128)(2,1)}, f32[40,256]{1,0:T(8,128)S(1)}, f32[3,40,384]{2,1,...) custom-call(f32[8,128]{1,0:T(8,128)S(1)} %get-tuple-element.21.weights, ...), custom_call_target="tpu_custom_call" | custom-call | tf_op jit(solution)/shard_map/plate/pallas_call | solution.py:632
  36.6 4.9 %all-to-all-start.1 = ((f32[8,8,128]{2,1,0:T(8,128)}), f32[8,8,128]{2,1,0:T(8,128)S(1)}, u32[]{:S(2)}, u32[]{:S(2)}) async-start(f32[8,8,128]{2,1,0:T(8,128)} %get-tuple-element.37), calls=%async_computation.1 | async-start | bytes 65536 | tf_op jit(solution)/shard_map/all_to_all | solution.py:569
  41.4 3.3 %collective-permute-start.4 = (f32[40,128]{1,0:T(8,128)S(1)}, f32[40,128]{1,0:T(8,128)S(1)}, u32[]{:S(2)}, u32[]{:S(2)}) collective-permute-start(f32[40,128]{1,0:T(8,128)S(1)} %get-tuple-element.35), channel_id=1, source_target_pairs={{0,1},{1,2},{2,3},{3,4},{4,5},{5,6},{6,7},{7,8},{8,9},{9,10},{10,1... | collective-permute-start | bytes 61448 | tf_op jit(solution)/shard_map/ppermute | solution.py:663
  44.7 0.9 %collective-permute-done.4.from_left = f32[40,128]{1,0:T(8,128)S(1)} collective-permute-done((f32[40,128]{1,0:T(8,128)S(1)}, f32[40,128]{1,0:T(8,128)S(1)}, u32[]{:S(2)}, u32[]{:S(2)}) %collective-permute-start.4) | collective-permute-done | bytes 20512 | tf_op jit(solution)/shard_map/ppermute | solution.py:663
  45.6 0.9 %all-to-all-done.1.tops = f32[8,8,128]{2,1,0:T(8,128)S(1)} async-done(((f32[8,8,128]{2,1,0:T(8,128)}), f32[8,8,128]{2,1,0:T(8,128)S(1)}, u32[]{:S(2)}, u32[]{:S(2)}) %all-to-all-start.1) | async-done | bytes 32800 | tf_op jit(solution)/shard_map/all_to_all | solution.py:569
  46.6 0.6 solve.1
  47.2 15.5 %all_to_all.15.recv = f32[16,24,128]{2,1,0:T(8,128)S(1)} all-to-all(f32[16,24,128]{2,1,0:T(8,128)S(1)} %solve.1), channel_id=1, replica_groups=mesh['gx'=8,'gy'=16] {'gy'}, dimensions={0} | all-to-all | bytes 393216 | tf_op jit(solution)/shard_map/all_to_all | solution.py:569
  62.7 0.0 copy-done.3
  62.7 1.0 %finish.1 = f32[2,4096]{1,0:T(2,128)} custom-call(f32[16,24,128]{2,1,0:T(8,128)S(1)} %all_to_all.15.recv, f32[2,4096]{1,0:T(2,128)S(1)} %copy-done.3), custom_call_target="tpu_custom_call" | custom-call | tf_op jit(solution)/shard_map/finish/pallas_call | solution.py:674
Async XLA Ops:
  0.6 26.0 %copy-start = (f32[2,64,512]{2,1,0:T(8,128)S(1)}, f32[2,64,512]{2,1,0:T(8,128)}, u32[]{:S(2)}) copy-start(f32[2,64,512]{2,1,0:T(8,128)} %u.1) | copy-start | bytes 786436
  0.6 26.0 %copy-start.1 = (f32[2,64,512]{2,1,0:T(8,128)S(1)}, f32[2,64,512]{2,1,0:T(8,128)}, u32[]{:S(2)}) copy-start(f32[2,64,512]{2,1,0:T(8,128)} %v.1) | copy-start | bytes 786436
  0.7 26.0 %copy-start.2 = (s32[2,64,512]{2,1,0:T(8,128)S(1)}, s32[2,64,512]{2,1,0:T(8,128)}, u32[]{:S(2)}) copy-start(s32[2,64,512]{2,1,0:T(8,128)} %d.1) | copy-start | bytes 786436
  3.0 19.9 %all-to-all-start = ((f32[16,56,128]{2,1,0:T(8,128)}), f32[16,56,128]{2,1,0:T(8,128)S(1)}, u32[]{:S(2)}, u32[]{:S(2)}) async-start(f32[16,56,128]{2,1,0:T(8,128)} %get-tuple-element.22), calls=%async_computation | async-start | bytes 917504 | tf_op jit(solution)/shard_map/all_to_all | solution.py:569
  13.4 13.2 %collective-permute-start = (f32[6,4,16,128]{3,2,1,0:T(8,128)S(1)}, f32[6,4,16,128]{3,2,1,0:T(8,128)S(1)}, u32[]{:S(2)}, u32[]{:S(2)}) collective-permute-start(f32[6,4,16,128]{3,2,1,0:T(8,128)S(1)} %get-tuple-element.23), channel_id=1, source_target_pairs={{0,16},{16,32},{32,48},{48,64},{64,80},{80,96},{96,112},{112,0},{1... | collective-permute-start | bytes 589832 | tf_op jit(solution)/shard_map/ppermute | solution.py:565
  14.8 11.8 %collective-permute-start.1 = (f32[6,4,16,128]{3,2,1,0:T(8,128)S(1)}, f32[6,4,16,128]{3,2,1,0:T(8,128)S(1)}, u32[]{:S(2)}, u32[]{:S(2)}) collective-permute-start(f32[6,4,16,128]{3,2,1,0:T(8,128)S(1)} %get-tuple-element.24), channel_id=1, source_target_pairs={{16,0},{32,16},{48,32},{64,48},{80,64},{96,80},{112,96},{0,112},{1... | collective-permute-start | bytes 589832 | tf_op jit(solution)/shard_map/ppermute | solution.py:565
  23.0 5.2 %collective-permute-start.2 = (f32[112,128]{1,0:T(8,128)S(1)}, f32[112,128]{1,0:T(8,128)S(1)}, u32[]{:S(2)}, u32[]{:S(2)}) collective-permute-start(f32[112,128]{1,0:T(8,128)S(1)} %get-tuple-element.29), channel_id=1, source_target_pairs={{0,16},{16,32},{32,48},{48,64},{64,80},{80,96},{96,112},{112,0},{1... | collective-permute-start | bytes 172040 | tf_op jit(solution)/shard_map/ppermute | solution.py:565
  24.3 3.8 %collective-permute-start.3 = (f32[112,128]{1,0:T(8,128)S(1)}, f32[112,128]{1,0:T(8,128)S(1)}, u32[]{:S(2)}, u32[]{:S(2)}) collective-permute-start(f32[112,128]{1,0:T(8,128)S(1)} %get-tuple-element.30), channel_id=1, source_target_pairs={{16,0},{32,16},{48,32},{64,48},{80,64},{96,80},{112,96},{0,112},{1... | collective-permute-start | bytes 172040 | tf_op jit(solution)/shard_map/ppermute | solution.py:565
  28.2 34.5 %copy-start.3 = (f32[2,4096]{1,0:T(2,128)S(1)}, f32[2,4096]{1,0:T(2,128)}, u32[]{:S(2)}) copy-start(f32[2,4096]{1,0:T(2,128)} %warm.1) | copy-start | bytes 98308
  36.6 10.0 %all-to-all-start.1 = ((f32[8,8,128]{2,1,0:T(8,128)}), f32[8,8,128]{2,1,0:T(8,128)S(1)}, u32[]{:S(2)}, u32[]{:S(2)}) async-start(f32[8,8,128]{2,1,0:T(8,128)} %get-tuple-element.37), calls=%async_computation.1 | async-start | bytes 65536 | tf_op jit(solution)/shard_map/all_to_all | solution.py:569
  41.4 4.2 %collective-permute-start.4 = (f32[40,128]{1,0:T(8,128)S(1)}, f32[40,128]{1,0:T(8,128)S(1)}, u32[]{:S(2)}, u32[]{:S(2)}) collective-permute-start(f32[40,128]{1,0:T(8,128)S(1)} %get-tuple-element.35), channel_id=1, source_target_pairs={{0,1},{1,2},{2,3},{3,4},{4,5},{5,6},{6,7},{7,8},{8,9},{9,10},{10,1... | collective-permute-start | bytes 61448 | tf_op jit(solution)/shard_map/ppermute | solution.py:663

commit v5 on v4

--- a/solution.py
+++ b/solution.py
@@ -22,7 +22,7 @@
 DAMPING = 0.05
 EXPANSION = 0.6
 LOG2E = 1.4426950408889634
-HI = lax.Precision.HIGHEST
+HI = lax.Precision.HIGH
 CHUNK = 56
 CORNER = 16 + 48 + 24 + 24
 

time: 64 us -> 63.6 us (level)
  no operation moved by 1% of the time
where the time goes in v5:
time: 63.6 us; the launch traced here: 63.2 us
  starting transfers between devices  24.7 us (39%)
  blocking collectives  15.5 us (24%)
  Pallas kernels  13.6 us (21%)
  waiting for transfers between devices  8.59 us (14%)
  between operations  0.72 us (1%)
    all_to_all x1, blocking collectives, exchange(): return lax.all_to_all(value, axis, split_axis=0, concat_axis=0, tiled=True)  15.5 us
    all_to_all x2, starting transfers between devices, exchange(): return lax.all_to_all(value, axis, split_axis=0, concat_axis=0, tiled=True)  14.2 us
    pallas_call x1, Pallas kernels, per_device(): pl.pallas_call(plate_kernel, out_shape=(shaped(2, ROWS, COLS), shaped(2,...  7.95 us
    all_to_all x2, waiting for transfers between devices, exchange(): return lax.all_to_all(value, axis, split_axis=0, concat_axis=0, tiled=True)  6.76 us
    ppermute x2, starting transfers between devices, neighbours(): lax.ppermute(value_down, axis, back)  4.56 us
    ppermute x1, starting transfers between devices, per_device(): from_left = lax.ppermute(edge, 'gy', ahead('gy'))  3.29 us
    ppermute x2, starting transfers between devices, neighbours(): lax.ppermute(value_up, axis, ahead(axis))  2.69 us
    pallas_call x1, Pallas kernels, per_device(): pl.pallas_call(pack_kernel, out_shape=(shaped(GY, CHUNK, 128), shaped(8,...  2.33 us
  transfers between devices with their start and end apart: 7, of which 4 were waited for; matrix products, arithmetic and copies ran while one was open for 0% of the time, Pallas kernels for 3%

profile of v5, /device:TPU:1, one launch (start us, length us, event | category | flops | bytes accessed | tf_op | source)
XLA Modules:
  0.0 63.2 jit_solution(1208246362210577310)
XLA Ops:
  0.6 0.0 copy-start
  0.6 0.0 copy-start.1
  0.7 0.0 copy-start.2
  0.7 2.3 %pack.1 = (f32[16,56,128]{2,1,0:T(8,128)}, f32[8,128]{1,0:T(8,128)S(1)}) custom-call(s32[8]{0:T(128)} %bitcast.1, f32[2,64,512]{2,1,0:T(8,128)} %u.1, f32[2,64,512]{2,1,0:T(8,128)} %v.1, s32[2,64,512]{2,1,0:T(8,128)} %d.1, f32[2,4096]{1,0:T(2,128)} %warm.1, f32[2,4096]{1,0:T(2,128)} %cap_hbm.1, f32[2,4096]{1,0:T(2,128)} %film_hbm.1, f32[2,4096]{1,0:T(2,128)} %bath_hbm.1), custom_call_target="tpu_custom_call" | custom-call | tf_op jit(solution)/shard_map/pack/pallas_call | solution.py:579
  3.0 9.3 %all-to-all-start = ((f32[16,56,128]{2,1,0:T(8,128)}), f32[16,56,128]{2,1,0:T(8,128)S(1)}, u32[]{:S(2)}, u32[]{:S(2)}) async-start(f32[16,56,128]{2,1,0:T(8,128)} %get-tuple-element.22), calls=%async_computation | async-start | bytes 917504 | tf_op jit(solution)/shard_map/all_to_all | solution.py:569
  12.3 1.1 %rows.1 = (f32[6,4,16,128]{3,2,1,0:T(8,128)S(1)}, f32[6,4,16,128]{3,2,1,0:T(8,128)S(1)}) custom-call(f32[8,128]{1,0:T(8,128)S(1)} %get-tuple-element.21.weights, f32[2,64,512]{2,1,0:T(8,128)} %u.1, f32[2,64,512]{2,1,0:T(8,128)} %v.1, s32[2,64,512]{2,1,0:T(8,128)} %d.1), custom_call_target="tpu_custom_call" | custom-call | tf_op jit(solution)/shard_map/rows/pallas_call | solution.py:592
  13.4 1.4 %collective-permute-start = (f32[6,4,16,128]{3,2,1,0:T(8,128)S(1)}, f32[6,4,16,128]{3,2,1,0:T(8,128)S(1)}, u32[]{:S(2)}, u32[]{:S(2)}) collective-permute-start(f32[6,4,16,128]{3,2,1,0:T(8,128)S(1)} %get-tuple-element.23), channel_id=1, source_target_pairs={{0,16},{16,32},{32,48},{48,64},{64,80},{80,96},{96,112},{112,0},{1... | collective-permute-start | bytes 589832 | tf_op jit(solution)/shard_map/ppermute | solution.py:565
  14.8 2.3 %collective-permute-start.1 = (f32[6,4,16,128]{3,2,1,0:T(8,128)S(1)}, f32[6,4,16,128]{3,2,1,0:T(8,128)S(1)}, u32[]{:S(2)}, u32[]{:S(2)}) collective-permute-start(f32[6,4,16,128]{3,2,1,0:T(8,128)S(1)} %get-tuple-element.24), channel_id=1, source_target_pairs={{16,0},{32,16},{48,32},{64,48},{80,64},{96,80},{112,96},{0,112},{1... | collective-permute-start | bytes 589832 | tf_op jit(solution)/shard_map/ppermute | solution.py:565
  17.1 5.8 %all-to-all-done.recv = f32[16,56,128]{2,1,0:T(8,128)S(1)} async-done(((f32[16,56,128]{2,1,0:T(8,128)}), f32[16,56,128]{2,1,0:T(8,128)S(1)}, u32[]{:S(2)}, u32[]{:S(2)}) %all-to-all-start) | async-done | bytes 458784 | tf_op jit(solution)/shard_map/all_to_all | solution.py:569
  22.9 0.1 rim.1
  23.0 1.3 %collective-permute-start.2 = (f32[112,128]{1,0:T(8,128)S(1)}, f32[112,128]{1,0:T(8,128)S(1)}, u32[]{:S(2)}, u32[]{:S(2)}) collective-permute-start(f32[112,128]{1,0:T(8,128)S(1)} %get-tuple-element.29), channel_id=1, source_target_pairs={{0,16},{16,32},{32,48},{48,64},{64,80},{80,96},{96,112},{112,0},{1... | collective-permute-start | bytes 172040 | tf_op jit(solution)/shard_map/ppermute | solution.py:565
  24.3 2.3 %collective-permute-start.3 = (f32[112,128]{1,0:T(8,128)S(1)}, f32[112,128]{1,0:T(8,128)S(1)}, u32[]{:S(2)}, u32[]{:S(2)}) collective-permute-start(f32[112,128]{1,0:T(8,128)S(1)} %get-tuple-element.30), channel_id=1, source_target_pairs={{16,0},{32,16},{48,32},{64,48},{80,64},{96,80},{112,96},{0,112},{1... | collective-permute-start | bytes 172040 | tf_op jit(solution)/shard_map/ppermute | solution.py:565
  26.6 0.0 collective-permute-done.above_rows
  26.6 0.0 collective-permute-done.1.below_rows
  26.6 0.0 copy-done
  26.6 0.0 copy-done.1
  26.6 0.0 copy-done.2
  26.6 0.6 prep.1
  27.2 0.9 %collective-permute-done.2.above = f32[112,128]{1,0:T(8,128)S(1)} collective-permute-done((f32[112,128]{1,0:T(8,128)S(1)}, f32[112,128]{1,0:T(8,128)S(1)}, u32[]{:S(2)}, u32[]{:S(2)}) %collective-permute-start.2) | collective-permute-done | bytes 57376 | tf_op jit(solution)/shard_map/ppermute | solution.py:565
  28.2 0.0 collective-permute-done.3.below
  28.2 0.0 copy-start.3
  28.2 8.0 %plate.1 = (f32[2,64,512]{2,1,0:T(8,128)}, f32[2,64,512]{2,1,0:T(8,128)}, bf16[2,64,512]{2,1,0:T(8,128)(2,1)}, f32[40,256]{1,0:T(8,128)S(1)}, f32[3,40,384]{2,1,...) custom-call(f32[8,128]{1,0:T(8,128)S(1)} %get-tuple-element.21.weights, ...), custom_call_target="tpu_custom_call" | custom-call | tf_op jit(solution)/shard_map/plate/pallas_call | solution.py:632
  36.1 4.9 %all-to-all-start.1 = ((f32[8,8,128]{2,1,0:T(8,128)}), f32[8,8,128]{2,1,0:T(8,128)S(1)}, u32[]{:S(2)}, u32[]{:S(2)}) async-start(f32[8,8,128]{2,1,0:T(8,128)} %get-tuple-element.37), calls=%async_computation.1 | async-start | bytes 65536 | tf_op jit(solution)/shard_map/all_to_all | solution.py:569
  41.0 3.3 %collective-permute-start.4 = (f32[40,128]{1,0:T(8,128)S(1)}, f32[40,128]{1,0:T(8,128)S(1)}, u32[]{:S(2)}, u32[]{:S(2)}) collective-permute-start(f32[40,128]{1,0:T(8,128)S(1)} %get-tuple-element.35), channel_id=1, source_target_pairs={{0,1},{1,2},{2,3},{3,4},{4,5},{5,6},{6,7},{7,8},{8,9},{9,10},{10,1... | collective-permute-start | bytes 61448 | tf_op jit(solution)/shard_map/ppermute | solution.py:663
  44.3 0.9 %collective-permute-done.4.from_left = f32[40,128]{1,0:T(8,128)S(1)} collective-permute-done((f32[40,128]{1,0:T(8,128)S(1)}, f32[40,128]{1,0:T(8,128)S(1)}, u32[]{:S(2)}, u32[]{:S(2)}) %collective-permute-start.4) | collective-permute-done | bytes 20512 | tf_op jit(solution)/shard_map/ppermute | solution.py:663
  45.2 0.9 %all-to-all-done.1.tops = f32[8,8,128]{2,1,0:T(8,128)S(1)} async-done(((f32[8,8,128]{2,1,0:T(8,128)}), f32[8,8,128]{2,1,0:T(8,128)S(1)}, u32[]{:S(2)}, u32[]{:S(2)}) %all-to-all-start.1) | async-done | bytes 32800 | tf_op jit(solution)/shard_map/all_to_all | solution.py:569
  46.1 0.6 solve.1
  46.7 15.5 %all_to_all.15.recv = f32[16,24,128]{2,1,0:T(8,128)S(1)} all-to-all(f32[16,24,128]{2,1,0:T(8,128)S(1)} %solve.1), channel_id=1, replica_groups=mesh['gx'=8,'gy'=16] {'gy'}, dimensions={0} | all-to-all | bytes 393216 | tf_op jit(solution)/shard_map/all_to_all | solution.py:569
  62.2 0.0 copy-done.3
  62.2 1.0 %finish.1 = f32[2,4096]{1,0:T(2,128)} custom-call(f32[16,24,128]{2,1,0:T(8,128)S(1)} %all_to_all.15.recv, f32[2,4096]{1,0:T(2,128)S(1)} %copy-done.3), custom_call_target="tpu_custom_call" | custom-call | tf_op jit(solution)/shard_map/finish/pallas_call | solution.py:674
Async XLA Ops:
  0.6 26.0 %copy-start = (f32[2,64,512]{2,1,0:T(8,128)S(1)}, f32[2,64,512]{2,1,0:T(8,128)}, u32[]{:S(2)}) copy-start(f32[2,64,512]{2,1,0:T(8,128)} %u.1) | copy-start | bytes 786436
  0.6 26.0 %copy-start.1 = (f32[2,64,512]{2,1,0:T(8,128)S(1)}, f32[2,64,512]{2,1,0:T(8,128)}, u32[]{:S(2)}) copy-start(f32[2,64,512]{2,1,0:T(8,128)} %v.1) | copy-start | bytes 786436
  0.7 26.0 %copy-start.2 = (s32[2,64,512]{2,1,0:T(8,128)S(1)}, s32[2,64,512]{2,1,0:T(8,128)}, u32[]{:S(2)}) copy-start(s32[2,64,512]{2,1,0:T(8,128)} %d.1) | copy-start | bytes 786436
  3.0 19.9 %all-to-all-start = ((f32[16,56,128]{2,1,0:T(8,128)}), f32[16,56,128]{2,1,0:T(8,128)S(1)}, u32[]{:S(2)}, u32[]{:S(2)}) async-start(f32[16,56,128]{2,1,0:T(8,128)} %get-tuple-element.22), calls=%async_computation | async-start | bytes 917504 | tf_op jit(solution)/shard_map/all_to_all | solution.py:569
  13.4 13.2 %collective-permute-start = (f32[6,4,16,128]{3,2,1,0:T(8,128)S(1)}, f32[6,4,16,128]{3,2,1,0:T(8,128)S(1)}, u32[]{:S(2)}, u32[]{:S(2)}) collective-permute-start(f32[6,4,16,128]{3,2,1,0:T(8,128)S(1)} %get-tuple-element.23), channel_id=1, source_target_pairs={{0,16},{16,32},{32,48},{48,64},{64,80},{80,96},{96,112},{112,0},{1... | collective-permute-start | bytes 589832 | tf_op jit(solution)/shard_map/ppermute | solution.py:565
  14.8 11.8 %collective-permute-start.1 = (f32[6,4,16,128]{3,2,1,0:T(8,128)S(1)}, f32[6,4,16,128]{3,2,1,0:T(8,128)S(1)}, u32[]{:S(2)}, u32[]{:S(2)}) collective-permute-start(f32[6,4,16,128]{3,2,1,0:T(8,128)S(1)} %get-tuple-element.24), channel_id=1, source_target_pairs={{16,0},{32,16},{48,32},{64,48},{80,64},{96,80},{112,96},{0,112},{1... | collective-permute-start | bytes 589832 | tf_op jit(solution)/shard_map/ppermute | solution.py:565
  23.0 5.2 %collective-permute-start.2 = (f32[112,128]{1,0:T(8,128)S(1)}, f32[112,128]{1,0:T(8,128)S(1)}, u32[]{:S(2)}, u32[]{:S(2)}) collective-permute-start(f32[112,128]{1,0:T(8,128)S(1)} %get-tuple-element.29), channel_id=1, source_target_pairs={{0,16},{16,32},{32,48},{48,64},{64,80},{80,96},{96,112},{112,0},{1... | collective-permute-start | bytes 172040 | tf_op jit(solution)/shard_map/ppermute | solution.py:565
  24.3 3.8 %collective-permute-start.3 = (f32[112,128]{1,0:T(8,128)S(1)}, f32[112,128]{1,0:T(8,128)S(1)}, u32[]{:S(2)}, u32[]{:S(2)}) collective-permute-start(f32[112,128]{1,0:T(8,128)S(1)} %get-tuple-element.30), channel_id=1, source_target_pairs={{16,0},{32,16},{48,32},{64,48},{80,64},{96,80},{112,96},{0,112},{1... | collective-permute-start | bytes 172040 | tf_op jit(solution)/shard_map/ppermute | solution.py:565
  28.2 34.0 %copy-start.3 = (f32[2,4096]{1,0:T(2,128)S(1)}, f32[2,4096]{1,0:T(2,128)}, u32[]{:S(2)}) copy-start(f32[2,4096]{1,0:T(2,128)} %warm.1) | copy-start | bytes 98308
  36.1 10.0 %all-to-all-start.1 = ((f32[8,8,128]{2,1,0:T(8,128)}), f32[8,8,128]{2,1,0:T(8,128)S(1)}, u32[]{:S(2)}, u32[]{:S(2)}) async-start(f32[8,8,128]{2,1,0:T(8,128)} %get-tuple-element.37), calls=%async_computation.1 | async-start | bytes 65536 | tf_op jit(solution)/shard_map/all_to_all | solution.py:569
  41.0 4.2 %collective-permute-start.4 = (f32[40,128]{1,0:T(8,128)S(1)}, f32[40,128]{1,0:T(8,128)S(1)}, u32[]{:S(2)}, u32[]{:S(2)}) collective-permute-start(f32[40,128]{1,0:T(8,128)S(1)} %get-tuple-element.35), channel_id=1, source_target_pairs={{0,1},{1,2},{2,3},{3,4},{4,5},{5,6},{6,7},{7,8},{8,9},{9,10},{10,1... | collective-permute-start | bytes 61448 | tf_op jit(solution)/shard_map/ppermute | solution.py:663

commit v6 on v5

--- a/solution.py
+++ b/solution.py
@@ -313,7 +313,7 @@
     tiles = [columns(k) for k in range(4)]
     tiles.append(jnp.where(lane64 < 64, columns(4), columns(-1)))
     for k in range(5):
-        temp[k] = jnp.dot(raise_, tiles[k], precision=HI, preferred_element_type=F32)
+        temp[k, 0:EROWS, :] = jnp.dot(raise_, tiles[k], precision=HI, preferred_element_type=F32)
 
     factor = -4.0 * LOG2E
     for rows, source in ((top, above), (low, below)):
@@ -622,7 +622,7 @@
         in_specs=vmem(1) + [ANY, ANY] + vmem(2) + [ANY, ANY],
         out_specs=tuple(vmem(4)),
         scratch_shapes=[
-            pltpu.VMEM((6, 4, EROWS, 128), F32),
+            pltpu.VMEM((6, 4, EROWS + 16, 128), F32),
             pltpu.SemaphoreType.DMA((10,)),
         ],
         compiler_params=PARAMS,
@@ -643,16 +643,16 @@
         in_specs=vmem(1) + [ANY] + vmem(5),
         out_specs=(ANY, ANY, ANY) + tuple(vmem(3)) + (ANY,),
         scratch_shapes=[
-            pltpu.VMEM((6, 5, EROWS, 128), F32),
-            pltpu.VMEM((2, EROWS, 128), F32),
-            pltpu.VMEM((5, EROWS, 128), F32),
+            pltpu.VMEM((6, 5, EROWS + 16, 128), F32),
+            pltpu.VMEM((2, EROWS + 16, 128), F32),
+            pltpu.VMEM((5, EROWS + 16, 128), F32),
             pltpu.VMEM((6, BAND, 8, ECOLS), F32),
             band,
             band,
             band,
             band,
             pltpu.VMEM((3, 64, WCOLS), F32),
-            pltpu.VMEM((4, 2 * HEAT_ROWS, 128), F32),
+            pltpu.VMEM((4, 2 * HEAT_ROWS + 8, 128), F32),
             pltpu.VMEM((2, ROWS, COLS), jnp.bfloat16),
             pltpu.VMEM((GX, 8, 128), F32),
             pltpu.SemaphoreType.DMA((11,)),

time: 63.6 us -> 63.6 us (level)
  no operation moved by 1% of the time
where the time goes in v6:
time: 63.6 us; the launch traced here: 63.2 us
  starting transfers between devices  24.7 us (39%)
  blocking collectives  15.5 us (24%)
  Pallas kernels  13.6 us (21%)
  waiting for transfers between devices  8.61 us (14%)
  between operations  0.72 us (1%)
    all_to_all x1, blocking collectives, exchange(): return lax.all_to_all(value, axis, split_axis=0, concat_axis=0, tiled=True)  15.5 us
    all_to_all x2, starting transfers between devices, exchange(): return lax.all_to_all(value, axis, split_axis=0, concat_axis=0, tiled=True)  14.2 us
    pallas_call x1, Pallas kernels, per_device(): pl.pallas_call(plate_kernel, out_shape=(shaped(2, ROWS, COLS), shaped(2,...  7.95 us
    all_to_all x2, waiting for transfers between devices, exchange(): return lax.all_to_all(value, axis, split_axis=0, concat_axis=0, tiled=True)  6.76 us
    ppermute x2, starting transfers between devices, neighbours(): lax.ppermute(value_down, axis, back)  4.56 us
    ppermute x1, starting transfers between devices, per_device(): from_left = lax.ppermute(edge, 'gy', ahead('gy'))  3.29 us
    ppermute x2, starting transfers between devices, neighbours(): lax.ppermute(value_up, axis, ahead(axis))  2.69 us
    pallas_call x1, Pallas kernels, per_device(): pl.pallas_call(pack_kernel, out_shape=(shaped(GY, CHUNK, 128), shaped(8,...  2.33 us
  transfers between devices with their start and end apart: 7, of which 4 were waited for; matrix products, arithmetic and copies ran while one was open for 0% of the time, Pallas kernels for 3%

profile of v6, /device:TPU:1, one launch (start us, length us, event | category | flops | bytes accessed | tf_op | source)
XLA Modules:
  0.0 63.2 jit_solution(901629657025811174)
XLA Ops:
  0.6 0.0 copy-start
  0.6 0.0 copy-start.1
  0.7 0.0 copy-start.2
  0.7 2.3 %pack.1 = (f32[16,56,128]{2,1,0:T(8,128)}, f32[8,128]{1,0:T(8,128)S(1)}) custom-call(s32[8]{0:T(128)} %bitcast.1, f32[2,64,512]{2,1,0:T(8,128)} %u.1, f32[2,64,512]{2,1,0:T(8,128)} %v.1, s32[2,64,512]{2,1,0:T(8,128)} %d.1, f32[2,4096]{1,0:T(2,128)} %warm.1, f32[2,4096]{1,0:T(2,128)} %cap_hbm.1, f32[2,4096]{1,0:T(2,128)} %film_hbm.1, f32[2,4096]{1,0:T(2,128)} %bath_hbm.1), custom_call_target="tpu_custom_call" | custom-call | tf_op jit(solution)/shard_map/pack/pallas_call | solution.py:579
  3.0 9.3 %all-to-all-start = ((f32[16,56,128]{2,1,0:T(8,128)}), f32[16,56,128]{2,1,0:T(8,128)S(1)}, u32[]{:S(2)}, u32[]{:S(2)}) async-start(f32[16,56,128]{2,1,0:T(8,128)} %get-tuple-element.22), calls=%async_computation | async-start | bytes 917504 | tf_op jit(solution)/shard_map/all_to_all | solution.py:569
  12.3 1.1 %rows.1 = (f32[6,4,16,128]{3,2,1,0:T(8,128)S(1)}, f32[6,4,16,128]{3,2,1,0:T(8,128)S(1)}) custom-call(f32[8,128]{1,0:T(8,128)S(1)} %get-tuple-element.21.weights, f32[2,64,512]{2,1,0:T(8,128)} %u.1, f32[2,64,512]{2,1,0:T(8,128)} %v.1, s32[2,64,512]{2,1,0:T(8,128)} %d.1), custom_call_target="tpu_custom_call" | custom-call | tf_op jit(solution)/shard_map/rows/pallas_call | solution.py:592
  13.4 1.4 %collective-permute-start = (f32[6,4,16,128]{3,2,1,0:T(8,128)S(1)}, f32[6,4,16,128]{3,2,1,0:T(8,128)S(1)}, u32[]{:S(2)}, u32[]{:S(2)}) collective-permute-start(f32[6,4,16,128]{3,2,1,0:T(8,128)S(1)} %get-tuple-element.23), channel_id=1, source_target_pairs={{0,16},{16,32},{32,48},{48,64},{64,80},{80,96},{96,112},{112,0},{1... | collective-permute-start | bytes 589832 | tf_op jit(solution)/shard_map/ppermute | solution.py:565
  14.8 2.3 %collective-permute-start.1 = (f32[6,4,16,128]{3,2,1,0:T(8,128)S(1)}, f32[6,4,16,128]{3,2,1,0:T(8,128)S(1)}, u32[]{:S(2)}, u32[]{:S(2)}) collective-permute-start(f32[6,4,16,128]{3,2,1,0:T(8,128)S(1)} %get-tuple-element.24), channel_id=1, source_target_pairs={{16,0},{32,16},{48,32},{64,48},{80,64},{96,80},{112,96},{0,112},{1... | collective-permute-start | bytes 589832 | tf_op jit(solution)/shard_map/ppermute | solution.py:565
  17.1 5.8 %all-to-all-done.recv = f32[16,56,128]{2,1,0:T(8,128)S(1)} async-done(((f32[16,56,128]{2,1,0:T(8,128)}), f32[16,56,128]{2,1,0:T(8,128)S(1)}, u32[]{:S(2)}, u32[]{:S(2)}) %all-to-all-start) | async-done | bytes 458784 | tf_op jit(solution)/shard_map/all_to_all | solution.py:569
  22.9 0.1 rim.1
  23.0 1.3 %collective-permute-start.2 = (f32[112,128]{1,0:T(8,128)S(1)}, f32[112,128]{1,0:T(8,128)S(1)}, u32[]{:S(2)}, u32[]{:S(2)}) collective-permute-start(f32[112,128]{1,0:T(8,128)S(1)} %get-tuple-element.29), channel_id=1, source_target_pairs={{0,16},{16,32},{32,48},{48,64},{64,80},{80,96},{96,112},{112,0},{1... | collective-permute-start | bytes 172040 | tf_op jit(solution)/shard_map/ppermute | solution.py:565
  24.3 2.3 %collective-permute-start.3 = (f32[112,128]{1,0:T(8,128)S(1)}, f32[112,128]{1,0:T(8,128)S(1)}, u32[]{:S(2)}, u32[]{:S(2)}) collective-permute-start(f32[112,128]{1,0:T(8,128)S(1)} %get-tuple-element.30), channel_id=1, source_target_pairs={{16,0},{32,16},{48,32},{64,48},{80,64},{96,80},{112,96},{0,112},{1... | collective-permute-start | bytes 172040 | tf_op jit(solution)/shard_map/ppermute | solution.py:565
  26.6 0.0 collective-permute-done.above_rows
  26.6 0.0 collective-permute-done.1.below_rows
  26.6 0.0 copy-done
  26.6 0.0 copy-done.1
  26.6 0.0 copy-done.2
  26.6 0.6 prep.1
  27.2 0.9 %collective-permute-done.2.above = f32[112,128]{1,0:T(8,128)S(1)} collective-permute-done((f32[112,128]{1,0:T(8,128)S(1)}, f32[112,128]{1,0:T(8,128)S(1)}, u32[]{:S(2)}, u32[]{:S(2)}) %collective-permute-start.2) | collective-permute-done | bytes 57376 | tf_op jit(solution)/shard_map/ppermute | solution.py:565
  28.2 0.0 collective-permute-done.3.below
  28.2 0.0 copy-start.3
  28.2 8.0 %plate.1 = (f32[2,64,512]{2,1,0:T(8,128)}, f32[2,64,512]{2,1,0:T(8,128)}, bf16[2,64,512]{2,1,0:T(8,128)(2,1)}, f32[40,256]{1,0:T(8,128)S(1)}, f32[3,40,384]{2,1,...) custom-call(f32[8,128]{1,0:T(8,128)S(1)} %get-tuple-element.21.weights, ...), custom_call_target="tpu_custom_call" | custom-call | tf_op jit(solution)/shard_map/plate/pallas_call | solution.py:632
  36.1 4.9 %all-to-all-start.1 = ((f32[8,8,128]{2,1,0:T(8,128)}), f32[8,8,128]{2,1,0:T(8,128)S(1)}, u32[]{:S(2)}, u32[]{:S(2)}) async-start(f32[8,8,128]{2,1,0:T(8,128)} %get-tuple-element.37), calls=%async_computation.1 | async-start | bytes 65536 | tf_op jit(solution)/shard_map/all_to_all | solution.py:569
  41.0 3.3 %collective-permute-start.4 = (f32[40,128]{1,0:T(8,128)S(1)}, f32[40,128]{1,0:T(8,128)S(1)}, u32[]{:S(2)}, u32[]{:S(2)}) collective-permute-start(f32[40,128]{1,0:T(8,128)S(1)} %get-tuple-element.35), channel_id=1, source_target_pairs={{0,1},{1,2},{2,3},{3,4},{4,5},{5,6},{6,7},{7,8},{8,9},{9,10},{10,1... | collective-permute-start | bytes 61448 | tf_op jit(solution)/shard_map/ppermute | solution.py:663
  44.3 0.9 %collective-permute-done.4.from_left = f32[40,128]{1,0:T(8,128)S(1)} collective-permute-done((f32[40,128]{1,0:T(8,128)S(1)}, f32[40,128]{1,0:T(8,128)S(1)}, u32[]{:S(2)}, u32[]{:S(2)}) %collective-permute-start.4) | collective-permute-done | bytes 20512 | tf_op jit(solution)/shard_map/ppermute | solution.py:663
  45.2 0.9 %all-to-all-done.1.tops = f32[8,8,128]{2,1,0:T(8,128)S(1)} async-done(((f32[8,8,128]{2,1,0:T(8,128)}), f32[8,8,128]{2,1,0:T(8,128)S(1)}, u32[]{:S(2)}, u32[]{:S(2)}) %all-to-all-start.1) | async-done | bytes 32800 | tf_op jit(solution)/shard_map/all_to_all | solution.py:569
  46.1 0.6 solve.1
  46.7 15.5 %all_to_all.15.recv = f32[16,24,128]{2,1,0:T(8,128)S(1)} all-to-all(f32[16,24,128]{2,1,0:T(8,128)S(1)} %solve.1), channel_id=1, replica_groups=mesh['gx'=8,'gy'=16] {'gy'}, dimensions={0} | all-to-all | bytes 393216 | tf_op jit(solution)/shard_map/all_to_all | solution.py:569
  62.2 0.0 copy-done.3
  62.2 1.0 %finish.1 = f32[2,4096]{1,0:T(2,128)} custom-call(f32[16,24,128]{2,1,0:T(8,128)S(1)} %all_to_all.15.recv, f32[2,4096]{1,0:T(2,128)S(1)} %copy-done.3), custom_call_target="tpu_custom_call" | custom-call | tf_op jit(solution)/shard_map/finish/pallas_call | solution.py:674
Async XLA Ops:
  0.6 26.0 %copy-start = (f32[2,64,512]{2,1,0:T(8,128)S(1)}, f32[2,64,512]{2,1,0:T(8,128)}, u32[]{:S(2)}) copy-start(f32[2,64,512]{2,1,0:T(8,128)} %u.1) | copy-start | bytes 786436
  0.6 26.0 %copy-start.1 = (f32[2,64,512]{2,1,0:T(8,128)S(1)}, f32[2,64,512]{2,1,0:T(8,128)}, u32[]{:S(2)}) copy-start(f32[2,64,512]{2,1,0:T(8,128)} %v.1) | copy-start | bytes 786436
  0.7 26.0 %copy-start.2 = (s32[2,64,512]{2,1,0:T(8,128)S(1)}, s32[2,64,512]{2,1,0:T(8,128)}, u32[]{:S(2)}) copy-start(s32[2,64,512]{2,1,0:T(8,128)} %d.1) | copy-start | bytes 786436
  3.0 19.9 %all-to-all-start = ((f32[16,56,128]{2,1,0:T(8,128)}), f32[16,56,128]{2,1,0:T(8,128)S(1)}, u32[]{:S(2)}, u32[]{:S(2)}) async-start(f32[16,56,128]{2,1,0:T(8,128)} %get-tuple-element.22), calls=%async_computation | async-start | bytes 917504 | tf_op jit(solution)/shard_map/all_to_all | solution.py:569
  13.4 13.2 %collective-permute-start = (f32[6,4,16,128]{3,2,1,0:T(8,128)S(1)}, f32[6,4,16,128]{3,2,1,0:T(8,128)S(1)}, u32[]{:S(2)}, u32[]{:S(2)}) collective-permute-start(f32[6,4,16,128]{3,2,1,0:T(8,128)S(1)} %get-tuple-element.23), channel_id=1, source_target_pairs={{0,16},{16,32},{32,48},{48,64},{64,80},{80,96},{96,112},{112,0},{1... | collective-permute-start | bytes 589832 | tf_op jit(solution)/shard_map/ppermute | solution.py:565
  14.8 11.8 %collective-permute-start.1 = (f32[6,4,16,128]{3,2,1,0:T(8,128)S(1)}, f32[6,4,16,128]{3,2,1,0:T(8,128)S(1)}, u32[]{:S(2)}, u32[]{:S(2)}) collective-permute-start(f32[6,4,16,128]{3,2,1,0:T(8,128)S(1)} %get-tuple-element.24), channel_id=1, source_target_pairs={{16,0},{32,16},{48,32},{64,48},{80,64},{96,80},{112,96},{0,112},{1... | collective-permute-start | bytes 589832 | tf_op jit(solution)/shard_map/ppermute | solution.py:565
  23.0 5.2 %collective-permute-start.2 = (f32[112,128]{1,0:T(8,128)S(1)}, f32[112,128]{1,0:T(8,128)S(1)}, u32[]{:S(2)}, u32[]{:S(2)}) collective-permute-start(f32[112,128]{1,0:T(8,128)S(1)} %get-tuple-element.29), channel_id=1, source_target_pairs={{0,16},{16,32},{32,48},{48,64},{64,80},{80,96},{96,112},{112,0},{1... | collective-permute-start | bytes 172040 | tf_op jit(solution)/shard_map/ppermute | solution.py:565
  24.3 3.8 %collective-permute-start.3 = (f32[112,128]{1,0:T(8,128)S(1)}, f32[112,128]{1,0:T(8,128)S(1)}, u32[]{:S(2)}, u32[]{:S(2)}) collective-permute-start(f32[112,128]{1,0:T(8,128)S(1)} %get-tuple-element.30), channel_id=1, source_target_pairs={{16,0},{32,16},{48,32},{64,48},{80,64},{96,80},{112,96},{0,112},{1... | collective-permute-start | bytes 172040 | tf_op jit(solution)/shard_map/ppermute | solution.py:565
  28.2 34.0 %copy-start.3 = (f32[2,4096]{1,0:T(2,128)S(1)}, f32[2,4096]{1,0:T(2,128)}, u32[]{:S(2)}) copy-start(f32[2,4096]{1,0:T(2,128)} %warm.1) | copy-start | bytes 98308
  36.1 10.0 %all-to-all-start.1 = ((f32[8,8,128]{2,1,0:T(8,128)}), f32[8,8,128]{2,1,0:T(8,128)S(1)}, u32[]{:S(2)}, u32[]{:S(2)}) async-start(f32[8,8,128]{2,1,0:T(8,128)} %get-tuple-element.37), calls=%async_computation.1 | async-start | bytes 65536 | tf_op jit(solution)/shard_map/all_to_all | solution.py:569
  41.0 4.2 %collective-permute-start.4 = (f32[40,128]{1,0:T(8,128)S(1)}, f32[40,128]{1,0:T(8,128)S(1)}, u32[]{:S(2)}, u32[]{:S(2)}) collective-permute-start(f32[40,128]{1,0:T(8,128)S(1)} %get-tuple-element.35), channel_id=1, source_target_pairs={{0,1},{1,2},{2,3},{3,4},{4,5},{5,6},{6,7},{7,8},{8,9},{9,10},{10,1... | collective-permute-start | bytes 61448 | tf_op jit(solution)/shard_map/ppermute | solution.py:663
